TPU v7x, 256 devices: a whole 4x4x8 slice. The times are simulated.
256 devices in a mesh: gx: 4 (over y), gy: 8 (over x, core), gz: 8 (over z).
Axes of the slice: x: 4, y: 4, z: 8, core: 2. Of those that a mesh axis runs over, the one named last changes fastest.
Arguments:
- velocity: float32 [3, 32, 64, 1024], P(None, 'gx', 'gy', 'gz'), may hold values from -6 to 6
- features: bfloat16 [16, 32, 64, 1024], P(None, 'gx', 'gy', 'gz'), may hold values from -6 to 6
- density: float32 [32, 64, 1024], P('gx', 'gy', 'gz'), may hold values from 0.5 to 2
- target: float32 [3, 32, 64, 1024], P(None, 'gx', 'gy', 'gz'), may hold values from -6 to 6
- weight_in: bfloat16 [16, 64], replicated, may hold values from -1.5 to 1.5
- bias_in: float32 [64], replicated, may hold values from -3 to 3
- weight_out: bfloat16 [64, 3], replicated, may hold values from -0.75 to 0.75
- open_faces: int32 [6], replicated, may hold values from 0 to 1
Outputs:
- new_velocity: float32 [3, 32, 64, 1024], P(None, 'gx', 'gy', 'gz')
- grad_weight_in: float32 [16, 64], replicated
- grad_bias_in: float32 [64], replicated
- grad_weight_out: float32 [64, 3], replicated
Inputs may be any that keep to these rules, and one draw needn't show every extreme that they name: `open_faces`: entries in the order low first, high first, low second, high second, low third, high third face; 1 marks an open face (pressure zero beyond it), 0 a wall.
All inputs are finite; a program needn't handle non-finite values.
Results may differ from a plain program's by a relative error of at most 0.0012.
Values sent between devices are 32-bit elements; how exact they have to be, the bound alone decides.
No kernel may reach another device: no remote copies, remote signals or barrier semaphores. Data moves between devices by JAX's collectives and lax.ppermute only.
A program may use at most 128 MiB of HBM per device.

v0:
```python
import jax
import jax.numpy as jnp
from jax import lax
from jax.experimental import pallas as pl
from jax.experimental.pallas import tpu as pltpu
from jax.sharding import Mesh
from jax.sharding import PartitionSpec as P

GY = ("gy_0", "gy_1")
XY = ("gx", "gy_0", "gy_1")
ALL = ("gx", "gy_0", "gy_1", "gz")
F32 = jnp.float32
BF16 = jnp.bfloat16
HIGHEST = lax.Precision.HIGHEST
MASS_SHIFT = 0.05
CELLS = 2097152.0

NXP, NYP, NZP = 22, 24, 256
REGION = (NXP, NYP, NZP)
L1 = (20, 32, 128)
L2 = (10, 16, 128)


def shaped(shape, dtype=F32):
    return jax.ShapeDtypeStruct(shape, dtype)


def call(body, outs, args, scratch=(), smem=()):
    specs = [
        pl.BlockSpec(memory_space=pltpu.SMEM if i in smem else pltpu.VMEM) for i in range(len(args))
    ]
    return pl.pallas_call(
        body,
        out_shape=outs,
        in_specs=specs,
        out_specs=[pl.BlockSpec(memory_space=pltpu.VMEM)] * len(outs),
        scratch_shapes=list(scratch),
        compiler_params=pltpu.CompilerParams(vmem_limit_bytes=48 << 20),
    )(*args)


def back(x, axis):
    return pltpu.roll(x, x.shape[axis] - 1, axis)


def forth(x, axis):
    return pltpu.roll(x, 1, axis)


def exact_dot(a, b):
    return jnp.dot(a, b, precision=HIGHEST, preferred_element_type=F32)


def planes(lo, hi, body, unroll=2):
    def step(i, carry):
        body(i)
        return carry

    lax.fori_loop(lo, hi, step, 0, unroll=unroll)


def around(src, ax, ay, az, i):
    v = src[i]
    y, z = ay[i], az[i]
    total = ax[i] * src[i + 1] + ax[i - 1] * src[i - 1]
    total = total + (y * back(v, 0) + forth(y * v, 0))
    return v, total + (z * back(v, 1) + forth(z * v, 1))


def sweep(src, dst, s, w, ax, ay, az, lo, hi):
    def one(i):
        v, total = around(src, ax, ay, az, i)
        dst[i] = 0.2 * v + w[i] * (s[i] + total)

    planes(lo, hi, one)


def first_sweep(dst, s, w, lo, hi):
    def one(i):
        dst[i] = w[i] * s[i]

    planes(lo, hi, one)


def face(here, there, weight, low, high):
    has, next_has = here > 0.0, there > 0.0
    factor = jnp.where(
        has, jnp.where(next_has, F32(1.0), high), jnp.where(next_has, low, F32(0.0))
    )
    total = jnp.where(has | next_has, here + there, F32(1.0))
    return weight * 2.0 / total * factor


def coefficients(rho, opens, weight, refs, lo, hi, whole_y):
    ax, ay, az, w, d = refs
    low, high = opens
    count = rho.shape[1]

    def one_face(i):
        ax[i] = face(rho[i], rho[i + 1], weight, low[0], high[0])

    planes(lo - 1, hi, one_face, 1)

    def one(i):
        r = rho[i]
        after = back(r, 0)
        before = forth(r, 0)
        row = lax.broadcasted_iota(jnp.int32, r.shape, 0)
        if whole_y:
            after = jnp.where(row == count - 1, F32(0.0), after)
            before = jnp.where(row == 0, F32(0.0), before)
        up_y = face(r, after, weight, low[1], high[1])
        down_y = face(before, r, weight, low[1], high[1])
        up_z = face(r, back(r, 1), weight, low[2], high[2])
        diagonal = MASS_SHIFT + ax[i] + ax[i - 1] + up_y + down_y + up_z + forth(up_z, 1)
        ay[i] = jnp.where(row == count - 1, F32(0.0), up_y) if whole_y else up_y
        az[i] = up_z
        d[i] = diagonal
        w[i] = jnp.where(r > 0.0, 0.8 / diagonal, F32(0.0))

    planes(lo, hi, one, 1)


def lane_pairs(cells, kept, repeat):
    row = lax.broadcasted_iota(jnp.int32, (cells, kept), 0)
    col = lax.broadcasted_iota(jnp.int32, (cells, kept), 1)
    return jnp.where(row // 2 == col % repeat, F32(1.0), F32(0.0))


def lane_spread(cells, kept):
    row = lax.broadcasted_iota(jnp.int32, (cells, kept), 0)
    col = lax.broadcasted_iota(jnp.int32, (cells, kept), 1)
    return jnp.where(col // 2 == row, F32(1.0), F32(0.0))


def block_means(read, rows, out, out_row):
    pairs = [read(7 + 2 * k) + read(8 + 2 * k) for k in range(4)]
    rows[...] = exact_dot(jnp.concatenate(pairs, axis=0), lane_pairs(256, 128, 128))
    total = rows[pl.ds(0, 16, stride=2), :] + rows[pl.ds(1, 16, stride=2), :]
    out[out_row : out_row + 16, :] = 0.125 * total


def presmooth(s, v, va, coefs, rows, out):
    ax, ay, az, w, d = coefs
    first_sweep(v, s, w, 1, 21)
    sweep(v, va, s, w, ax, ay, az, 2, 20)
    sweep(va, v, s, w, ax, ay, az, 3, 19)

    def residue(i):
        centre, total = around(v, ax, ay, az, i)
        return (s[i] + total - d[i] * centre)[8:16]

    block_means(residue, rows, out, 0)


def opens_of(sc):
    values = [sc[3 + k].astype(F32) for k in range(6)]
    return values[0::2], values[1::2]


def start_body(sc, b, rho, ax, ay, az, w, d, v, out, va, rows):
    coefs = (ax, ay, az, w, d)
    for ref in (ax, ay, az, w, d, v):
        ref[0] = jnp.zeros((NYP, NZP), F32)
        ref[21] = jnp.zeros((NYP, NZP), F32)
    coefficients(rho, opens_of(sc), 1.0, coefs, 1, 21, False)
    presmooth(b, v, va, coefs, rows, out)
    block_means(lambda i: rho[i, 8:16, :], rows, out, 16)


def pre_body(b, ax, ay, az, w, d, v, out, va, rows):
    v[0] = jnp.zeros((NYP, NZP), F32)
    v[21] = jnp.zeros((NYP, NZP), F32)
    presmooth(b, v, va, (ax, ay, az, w, d), rows, out)


def again_body(b, p, ax, ay, az, w, d, s, v, out, va, rows):
    for ref in (s, v):
        ref[0] = jnp.zeros((NYP, NZP), F32)
        ref[21] = jnp.zeros((NYP, NZP), F32)

    def one(i):
        centre, total = around(p, ax, ay, az, i)
        s[i] = b[i] + total - d[i] * centre

    planes(1, 21, one)
    presmooth(s, v, va, (ax, ay, az, w, d), rows, out)


def whole_plane(parts, first, dst):
    for k in range(2):
        dst[k] = jnp.zeros((32, 128), F32)
        dst[18 + k] = jnp.zeros((32, 128), F32)
    for device in range(32):
        x, y = divmod(device, 8)
        for k in range(4):
            dst[2 + 4 * x + k, 4 * y : 4 * y + 4, :] = parts[
                device, first + 4 * k : first + 4 * k + 4, :
            ]


def restrict_whole(read, rows, dst):
    for k in range(8):
        rows[32 * k : 32 * k + 32, :] = read(2 + 2 * k) + read(3 + 2 * k)
    rows[...] = exact_dot(rows[...], lane_pairs(128, 128, 64))
    for k in range(8):
        total = (
            rows[pl.ds(32 * k, 16, stride=2), :] + rows[pl.ds(32 * k + 1, 16, stride=2), :]
        )
        dst[1 + k] = 0.125 * total


def coarse_body(
    sc, parts, ax1, ay1, az1, w1, d1, ax2, ay2, az2, w2, d2, rho1, rho2, rows
):
    for ref in (ax1, ay1, az1, w1, d1):
        ref[...] = jnp.zeros(L1, F32)
    for ref in (ax2, ay2, az2, w2, d2, rho2):
        ref[...] = jnp.zeros(L2, F32)
    opens = opens_of(sc)
    whole_plane(parts, 16, rho1)
    coefficients(rho1, opens, 0.25, (ax1, ay1, az1, w1, d1), 2, 18, True)
    restrict_whole(lambda i: rho1[i], rows, rho2)
    coefficients(rho2, opens, 0.0625, (ax2, ay2, az2, w2, d2), 1, 9, True)


def correct(
    sc, parts, coefs1, coefs2, s1, v1, u1, s2, v2, u2, rows, wide_a, wide_b
):
    ax1, ay1, az1, w1, d1 = coefs1
    ax2, ay2, az2, w2, d2 = coefs2
    whole_plane(parts, 0, s1)
    for ref in (v1, u1):
        for k in (0, 1, 18, 19):
            ref[k] = jnp.zeros((32, 128), F32)
    for ref in (v2, u2):
        for k in (0, 9):
            ref[k] = jnp.zeros((16, 128), F32)
    first_sweep(v1, s1, w1, 2, 18)
    sweep(v1, u1, s1, w1, ax1, ay1, az1, 2, 18)
    sweep(u1, v1, s1, w1, ax1, ay1, az1, 2, 18)

    def residue(i):
        centre, total = around(v1, ax1, ay1, az1, i)
        return s1[i] + total - d1[i] * centre

    restrict_whole(residue, rows, s2)
    first_sweep(v2, s2, w2, 1, 9)
    for k in range(5):
        a, b = (v2, u2) if k % 2 == 0 else (u2, v2)
        sweep(a, b, s2, w2, ax2, ay2, az2, 1, 9)
    spread = exact_dot(
        jnp.concatenate([u2[1 + k] for k in range(8)], axis=0), lane_spread(128, 128)
    )
    rows[pl.ds(0, 128, stride=2), :] = spread
    rows[pl.ds(1, 128, stride=2), :] = spread
    for k in range(8):
        more = rows[32 * k : 32 * k + 32, :]
        v1[2 + 2 * k] = v1[2 + 2 * k] + more
        v1[3 + 2 * k] = v1[3 + 2 * k] + more
    sweep(v1, u1, s1, w1, ax1, ay1, az1, 2, 18)
    sweep(u1, v1, s1, w1, ax1, ay1, az1, 2, 18)
    sweep(v1, u1, s1, w1, ax1, ay1, az1, 2, 18)
    base = sc[0] * 4
    near = jnp.concatenate([u1[base + k] for k in range(8)], axis=0)
    wide = exact_dot(near, lane_spread(128, 256))
    for lanes, ref in ((slice(0, 128), wide_a), (slice(128, 256), wide_b)):
        for k in range(8):
            ref[80 * k : 80 * k + 8, :] = jnp.zeros((8, 128), F32)
            ref[80 * k + 72 : 80 * k + 80, :] = jnp.zeros((8, 128), F32)
            part = wide[32 * k : 32 * k + 32, lanes]
            ref[pl.ds(80 * k + 8, 32, stride=2), :] = part
            ref[pl.ds(80 * k + 9, 32, stride=2), :] = part


def postsmooth(sc, s, v, coefs, wide_a, wide_b, va, vb):
    ax, ay, az, w = coefs
    row = pl.multiple_of(sc[1] * 8, 8)
    for i in range(3, 19):
        k = (i - 3) // 2
        more = jnp.concatenate(
            [wide_a[pl.ds(80 * k + row, 24), :], wide_b[pl.ds(80 * k + row, 24), :]], axis=1
        )
        va[i] = v[i] + more
    sweep(va, vb, s, w, ax, ay, az, 4, 18)
    sweep(vb, va, s, w, ax, ay, az, 5, 17)


POST_SCRATCH = (
    [pltpu.VMEM(L1, F32)] * 3
    + [pltpu.VMEM(L2, F32)] * 3
    + [pltpu.VMEM((256, 128), F32)]
    + [pltpu.VMEM((640, 128), F32)] * 2
    + [pltpu.VMEM(REGION, F32)] * 2
)


def post_own_body(
    sc, parts, ax1, ay1, az1, w1, d1, ax2, ay2, az2, w2, d2, s, v, ax, ay, az, w, out, *scratch
):
    *inner, wide_a, wide_b, va, vb = scratch
    correct(
        sc,
        parts,
        (ax1, ay1, az1, w1, d1),
        (ax2, ay2, az2, w2, d2),
        *inner,
        wide_a,
        wide_b,
    )
    postsmooth(sc, s, v, (ax, ay, az, w), wide_a, wide_b, va, vb)
    for i in range(8):
        centre, total = around(va, ax, ay, az, i + 7)
        new = 0.2 * centre + w[i + 7] * (s[i + 7] + total)
        out[i] = new[8:16, 0:128]


def post_near_body(
    sc, parts, ax1, ay1, az1, w1, d1, ax2, ay2, az2, w2, d2, s, v, ax, ay, az, w, p, out, *scratch
):
    *inner, wide_a, wide_b, va, vb = scratch
    correct(
        sc,
        parts,
        (ax1, ay1, az1, w1, d1),
        (ax2, ay2, az2, w2, d2),
        *inner,
        wide_a,
        wide_b,
    )
    postsmooth(sc, s, v, (ax, ay, az, w), wide_a, wide_b, va, vb)
    for i in range(10):
        centre, total = around(va, ax, ay, az, i + 6)
        out[i] = p[i + 6] + 0.2 * centre + w[i + 6] * (s[i + 6] + total)


def closure_body(
    sc, features, kin, bias, kout, velocity, target, flux, slope, hidden, face_x, face_y, face_z
):
    _, high = opens_of(sc)
    high_x = jnp.where(sc[0] == 3, high[0], F32(1.0))
    high_y = jnp.where(sc[1] == 7, high[1], F32(1.0))
    high_z = jnp.where(sc[2] == 7, high[2], F32(1.0))
    row = lax.broadcasted_iota(jnp.int32, (8, 128), 0)
    col = lax.broadcasted_iota(jnp.int32, (8, 128), 1)
    factor_y = jnp.where(row == 7, high_y, F32(1.0))
    factor_z = jnp.where(col == 127, high_z, F32(1.0))

    def one(x):
        columns = features[:, x, :, :].astype(F32).reshape(128, 128).astype(BF16)
        before = jnp.dot(kin[...], columns, preferred_element_type=F32) + bias[...]
        gate = 1.0 / (1.0 + jnp.exp(-before))
        unit = (before * gate).astype(BF16)
        hidden[x] = unit
        slope[x] = gate * (1.0 + before * (1.0 - gate))
        shift = jnp.dot(kout[...], unit, preferred_element_type=F32)
        factor_x = jnp.where(x == 7, high_x, F32(1.0))
        flux[0, x] = (velocity[0, x] + shift[0:8]) * factor_x
        flux[1, x] = (velocity[1, x] + shift[8:16]) * factor_y
        flux[2, x] = (velocity[2, x] + shift[16:24]) * factor_z

    planes(0, 8, one, 1)
    face_x[0] = flux[0, 7]
    face_x[1] = target[0, 7]
    for x in range(8):
        face_y[0, x : x + 1, :] = flux[1, x, 7:8, :]
        face_y[1, x : x + 1, :] = target[1, x, 7:8, :]
    face_z[0] = flux[2]
    face_z[1] = target[2]


def shifted(field, low_x, low_y, low_z, x):
    row = lax.broadcasted_iota(jnp.int32, (8, 128), 0)
    col = lax.broadcasted_iota(jnp.int32, (8, 128), 1)
    before_x = low_x() if x == 0 else field(0, x - 1)
    before_y = jnp.where(row == 0, low_y(x), forth(field(1, x), 0))
    before_z = jnp.where(col == 0, low_z(x), forth(field(2, x), 1))
    return before_x, before_y, before_z


def source_body(flux, low_x, low_y, low_z, out):
    for x in range(8):
        bx, by, bz = shifted(
            lambda d, i: flux[d, i],
            lambda: low_x[0],
            lambda i: jnp.broadcast_to(low_y[0, i : i + 1, :], (8, 128)),
            lambda i: forth(low_z[0, i], 1),
            x,
        )
        out[x] = -((flux[0, x] - bx) + (flux[1, x] - by) + (flux[2, x] - bz))


def middle_body(sc, near, flux, target, low_x, low_y, low_z, ax, ay, az, new, misfit, out):
    scale = F32(1.0 / CELLS)
    inner = [jnp.where(sc[d] > 0, F32(1.0), F32(0.0)) for d in range(3)]

    def rises(i):
        p = near[i]
        return p, back(p, 0) - p, back(p, 1) - p

    for x in range(8):
        p, rise_y, rise_z = rises(x + 1)
        rise_x = near[x + 2] - p
        parts = (ax[x + 7] * rise_x, ay[x + 7] * rise_y, az[x + 7] * rise_z)
        for d in range(3):
            value = flux[d, x] - parts[d][8:16, 0:128]
            new[d, x] = value
            misfit[d, x] = (value - target[d, x]) * scale

    def low_weighted_x():
        up = ax[6, 8:16, 0:128]
        rise = (near[1] - near[0])[8:16, 0:128]
        return up * ((low_x[0] - up * rise - low_x[1]) * (scale * inner[0]))

    def low_weighted_y(x):
        up = ay[x + 7, 7:8, 0:128]
        rise = near[x + 1, 8:9, 0:128] - near[x + 1, 7:8, 0:128]
        value = low_y[0, x : x + 1, :] - up * rise - low_y[1, x : x + 1, :]
        return jnp.broadcast_to(up * (value * (scale * inner[1])), (8, 128))

    def low_weighted_z(x):
        p = near[x + 1, 8:16, :]
        rise = (back(p, 1) - p)[:, 128:256]
        up = az[x + 7, 8:16, 128:256]
        value = up * ((low_z[0, x] - up * rise - low_z[1, x]) * (scale * inner[2]))
        return forth(value, 1)

    refs = (ax, ay, az)

    def weighted(d, x):
        return refs[d][x + 7, 8:16, 0:128] * misfit[d, x]

    for x in range(8):
        bx, by, bz = shifted(weighted, low_weighted_x, low_weighted_y, low_weighted_z, x)
        out[x] = (weighted(0, x) - bx) + (weighted(1, x) - by) + (weighted(2, x) - bz)


def gradient_body(sc, near, misfit, features, slope, hidden, kback, out, acc_in, acc_bias, acc_out):
    _, high = opens_of(sc)
    high_x = jnp.where(sc[0] == 3, high[0], F32(1.0))
    high_y = jnp.where(sc[1] == 7, high[1], F32(1.0))
    high_z = jnp.where(sc[2] == 7, high[2], F32(1.0))
    row = lax.broadcasted_iota(jnp.int32, (8, 128), 0)
    col = lax.broadcasted_iota(jnp.int32, (8, 128), 1)
    factor_y = jnp.where(row == 7, high_y, F32(1.0))
    factor_z = jnp.where(col == 127, high_z, F32(1.0))
    acc_in[...] = jnp.zeros((128, 512), F32)
    acc_bias[...] = jnp.zeros((512, 128), F32)
    acc_out[...] = jnp.zeros((24, 512), F32)
    across = (((1,), (1,)), ((), ()))

    def one(x):
        p = near[x + 1]
        rise_x = (near[x + 2] - p)[8:16, 0:128]
        rise_y = (back(p, 0) - p)[8:16, 0:128]
        rise_z = (back(p, 1) - p)[8:16, 0:128]
        factor_x = jnp.where(x == 7, high_x, F32(1.0))
        grads = jnp.concatenate(
            [
                (misfit[0, x] + rise_x) * factor_x,
                (misfit[1, x] + rise_y) * factor_y,
                (misfit[2, x] + rise_z) * factor_z,
            ],
            axis=0,
        ).astype(BF16)
        columns = features[:, x, :, :].astype(F32).reshape(128, 128).astype(BF16)
        grad_before = jnp.dot(kback[...], grads, preferred_element_type=F32) * slope[x]
        acc_bias[...] += grad_before
        acc_in[...] += lax.dot_general(
            columns, grad_before.astype(BF16), across, preferred_element_type=F32
        )
        acc_out[...] += lax.dot_general(grads, hidden[x], across, preferred_element_type=F32)

    planes(0, 8, one, 1)

    def same(count):
        r = lax.broadcasted_iota(jnp.int32, (count, 512), 0)
        c = lax.broadcasted_iota(jnp.int32, (count, 512), 1)
        return r % 8 == c % 8

    def grouped(count, groups):
        r = lax.broadcasted_iota(jnp.int32, (groups, count), 0)
        c = lax.broadcasted_iota(jnp.int32, (groups, count), 1)
        return jnp.where(c // 8 == r, F32(1.0), F32(0.0))

    hr = lax.broadcasted_iota(jnp.int32, (512, 64), 0)
    hc = lax.broadcasted_iota(jnp.int32, (512, 64), 1)
    fold = jnp.where(hr // 8 == hc, F32(1.0), F32(0.0))
    in_part = exact_dot(grouped(128, 16), jnp.where(same(128), acc_in[...], F32(0.0)))
    out_part = exact_dot(grouped(24, 8), jnp.where(same(24), acc_out[...], F32(0.0)))
    bias_part = lax.dot_general(
        jnp.ones((8, 128), F32), acc_bias[...], across, precision=HIGHEST, preferred_element_type=F32
    )
    folded = exact_dot(jnp.concatenate([in_part, out_part, bias_part], axis=0), fold)
    out[0:8, 0:64] = folded[0:8]
    out[0:8, 64:128] = folded[8:16]
    out[8:16, 0:64] = folded[16:24]
    out[8:16, 64:128] = folded[24:32]


def ups(axis):
    count = lax.axis_size(axis)
    return [(i, i + 1) for i in range(count - 1)]


def downs(axis):
    return [(b, a) for a, b in ups(axis)]


def exchanged(own):
    after = lax.ppermute(own, "gz", downs("gz"))
    before = lax.ppermute(own, "gz", ups("gz"))
    lane = lax.broadcasted_iota(jnp.int32, own.shape, 3)
    wide = jnp.concatenate([own, jnp.where(lane < 64, after, before)], axis=3)
    low = lax.ppermute(wide[:, 1:8], "gx", ups("gx"))
    high = lax.ppermute(wide[:, 0:7], "gx", downs("gx"))
    wide = jnp.concatenate([low, wide, high], axis=1)
    low = lax.ppermute(wide, GY, ups(GY))
    high = lax.ppermute(wide, GY, downs(GY))
    return jnp.concatenate([low, wide, high], axis=2)


def over_plane(part):
    copies = jnp.broadcast_to(part, (32, *part.shape))
    return lax.all_to_all(copies, XY, split_axis=0, concat_axis=0, tiled=True)


def summed(part, axes):
    for axis in axes:
        copies = jnp.broadcast_to(part, (lax.axis_size(axis), *part.shape))
        part = jnp.sum(lax.all_to_all(copies, axis, split_axis=0, concat_axis=0, tiled=True), axis=0)
    return part


def per_device(velocity, features, density, target, weight_in, bias_in, weight_out, open_faces):
    place = jnp.stack([lax.axis_index("gx"), lax.axis_index(GY), lax.axis_index("gz")])
    sc = jnp.concatenate([place.astype(jnp.int32), open_faces])
    eye = jnp.eye(8, dtype=BF16)
    kin = jnp.kron(weight_in.T, eye)
    kout = jnp.kron(weight_out.T, eye)
    kback = jnp.kron(weight_out, eye)
    bias = jnp.broadcast_to(bias_in[:, None, None], (64, 8, 128)).reshape(512, 128)
    block = (8, 8, 128)
    flux, slope, hidden, face_x, face_y, face_z = call(
        closure_body,
        [
            shaped((3, *block)),
            shaped((8, 512, 128)),
            shaped((8, 512, 128), BF16),
            shaped((2, 8, 128)),
            shaped((2, 8, 128)),
            shaped((2, *block)),
        ],
        (sc, features, kin, bias, kout, velocity, target),
        smem=(0,),
    )
    low_x = lax.ppermute(face_x, "gx", ups("gx"))
    low_y = lax.ppermute(face_y, GY, ups(GY))
    low_z = lax.ppermute(face_z, "gz", ups("gz"))
    (source,) = call(source_body, [shaped(block)], (flux, low_x, low_y, low_z))
    both = exchanged(jnp.stack([source, density]))
    region = shaped(REGION)
    one_region = [pltpu.VMEM(REGION, F32), pltpu.VMEM((32, 128), F32)]
    *coefs, v, part = call(
        start_body,
        [region] * 6 + [shaped((32, 128))],
        (sc, both[0], both[1]),
        one_region,
        smem=(0,),
    )
    ax, ay, az, w, d = coefs
    parts = over_plane(part)
    coarse = call(
        coarse_body,
        [shaped(L1)] * 5 + [shaped(L2)] * 5,
        (sc, parts),
        [pltpu.VMEM(L1, F32), pltpu.VMEM(L2, F32), pltpu.VMEM((256, 128), F32)],
        smem=(0,),
    )

    def finish_solve(b, v, parts):
        (own,) = call(
            post_own_body,
            [shaped(block)],
            (sc, parts, *coarse, b, v, ax, ay, az, w),
            POST_SCRATCH,
            smem=(0,),
        )
        p = exchanged(own[None])[0]
        s, v, part = call(
            again_body, [region, region, shaped((16, 128))], (b, p, *coefs), one_region
        )
        (near,) = call(
            post_near_body,
            [shaped((10, NYP, NZP))],
            (sc, over_plane(part), *coarse, s, v, ax, ay, az, w, p),
            POST_SCRATCH,
            smem=(0,),
        )
        return near

    near = finish_solve(both[0], v, parts)
    new_velocity, misfit, grad_pressure = call(
        middle_body,
        [shaped((3, *block)), shaped((3, *block)), shaped(block)],
        (sc, near, flux, target, low_x, low_y, low_z, ax, ay, az),
        smem=(0,),
    )
    b = exchanged(grad_pressure[None])[0]
    v, part = call(pre_body, [region, shaped((16, 128))], (b, *coefs), one_region)
    near = finish_solve(b, v, over_plane(part))
    (packed,) = call(
        gradient_body,
        [shaped((16, 128))],
        (sc, near, misfit, features, slope, hidden, kback),
        [pltpu.VMEM((128, 512), F32), pltpu.VMEM((512, 128), F32), pltpu.VMEM((24, 512), F32)],
        smem=(0,),
    )
    total = summed(packed, (("gy_1", "gz"), ("gx", "gy_0")))
    grad_in = jnp.concatenate([total[0:8, 0:64], total[0:8, 64:128]], axis=0)
    return new_velocity, grad_in, total[8, 64:128], total[8:11, 0:64].T


def solution(mesh):
    split = Mesh(
        mesh.devices.reshape(mesh.shape["gx"], 4, 2, mesh.shape["gz"]), ("gx", "gy_0", "gy_1", "gz")
    )
    placed = (
        P(None, "gx", GY, "gz"),
        P(None, "gx", GY, "gz"),
        P("gx", GY, "gz"),
        P(None, "gx", GY, "gz"),
        P(),
        P(),
        P(),
        P(),
    )
    return jax.shard_map(
        per_device,
        mesh=split,
        in_specs=placed,
        out_specs=(P(None, "gx", GY, "gz"), P(), P(), P()),
        check_vma=False,
    )
```

profile of v0, /device:TPU:1, one launch (start us, length us, event | category | flops | bytes accessed | tf_op | source)
XLA Modules:
  0.0 297.0 jit_solution(17843459560634444698)
XLA Ops:
  2.3 2.3 mul.79.kin
  5.7 3.6 %shard_map.111 = (f32[3,8,8,128]{3,2,1,0:T(8,128)S(1)}, f32[8,512,128]{2,1,0:T(8,128)S(1)}, bf16[8,512,128]{2,1,0:T(8,128)(2,1)S(1)}, f32[2,8,128]{2,1,0:T(8,128...) custom-call(s32[9]{0:T(128)S(1)} %pad_add_fusion.sc, bf16[16,8,8,128]{3,2,1,0:T(8,128)(2,1)S(1)} %copy-done.14, ...), custom_call_target="tpu_custom_call" | custom-call | tf_op jit(solution)/shard_map/pallas_call | solution.py:32
  9.3 4.4 %collective-permute-start.2 = (f32[2,8,8,128]{3,2,1,0:T(8,128)S(1)}, f32[2,8,8,128]{3,2,1,0:T(8,128)S(1)}, u32[]{:S(2)}, u32[]{:S(2)}) collective-permute-start(f32[2,8,8,128]{3,2,1,0:T(8,128)S(1)} %get-tuple-element.41), channel_id=1, source_target_pairs={{0,1},{1,2},{2,3},{3,4},{4,5},{5,6},{6,7},{8,9},{9,10},{10,11},{11... | collective-permute-start | bytes 196616 | tf_op jit(solution)/shard_map/ppermute | solution.py:559
  13.7 3.2 %collective-permute-start = (f32[2,8,128]{2,1,0:T(8,128)S(1)}, f32[2,8,128]{2,1,0:T(8,128)S(1)}, u32[]{:S(2)}, u32[]{:S(2)}) collective-permute-start(f32[2,8,128]{2,1,0:T(8,128)S(1)} %get-tuple-element.39), channel_id=1, source_target_pairs={{0,64},{64,128},{128,192},{1,65},{65,129},{129,193},{2,66},{66,130... | collective-permute-start | bytes 24584 | tf_op jit(solution)/shard_map/ppermute | solution.py:557
  16.9 4.2 %collective-permute-start.1 = (f32[2,8,128]{2,1,0:T(8,128)S(1)}, f32[2,8,128]{2,1,0:T(8,128)S(1)}, u32[]{:S(2)}, u32[]{:S(2)}) collective-permute-start(f32[2,8,128]{2,1,0:T(8,128)S(1)} %get-tuple-element.40), channel_id=1, source_target_pairs={{0,8},{8,16},{16,24},{24,32},{32,40},{40,48},{48,56},{1,9},{9,17},... | collective-permute-start | bytes 24584 | tf_op jit(solution)/shard_map/ppermute | solution.py:558
  22.0 1.3 collective-permute-start.3
  23.3 4.2 %collective-permute-start.4 = (f32[2,8,8,128]{3,2,1,0:T(8,128)S(1)}, f32[2,8,8,128]{3,2,1,0:T(8,128)S(1)}, u32[]{:S(2)}, u32[]{:S(2)}) collective-permute-start(f32[2,8,8,128]{3,2,1,0:T(8,128)S(1)} %pad_maximum_fusion.6), channel_id=1, source_target_pairs={{0,1},{1,2},{2,3},{3,4},{4,5},{5,6},{6,7},{8,9},{9,10},{10,11},{11... | collective-permute-start | bytes 196616 | tf_op jit(solution)/shard_map/ppermute | solution.py:512
  27.6 1.3 collective-permute-done.4
  28.9 3.2 %collective-permute-start.5 = (f32[2,7,8,256]{3,2,1,0:T(8,128)S(1)}, f32[2,7,8,256]{3,2,1,0:T(8,128)S(1)}, u32[]{:S(2)}, u32[]{:S(2)}) collective-permute-start(f32[2,7,8,256]{3,2,1,0:T(8,128)S(1)} %get-tuple-element.74), channel_id=1, source_target_pairs={{0,64},{64,128},{128,192},{1,65},{65,129},{129,193},{2,66},{66,130... | collective-permute-start | bytes 344072 | tf_op jit(solution)/shard_map/ppermute | solution.py:515
  32.1 1.3 collective-permute-start.6
  33.4 1.4 collective-permute-done.5
  34.8 4.4 %collective-permute-done.6 = f32[2,7,8,256]{3,2,1,0:T(8,128)S(1)} collective-permute-done((f32[2,7,8,256]{3,2,1,0:T(8,128)S(1)}, f32[2,7,8,256]{3,2,1,0:T(8,128)S(1)}, u32[]{:S(2)}, u32[]{:S(2)}) %collective-permute-start.6) | collective-permute-done | bytes 114720 | tf_op jit(solution)/shard_map/ppermute | solution.py:516
  39.2 5.1 %collective-permute-start.7 = (f32[2,22,8,256]{3,2,1,0:T(8,128)S(1)}, f32[2,22,8,256]{3,2,1,0:T(8,128)S(1)}, u32[]{:S(2)}, u32[]{:S(2)}) collective-permute-start(f32[2,22,8,256]{3,2,1,0:T(8,128)S(1)} %pad_maximum_fusion.1), channel_id=1, source_target_pairs={{0,8},{8,16},{16,24},{24,32},{32,40},{40,48},{48,56},{1,9},{9,17},... | collective-permute-start | bytes 1081352 | tf_op jit(solution)/shard_map/ppermute | solution.py:518
  44.3 1.9 collective-permute-start.8
  46.2 2.4 collective-permute-done.7
  48.6 4.4 %collective-permute-done.8 = f32[2,22,8,256]{3,2,1,0:T(8,128)S(1)} collective-permute-done((f32[2,22,8,256]{3,2,1,0:T(8,128)S(1)}, f32[2,22,8,256]{3,2,1,0:T(8,128)S(1)}, u32[]{:S(2)}, u32[]{:S(2)}) %collective-permute-start.8) | collective-permute-done | bytes 360480 | tf_op jit(solution)/shard_map/ppermute | solution.py:519
  53.2 6.4 %shard_map.113 = (f32[22,24,256]{2,1,0:T(8,128)S(1)}, f32[22,24,256]{2,1,0:T(8,128)S(1)}, f32[22,24,256]{2,1,0:T(8,128)S(1)}, f32[22,24,256]{2,1,0:T(8,128)S(1)}...) custom-call(s32[9]{0:T(128)S(1)} %pad_add_fusion.sc, ...), custom_call_target="tpu_custom_call" | custom-call | tf_op jit(solution)/shard_map/pallas_call | solution.py:32
  59.7 16.3 %all_to_all.30.parts = f32[32,32,128]{2,1,0:T(8,128)S(1)} all-to-all(f32[32,32,128]{2,1,0:T(8,128)S(1)} %broadcast_in_dim.52), channel_id=1, replica_groups=mesh['gx'=4,'gy_0'=4,'gy_1'=2,'gz'=8] {'gx','gy_0','gy_1'}, dimensions={0} | all-to-all | bytes 1048576 | tf_op jit(solution)/shard_map/all_to_all | solution.py:525
  75.9 5.1 %shard_map.114 = (f32[20,32,128]{2,1,0:T(8,128)S(1)}, f32[20,32,128]{2,1,0:T(8,128)S(1)}, f32[20,32,128]{2,1,0:T(8,128)S(1)}, f32[20,32,128]{2,1,0:T(8,128)S(1)}...) custom-call(s32[9]{0:T(128)S(1)} %pad_add_fusion.sc, ...), custom_call_target="tpu_custom_call" | custom-call | tf_op jit(solution)/shard_map/pallas_call | solution.py:32
  81.1 8.6 %shard_map.115 = f32[8,8,128]{2,1,0:T(8,128)S(1)} custom-call(s32[9]{0:T(128)S(1)} %pad_add_fusion.sc, f32[32,32,128]{2,1,0:T(8,128)S(1)} %all_to_all.30.parts, f32[20,32,128]{2,1,0:T(8,128)S(1)} %get-tuple-element.43.ax1, f32[20,32,128]{2,1,0:T(8,128)S(1)} %get-tuple-element.44.ay1, f32[20,32,128]{2,1,0:T(8,128)S(1)} %get-tuple-element.45.az1, ...), custom_call_target="tpu_custom_call" | custom-call | tf_op jit(solution)/shard_map/pallas_call | solution.py:32
  89.7 4.0 %collective-permute-start.10 = (f32[1,8,8,128]{3,2,1,0:T(8,128)S(1)}, f32[1,8,8,128]{3,2,1,0:T(8,128)S(1)}, u32[]{:S(2)}, u32[]{:S(2)}) collective-permute-start(f32[1,8,8,128]{3,2,1,0:T(8,128)S(1)} %bitcast.41), channel_id=1, source_target_pairs={{0,1},{1,2},{2,3},{3,4},{4,5},{5,6},{6,7},{8,9},{9,10},{10,11},{11... | collective-permute-start | bytes 98312 | tf_op jit(solution)/shard_map/ppermute | solution.py:512
  93.7 1.3 collective-permute-start.9
  95.1 4.2 %collective-permute-done.9 = f32[1,8,8,128]{3,2,1,0:T(8,128)S(1)} collective-permute-done((f32[1,8,8,128]{3,2,1,0:T(8,128)S(1)}, f32[1,8,8,128]{3,2,1,0:T(8,128)S(1)}, u32[]{:S(2)}, u32[]{:S(2)}) %collective-permute-start.9) | collective-permute-done | bytes 32800 | tf_op jit(solution)/shard_map/ppermute | solution.py:511
  99.3 2.8 collective-permute-start.11
  102.1 1.3 collective-permute-start.12
  103.4 3.6 %collective-permute-done.12 = f32[1,7,8,256]{3,2,1,0:T(8,128)S(1)} collective-permute-done((f32[1,7,8,256]{3,2,1,0:T(8,128)S(1)}, f32[1,7,8,256]{3,2,1,0:T(8,128)S(1)}, u32[]{:S(2)}, u32[]{:S(2)}) %collective-permute-start.12) | collective-permute-done | bytes 57376 | tf_op jit(solution)/shard_map/ppermute | solution.py:516
  107.0 3.6 %collective-permute-start.13 = (f32[1,22,8,256]{3,2,1,0:T(8,128)S(1)}, f32[1,22,8,256]{3,2,1,0:T(8,128)S(1)}, u32[]{:S(2)}, u32[]{:S(2)}) collective-permute-start(f32[1,22,8,256]{3,2,1,0:T(8,128)S(1)} %pad_maximum_fusion.2), channel_id=1, source_target_pairs={{0,8},{8,16},{16,24},{24,32},{32,40},{40,48},{48,56},{1,9},{9,17},... | collective-permute-start | bytes 540680 | tf_op jit(solution)/shard_map/ppermute | solution.py:518
  110.6 1.9 collective-permute-start.14
  113.0 4.4 %collective-permute-done.14 = f32[1,22,8,256]{3,2,1,0:T(8,128)S(1)} collective-permute-done((f32[1,22,8,256]{3,2,1,0:T(8,128)S(1)}, f32[1,22,8,256]{3,2,1,0:T(8,128)S(1)}, u32[]{:S(2)}, u32[]{:S(2)}) %collective-permute-start.14) | collective-permute-done | bytes 180256 | tf_op jit(solution)/shard_map/ppermute | solution.py:519
  117.5 3.1 %shard_map.116 = (f32[22,24,256]{2,1,0:T(8,128)S(1)}, f32[22,24,256]{2,1,0:T(8,128)S(1)}, f32[16,128]{1,0:T(8,128)S(1)}) custom-call(f32[22,24,256]{2,1,0:T(8,128)S(1)} %get-tuple-element.73.b.s, f32[22,24,256]{2,1,0:T(8,128)S(1)} %maximum_bitcast_fusion.p, f32[22,24,256]{2,1,0:T(8,128)S(1)} %get-tuple-element.54.ax, ...), custom_call_target="tpu_custom_call" | custom-call | tf_op jit(solution)/shard_map/pallas_call | solution.py:32
  120.6 14.6 %all_to_all.31.parts = f32[32,16,128]{2,1,0:T(8,128)S(1)} all-to-all(f32[32,16,128]{2,1,0:T(8,128)S(1)} %broadcast_in_dim.54), channel_id=1, replica_groups=mesh['gx'=4,'gy_0'=4,'gy_1'=2,'gz'=8] {'gx','gy_0','gy_1'}, dimensions={0} | all-to-all | bytes 524288 | tf_op jit(solution)/shard_map/all_to_all | solution.py:525
  135.2 9.3 %shard_map.117.near = f32[10,24,256]{2,1,0:T(8,128)S(1)} custom-call(s32[9]{0:T(128)S(1)} %pad_add_fusion.sc, f32[32,16,128]{2,1,0:T(8,128)S(1)} %all_to_all.31.parts, f32[20,32,128]{2,1,0:T(8,128)S(1)} %get-tuple-element.43.ax1, f32[20,32,128]{2,1,0:T(8,128)S(1)} %get-tuple-element.44.ay1, f32[20,32,128]{2,1,0:T(8,128)S(1)} %get-tuple-element.45.az1, ...), custom_call_target="tpu_custom_call" | custom-call | tf_op jit(solution)/shard_map/pallas_call | solution.py:32
  144.5 1.3 shard_map.118
  145.8 1.3 collective-permute-start.15
  147.1 5.5 %collective-permute-start.16 = (f32[1,8,8,128]{3,2,1,0:T(8,128)S(1)}, f32[1,8,8,128]{3,2,1,0:T(8,128)S(1)}, u32[]{:S(2)}, u32[]{:S(2)}) collective-permute-start(f32[1,8,8,128]{3,2,1,0:T(8,128)S(1)} %bitcast.47), channel_id=1, source_target_pairs={{0,1},{1,2},{2,3},{3,4},{4,5},{5,6},{6,7},{8,9},{9,10},{10,11},{11... | collective-permute-start | bytes 98312 | tf_op jit(solution)/shard_map/ppermute | solution.py:512
  153.6 2.2 collective-permute-start.17
  155.8 1.3 collective-permute-start.18
  157.1 3.6 %collective-permute-done.18 = f32[1,7,8,256]{3,2,1,0:T(8,128)S(1)} collective-permute-done((f32[1,7,8,256]{3,2,1,0:T(8,128)S(1)}, f32[1,7,8,256]{3,2,1,0:T(8,128)S(1)}, u32[]{:S(2)}, u32[]{:S(2)}) %collective-permute-start.18) | collective-permute-done | bytes 57376 | tf_op jit(solution)/shard_map/ppermute | solution.py:516
  160.7 4.3 %collective-permute-start.19 = (f32[1,22,8,256]{3,2,1,0:T(8,128)S(1)}, f32[1,22,8,256]{3,2,1,0:T(8,128)S(1)}, u32[]{:S(2)}, u32[]{:S(2)}) collective-permute-start(f32[1,22,8,256]{3,2,1,0:T(8,128)S(1)} %pad_maximum_fusion.3), channel_id=1, source_target_pairs={{0,8},{8,16},{16,24},{24,32},{32,40},{40,48},{48,56},{1,9},{9,17},... | collective-permute-start | bytes 540680 | tf_op jit(solution)/shard_map/ppermute | solution.py:518
  165.1 1.9 collective-permute-start.20
  167.5 4.4 %collective-permute-done.20 = f32[1,22,8,256]{3,2,1,0:T(8,128)S(1)} collective-permute-done((f32[1,22,8,256]{3,2,1,0:T(8,128)S(1)}, f32[1,22,8,256]{3,2,1,0:T(8,128)S(1)}, u32[]{:S(2)}, u32[]{:S(2)}) %collective-permute-start.20) | collective-permute-done | bytes 180256 | tf_op jit(solution)/shard_map/ppermute | solution.py:519
  171.9 2.1 shard_map.119
  174.1 14.1 %all_to_all.32.parts = f32[32,16,128]{2,1,0:T(8,128)S(1)} all-to-all(f32[32,16,128]{2,1,0:T(8,128)S(1)} %broadcast_in_dim.56), channel_id=1, replica_groups=mesh['gx'=4,'gy_0'=4,'gy_1'=2,'gz'=8] {'gx','gy_0','gy_1'}, dimensions={0} | all-to-all | bytes 524288 | tf_op jit(solution)/shard_map/all_to_all | solution.py:525
  188.2 8.6 %shard_map.120 = f32[8,8,128]{2,1,0:T(8,128)S(1)} custom-call(s32[9]{0:T(128)S(1)} %pad_add_fusion.sc, f32[32,16,128]{2,1,0:T(8,128)S(1)} %all_to_all.32.parts, f32[20,32,128]{2,1,0:T(8,128)S(1)} %get-tuple-element.43.ax1, f32[20,32,128]{2,1,0:T(8,128)S(1)} %get-tuple-element.44.ay1, f32[20,32,128]{2,1,0:T(8,128)S(1)} %get-tuple-element.45.az1, ...), custom_call_target="tpu_custom_call" | custom-call | tf_op jit(solution)/shard_map/pallas_call | solution.py:32
  196.8 1.3 collective-permute-start.21
  198.1 5.8 %collective-permute-start.22 = (f32[1,8,8,128]{3,2,1,0:T(8,128)S(1)}, f32[1,8,8,128]{3,2,1,0:T(8,128)S(1)}, u32[]{:S(2)}, u32[]{:S(2)}) collective-permute-start(f32[1,8,8,128]{3,2,1,0:T(8,128)S(1)} %bitcast.37), channel_id=1, source_target_pairs={{0,1},{1,2},{2,3},{3,4},{4,5},{5,6},{6,7},{8,9},{9,10},{10,11},{11... | collective-permute-start | bytes 98312 | tf_op jit(solution)/shard_map/ppermute | solution.py:512
  205.0 2.2 collective-permute-start.23
  207.2 1.3 collective-permute-start.24
  208.5 3.6 %collective-permute-done.24 = f32[1,7,8,256]{3,2,1,0:T(8,128)S(1)} collective-permute-done((f32[1,7,8,256]{3,2,1,0:T(8,128)S(1)}, f32[1,7,8,256]{3,2,1,0:T(8,128)S(1)}, u32[]{:S(2)}, u32[]{:S(2)}) %collective-permute-start.24) | collective-permute-done | bytes 57376 | tf_op jit(solution)/shard_map/ppermute | solution.py:516
  212.2 4.3 %collective-permute-start.25 = (f32[1,22,8,256]{3,2,1,0:T(8,128)S(1)}, f32[1,22,8,256]{3,2,1,0:T(8,128)S(1)}, u32[]{:S(2)}, u32[]{:S(2)}) collective-permute-start(f32[1,22,8,256]{3,2,1,0:T(8,128)S(1)} %pad_maximum_fusion.4), channel_id=1, source_target_pairs={{0,8},{8,16},{16,24},{24,32},{32,40},{40,48},{48,56},{1,9},{9,17},... | collective-permute-start | bytes 540680 | tf_op jit(solution)/shard_map/ppermute | solution.py:518
  216.5 1.9 collective-permute-start.26
  218.9 4.4 %collective-permute-done.26 = f32[1,22,8,256]{3,2,1,0:T(8,128)S(1)} collective-permute-done((f32[1,22,8,256]{3,2,1,0:T(8,128)S(1)}, f32[1,22,8,256]{3,2,1,0:T(8,128)S(1)}, u32[]{:S(2)}, u32[]{:S(2)}) %collective-permute-start.26) | collective-permute-done | bytes 180256 | tf_op jit(solution)/shard_map/ppermute | solution.py:519
  223.4 3.1 %shard_map.121 = (f32[22,24,256]{2,1,0:T(8,128)S(1)}, f32[22,24,256]{2,1,0:T(8,128)S(1)}, f32[16,128]{1,0:T(8,128)S(1)}) custom-call(f32[22,24,256]{2,1,0:T(8,128)S(1)} %maximum_bitcast_fusion.1.b.s, f32[22,24,256]{2,1,0:T(8,128)S(1)} %maximum_bitcast_fusion.2.p, f32[22,24,256]{2,1,0:T(8,128)S(1)} %get-tuple-element.54.ax, ...), custom_call_target="tpu_custom_call" | custom-call | tf_op jit(solution)/shard_map/pallas_call | solution.py:32
  228.8 5.4 %all-to-all-start.3 = ((f32[32,16,128]{2,1,0:T(8,128)}), f32[32,16,128]{2,1,0:T(8,128)}, u32[]{:S(2)}, u32[]{:S(2)}) async-start(f32[32,16,128]{2,1,0:T(8,128)} %broadcast_in_dim.58), calls=%async_computation.3 | async-start | bytes 524288 | tf_op jit(solution)/shard_map/all_to_all | solution.py:525
  234.3 1.5 broadcast_multiply_fusion.1
  235.8 2.1 mul.87
  237.9 1.5 copy.21.kback
  239.4 3.8 %all-to-all-done.3.parts = f32[32,16,128]{2,1,0:T(8,128)} async-done(((f32[32,16,128]{2,1,0:T(8,128)}), f32[32,16,128]{2,1,0:T(8,128)}, u32[]{:S(2)}, u32[]{:S(2)}) %all-to-all-start.3) | async-done | bytes 262176 | tf_op jit(solution)/shard_map/all_to_all | solution.py:525
  247.7 1.0 copy-done.19
  248.8 1.0 copy-done.21
  250.5 9.5 %shard_map.122.near = f32[10,24,256]{2,1,0:T(8,128)S(1)} custom-call(s32[9]{0:T(128)S(1)} %copy-done.29, f32[32,16,128]{2,1,0:T(8,128)} %all-to-all-done.3.parts, f32[20,32,128]{2,1,0:T(8,128)S(1)} %get-tuple-element.43.ax1, f32[20,32,128]{2,1,0:T(8,128)S(1)} %get-tuple-element.44.ay1, f32[20,32,128]{2,1,0:T(8,128)S(1)} %get-tuple-element.45.az1, ...), custom_call_target="tpu_custom_call" | custom-call | tf_op jit(solution)/shard_map/pallas_call | solution.py:32
  260.1 4.9 %shard_map.123 = f32[16,128]{1,0:T(8,128)S(1)} custom-call(s32[9]{0:T(128)S(1)} %copy-done.29, f32[10,24,256]{2,1,0:T(8,128)S(1)} %shard_map.122.near, f32[3,8,8,128]{3,2,1,0:T(8,128)S(1)} %copy-done.27, bf16[16,8,8,128]{3,2,1,0:T(8,128)(2,1)S(1)} %copy-done.15, f32[8,512,128]{2,1,0:T(8,128)S(1)} %copy-done.5, bf16[8,512,128]{2,1,0:T(8,128)(2,1)S(1)} %copy-done.17, ...), custom_call_target="tpu_custom_call" | custom-call | tf_op jit(solution)/shard_map/pallas_call | solution.py:32
  264.9 20.3 %all_to_all.33 = f32[16,16,128]{2,1,0:T(8,128)S(1)} all-to-all(f32[16,16,128]{2,1,0:T(8,128)S(1)} %broadcast_in_dim.59), channel_id=1, replica_groups=mesh['gx'=4,'gy_0'=4,'gy_1'=2,'gz'=8] {'gy_1','gz'}, dimensions={0} | all-to-all | bytes 262144 | tf_op jit(solution)/shard_map/all_to_all | solution.py:531
  285.3 9.9 %all_to_all.34 = f32[16,16,128]{2,1,0:T(8,128)S(1)} all-to-all(f32[16,16,128]{2,1,0:T(8,128)S(1)} %broadcast_in_dim.60), channel_id=1, replica_groups=mesh['gx'=4,'gy_0'=4,'gy_1'=2,'gz'=8] {'gx','gy_0'}, dimensions={0} | all-to-all | bytes 262144 | tf_op jit(solution)/shard_map/all_to_all | solution.py:531
  (126 shorter events, 17.0 us)
Async XLA Ops:
  0.6 0.6 copy-start.31
  2.2 2.3 copy-start.32
  2.2 3.0 %copy-start.33 = (f32[64]{0:T(128)S(1)}, f32[64]{0:T(128)}, u32[]{:S(2)}) copy-start(f32[64]{0:T(128)} %param.13) | copy-start | bytes 772
  2.2 3.2 %copy-start.34 = (s32[6]{0:T(128)S(1)}, s32[6]{0:T(128)}, u32[]{:S(2)}) copy-start(s32[6]{0:T(128)} %param.15) | copy-start | bytes 76
  4.5 1.1 copy-start.14
  4.5 1.1 copy-start.23
  4.6 1.1 copy-start.25
  4.6 17.4 %copy-start.30 = (f32[8,8,128]{2,1,0:T(8,128)S(1)}, f32[8,8,128]{2,1,0:T(8,128)}, u32[]{:S(2)}) copy-start(f32[8,8,128]{2,1,0:T(8,128)} %param.10) | copy-start | bytes 98308
  5.5 182.6 %copy-start.28 = (s32[9]{0:T(128)}, s32[9]{0:T(128)S(1)}, u32[]{:S(2)}) copy-start(s32[9]{0:T(128)S(1)} %pad_add_fusion.sc) | copy-start | bytes 112
  9.3 43.8 %copy-start.4 = (f32[8,512,128]{2,1,0:T(8,128)}, f32[8,512,128]{2,1,0:T(8,128)S(1)}, u32[]{:S(2)}) copy-start(f32[8,512,128]{2,1,0:T(8,128)S(1)} %get-tuple-element.70.slope) | copy-start | bytes 6291460
  9.3 43.8 %copy-start.16 = (bf16[8,512,128]{2,1,0:T(8,128)(2,1)}, bf16[8,512,128]{2,1,0:T(8,128)(2,1)S(1)}, u32[]{:S(2)}) copy-start(bf16[8,512,128]{2,1,0:T(8,128)(2,1)S(1)} %get-tuple-element.71.hidden) | copy-start | bytes 3145732
  9.3 12.6 %collective-permute-start.2 = (f32[2,8,8,128]{3,2,1,0:T(8,128)S(1)}, f32[2,8,8,128]{3,2,1,0:T(8,128)S(1)}, u32[]{:S(2)}, u32[]{:S(2)}) collective-permute-start(f32[2,8,8,128]{3,2,1,0:T(8,128)S(1)} %get-tuple-element.41), channel_id=1, source_target_pairs={{0,1},{1,2},{2,3},{3,4},{4,5},{5,6},{6,7},{8,9},{9,10},{10,11},{11... | collective-permute-start | bytes 196616 | tf_op jit(solution)/shard_map/ppermute | solution.py:559
  13.7 7.5 %collective-permute-start = (f32[2,8,128]{2,1,0:T(8,128)S(1)}, f32[2,8,128]{2,1,0:T(8,128)S(1)}, u32[]{:S(2)}, u32[]{:S(2)}) collective-permute-start(f32[2,8,128]{2,1,0:T(8,128)S(1)} %get-tuple-element.39), channel_id=1, source_target_pairs={{0,64},{64,128},{128,192},{1,65},{65,129},{129,193},{2,66},{66,130... | collective-permute-start | bytes 24584 | tf_op jit(solution)/shard_map/ppermute | solution.py:557
  16.9 5.0 %collective-permute-start.1 = (f32[2,8,128]{2,1,0:T(8,128)S(1)}, f32[2,8,128]{2,1,0:T(8,128)S(1)}, u32[]{:S(2)}, u32[]{:S(2)}) collective-permute-start(f32[2,8,128]{2,1,0:T(8,128)S(1)} %get-tuple-element.40), channel_id=1, source_target_pairs={{0,8},{8,16},{16,24},{24,32},{32,40},{40,48},{48,56},{1,9},{9,17},... | collective-permute-start | bytes 24584 | tf_op jit(solution)/shard_map/ppermute | solution.py:558
  22.0 5.5 %collective-permute-start.3 = (f32[2,8,8,128]{3,2,1,0:T(8,128)S(1)}, f32[2,8,8,128]{3,2,1,0:T(8,128)S(1)}, u32[]{:S(2)}, u32[]{:S(2)}) collective-permute-start(f32[2,8,8,128]{3,2,1,0:T(8,128)S(1)} %pad_maximum_fusion.6), channel_id=1, source_target_pairs={{1,0},{2,1},{3,2},{4,3},{5,4},{6,5},{7,6},{9,8},{10,9},{11,10},{12... | collective-permute-start | bytes 196616 | tf_op jit(solution)/shard_map/ppermute | solution.py:511
  23.3 5.5 %collective-permute-start.4 = (f32[2,8,8,128]{3,2,1,0:T(8,128)S(1)}, f32[2,8,8,128]{3,2,1,0:T(8,128)S(1)}, u32[]{:S(2)}, u32[]{:S(2)}) collective-permute-start(f32[2,8,8,128]{3,2,1,0:T(8,128)S(1)} %pad_maximum_fusion.6), channel_id=1, source_target_pairs={{0,1},{1,2},{2,3},{3,4},{4,5},{5,6},{6,7},{8,9},{9,10},{10,11},{11... | collective-permute-start | bytes 196616 | tf_op jit(solution)/shard_map/ppermute | solution.py:512
  28.9 5.9 %collective-permute-start.5 = (f32[2,7,8,256]{3,2,1,0:T(8,128)S(1)}, f32[2,7,8,256]{3,2,1,0:T(8,128)S(1)}, u32[]{:S(2)}, u32[]{:S(2)}) collective-permute-start(f32[2,7,8,256]{3,2,1,0:T(8,128)S(1)} %get-tuple-element.74), channel_id=1, source_target_pairs={{0,64},{64,128},{128,192},{1,65},{65,129},{129,193},{2,66},{66,130... | collective-permute-start | bytes 344072 | tf_op jit(solution)/shard_map/ppermute | solution.py:515
  32.1 7.0 %collective-permute-start.6 = (f32[2,7,8,256]{3,2,1,0:T(8,128)S(1)}, f32[2,7,8,256]{3,2,1,0:T(8,128)S(1)}, u32[]{:S(2)}, u32[]{:S(2)}) collective-permute-start(f32[2,7,8,256]{3,2,1,0:T(8,128)S(1)} %get-tuple-element.75), channel_id=1, source_target_pairs={{64,0},{128,64},{192,128},{65,1},{129,65},{193,129},{66,2},{130,66... | collective-permute-start | bytes 344072 | tf_op jit(solution)/shard_map/ppermute | solution.py:516
  39.2 9.4 %collective-permute-start.7 = (f32[2,22,8,256]{3,2,1,0:T(8,128)S(1)}, f32[2,22,8,256]{3,2,1,0:T(8,128)S(1)}, u32[]{:S(2)}, u32[]{:S(2)}) collective-permute-start(f32[2,22,8,256]{3,2,1,0:T(8,128)S(1)} %pad_maximum_fusion.1), channel_id=1, source_target_pairs={{0,8},{8,16},{16,24},{24,32},{32,40},{40,48},{48,56},{1,9},{9,17},... | collective-permute-start | bytes 1081352 | tf_op jit(solution)/shard_map/ppermute | solution.py:518
  44.3 8.7 %collective-permute-start.8 = (f32[2,22,8,256]{3,2,1,0:T(8,128)S(1)}, f32[2,22,8,256]{3,2,1,0:T(8,128)S(1)}, u32[]{:S(2)}, u32[]{:S(2)}) collective-permute-start(f32[2,22,8,256]{3,2,1,0:T(8,128)S(1)} %pad_maximum_fusion.1), channel_id=1, source_target_pairs={{8,0},{16,8},{24,16},{32,24},{40,32},{48,40},{56,48},{9,1},{17,9},... | collective-permute-start | bytes 1081352 | tf_op jit(solution)/shard_map/ppermute | solution.py:519
  81.1 107.1 %copy-start = (f32[20,32,128]{2,1,0:T(8,128)}, f32[20,32,128]{2,1,0:T(8,128)S(1)}, u32[]{:S(2)}) copy-start(f32[20,32,128]{2,1,0:T(8,128)S(1)} %get-tuple-element.47.d1) | copy-start | bytes 983044
  81.1 107.1 %copy-start.6 = (f32[10,16,128]{2,1,0:T(8,128)}, f32[10,16,128]{2,1,0:T(8,128)S(1)}, u32[]{:S(2)}) copy-start(f32[10,16,128]{2,1,0:T(8,128)S(1)} %get-tuple-element.49.ay2) | copy-start | bytes 245764
  81.1 107.1 %copy-start.8 = (f32[10,16,128]{2,1,0:T(8,128)}, f32[10,16,128]{2,1,0:T(8,128)S(1)}, u32[]{:S(2)}) copy-start(f32[10,16,128]{2,1,0:T(8,128)S(1)} %get-tuple-element.50.az2) | copy-start | bytes 245764
  81.1 107.1 %copy-start.10 = (f32[10,16,128]{2,1,0:T(8,128)}, f32[10,16,128]{2,1,0:T(8,128)S(1)}, u32[]{:S(2)}) copy-start(f32[10,16,128]{2,1,0:T(8,128)S(1)} %get-tuple-element.51.w2) | copy-start | bytes 245764
  81.1 107.1 %copy-start.12 = (f32[10,16,128]{2,1,0:T(8,128)}, f32[10,16,128]{2,1,0:T(8,128)S(1)}, u32[]{:S(2)}) copy-start(f32[10,16,128]{2,1,0:T(8,128)S(1)} %get-tuple-element.52.d2) | copy-start | bytes 245764
  89.7 5.3 %collective-permute-start.10 = (f32[1,8,8,128]{3,2,1,0:T(8,128)S(1)}, f32[1,8,8,128]{3,2,1,0:T(8,128)S(1)}, u32[]{:S(2)}, u32[]{:S(2)}) collective-permute-start(f32[1,8,8,128]{3,2,1,0:T(8,128)S(1)} %bitcast.41), channel_id=1, source_target_pairs={{0,1},{1,2},{2,3},{3,4},{4,5},{5,6},{6,7},{8,9},{9,10},{10,11},{11... | collective-permute-start | bytes 98312 | tf_op jit(solution)/shard_map/ppermute | solution.py:512
  93.7 5.5 %collective-permute-start.9 = (f32[1,8,8,128]{3,2,1,0:T(8,128)S(1)}, f32[1,8,8,128]{3,2,1,0:T(8,128)S(1)}, u32[]{:S(2)}, u32[]{:S(2)}) collective-permute-start(f32[1,8,8,128]{3,2,1,0:T(8,128)S(1)} %bitcast.42), channel_id=1, source_target_pairs={{1,0},{2,1},{3,2},{4,3},{5,4},{6,5},{7,6},{9,8},{10,9},{11,10},{12... | collective-permute-start | bytes 98312 | tf_op jit(solution)/shard_map/ppermute | solution.py:511
  99.3 4.1 %collective-permute-start.11 = (f32[1,7,8,256]{3,2,1,0:T(8,128)S(1)}, f32[1,7,8,256]{3,2,1,0:T(8,128)S(1)}, u32[]{:S(2)}, u32[]{:S(2)}) collective-permute-start(f32[1,7,8,256]{3,2,1,0:T(8,128)S(1)} %get-tuple-element.80), channel_id=1, source_target_pairs={{0,64},{64,128},{128,192},{1,65},{65,129},{129,193},{2,66},{66,130... | collective-permute-start | bytes 172040 | tf_op jit(solution)/shard_map/ppermute | solution.py:515
  102.1 4.9 %collective-permute-start.12 = (f32[1,7,8,256]{3,2,1,0:T(8,128)S(1)}, f32[1,7,8,256]{3,2,1,0:T(8,128)S(1)}, u32[]{:S(2)}, u32[]{:S(2)}) collective-permute-start(f32[1,7,8,256]{3,2,1,0:T(8,128)S(1)} %get-tuple-element.81), channel_id=1, source_target_pairs={{64,0},{128,64},{192,128},{65,1},{129,65},{193,129},{66,2},{130,66... | collective-permute-start | bytes 172040 | tf_op jit(solution)/shard_map/ppermute | solution.py:516
  107.0 6.0 %collective-permute-start.13 = (f32[1,22,8,256]{3,2,1,0:T(8,128)S(1)}, f32[1,22,8,256]{3,2,1,0:T(8,128)S(1)}, u32[]{:S(2)}, u32[]{:S(2)}) collective-permute-start(f32[1,22,8,256]{3,2,1,0:T(8,128)S(1)} %pad_maximum_fusion.2), channel_id=1, source_target_pairs={{0,8},{8,16},{16,24},{24,32},{32,40},{40,48},{48,56},{1,9},{9,17},... | collective-permute-start | bytes 540680 | tf_op jit(solution)/shard_map/ppermute | solution.py:518
  110.6 6.8 %collective-permute-start.14 = (f32[1,22,8,256]{3,2,1,0:T(8,128)S(1)}, f32[1,22,8,256]{3,2,1,0:T(8,128)S(1)}, u32[]{:S(2)}, u32[]{:S(2)}) collective-permute-start(f32[1,22,8,256]{3,2,1,0:T(8,128)S(1)} %pad_maximum_fusion.2), channel_id=1, source_target_pairs={{8,0},{16,8},{24,16},{32,24},{40,32},{48,40},{56,48},{9,1},{17,9},... | collective-permute-start | bytes 540680 | tf_op jit(solution)/shard_map/ppermute | solution.py:519
  117.4 3.1 %copy-start.3 = (f32[22,24,256]{2,1,0:T(8,128)}, f32[22,24,256]{2,1,0:T(8,128)S(1)}, u32[]{:S(2)}) copy-start(f32[22,24,256]{2,1,0:T(8,128)S(1)} %maximum_bitcast_fusion.p) | copy-start | bytes 1622020
  135.2 9.3 %copy-start.24 = (f32[3,8,8,128]{3,2,1,0:T(8,128)S(1)}, f32[3,8,8,128]{3,2,1,0:T(8,128)}, u32[]{:S(2)}) copy-start(f32[3,8,8,128]{3,2,1,0:T(8,128)} %target.3) | copy-start | bytes 294916
  145.8 21.7 %copy-start.26 = (f32[3,8,8,128]{3,2,1,0:T(8,128)}, f32[3,8,8,128]{3,2,1,0:T(8,128)S(1)}, u32[]{:S(2)}) copy-start(f32[3,8,8,128]{3,2,1,0:T(8,128)S(1)} %get-tuple-element.69.misfit) | copy-start | bytes 294916
  145.8 6.8 %collective-permute-start.15 = (f32[1,8,8,128]{3,2,1,0:T(8,128)S(1)}, f32[1,8,8,128]{3,2,1,0:T(8,128)S(1)}, u32[]{:S(2)}, u32[]{:S(2)}) collective-permute-start(f32[1,8,8,128]{3,2,1,0:T(8,128)S(1)} %bitcast.46), channel_id=1, source_target_pairs={{1,0},{2,1},{3,2},{4,3},{5,4},{6,5},{7,6},{9,8},{10,9},{11,10},{12... | collective-permute-start | bytes 98312 | tf_op jit(solution)/shard_map/ppermute | solution.py:511
  147.1 6.5 %collective-permute-start.16 = (f32[1,8,8,128]{3,2,1,0:T(8,128)S(1)}, f32[1,8,8,128]{3,2,1,0:T(8,128)S(1)}, u32[]{:S(2)}, u32[]{:S(2)}) collective-permute-start(f32[1,8,8,128]{3,2,1,0:T(8,128)S(1)} %bitcast.47), channel_id=1, source_target_pairs={{0,1},{1,2},{2,3},{3,4},{4,5},{5,6},{6,7},{8,9},{9,10},{10,11},{11... | collective-permute-start | bytes 98312 | tf_op jit(solution)/shard_map/ppermute | solution.py:512
  153.6 3.6 %collective-permute-start.17 = (f32[1,7,8,256]{3,2,1,0:T(8,128)S(1)}, f32[1,7,8,256]{3,2,1,0:T(8,128)S(1)}, u32[]{:S(2)}, u32[]{:S(2)}) collective-permute-start(f32[1,7,8,256]{3,2,1,0:T(8,128)S(1)} %get-tuple-element.78), channel_id=1, source_target_pairs={{0,64},{64,128},{128,192},{1,65},{65,129},{129,193},{2,66},{66,130... | collective-permute-start | bytes 172040 | tf_op jit(solution)/shard_map/ppermute | solution.py:515
  155.8 4.9 %collective-permute-start.18 = (f32[1,7,8,256]{3,2,1,0:T(8,128)S(1)}, f32[1,7,8,256]{3,2,1,0:T(8,128)S(1)}, u32[]{:S(2)}, u32[]{:S(2)}) collective-permute-start(f32[1,7,8,256]{3,2,1,0:T(8,128)S(1)} %get-tuple-element.79), channel_id=1, source_target_pairs={{64,0},{128,64},{192,128},{65,1},{129,65},{193,129},{66,2},{130,66... | collective-permute-start | bytes 172040 | tf_op jit(solution)/shard_map/ppermute | solution.py:516
  160.7 6.7 %collective-permute-start.19 = (f32[1,22,8,256]{3,2,1,0:T(8,128)S(1)}, f32[1,22,8,256]{3,2,1,0:T(8,128)S(1)}, u32[]{:S(2)}, u32[]{:S(2)}) collective-permute-start(f32[1,22,8,256]{3,2,1,0:T(8,128)S(1)} %pad_maximum_fusion.3), channel_id=1, source_target_pairs={{0,8},{8,16},{16,24},{24,32},{32,40},{40,48},{48,56},{1,9},{9,17},... | collective-permute-start | bytes 540680 | tf_op jit(solution)/shard_map/ppermute | solution.py:518
  165.1 6.8 %collective-permute-start.20 = (f32[1,22,8,256]{3,2,1,0:T(8,128)S(1)}, f32[1,22,8,256]{3,2,1,0:T(8,128)S(1)}, u32[]{:S(2)}, u32[]{:S(2)}) collective-permute-start(f32[1,22,8,256]{3,2,1,0:T(8,128)S(1)} %pad_maximum_fusion.3), channel_id=1, source_target_pairs={{8,0},{16,8},{24,16},{32,24},{40,32},{48,40},{56,48},{9,1},{17,9},... | collective-permute-start | bytes 540680 | tf_op jit(solution)/shard_map/ppermute | solution.py:519
  196.8 7.1 %collective-permute-start.21 = (f32[1,8,8,128]{3,2,1,0:T(8,128)S(1)}, f32[1,8,8,128]{3,2,1,0:T(8,128)S(1)}, u32[]{:S(2)}, u32[]{:S(2)}) collective-permute-start(f32[1,8,8,128]{3,2,1,0:T(8,128)S(1)} %bitcast.36), channel_id=1, source_target_pairs={{1,0},{2,1},{3,2},{4,3},{5,4},{6,5},{7,6},{9,8},{10,9},{11,10},{12... | collective-permute-start | bytes 98312 | tf_op jit(solution)/shard_map/ppermute | solution.py:511
  198.1 6.8 %collective-permute-start.22 = (f32[1,8,8,128]{3,2,1,0:T(8,128)S(1)}, f32[1,8,8,128]{3,2,1,0:T(8,128)S(1)}, u32[]{:S(2)}, u32[]{:S(2)}) collective-permute-start(f32[1,8,8,128]{3,2,1,0:T(8,128)S(1)} %bitcast.37), channel_id=1, source_target_pairs={{0,1},{1,2},{2,3},{3,4},{4,5},{5,6},{6,7},{8,9},{9,10},{10,11},{11... | collective-permute-start | bytes 98312 | tf_op jit(solution)/shard_map/ppermute | solution.py:512
  205.0 3.6 %collective-permute-start.23 = (f32[1,7,8,256]{3,2,1,0:T(8,128)S(1)}, f32[1,7,8,256]{3,2,1,0:T(8,128)S(1)}, u32[]{:S(2)}, u32[]{:S(2)}) collective-permute-start(f32[1,7,8,256]{3,2,1,0:T(8,128)S(1)} %get-tuple-element.76), channel_id=1, source_target_pairs={{0,64},{64,128},{128,192},{1,65},{65,129},{129,193},{2,66},{66,130... | collective-permute-start | bytes 172040 | tf_op jit(solution)/shard_map/ppermute | solution.py:515
  207.2 4.9 %collective-permute-start.24 = (f32[1,7,8,256]{3,2,1,0:T(8,128)S(1)}, f32[1,7,8,256]{3,2,1,0:T(8,128)S(1)}, u32[]{:S(2)}, u32[]{:S(2)}) collective-permute-start(f32[1,7,8,256]{3,2,1,0:T(8,128)S(1)} %get-tuple-element.77), channel_id=1, source_target_pairs={{64,0},{128,64},{192,128},{65,1},{129,65},{193,129},{66,2},{130,66... | collective-permute-start | bytes 172040 | tf_op jit(solution)/shard_map/ppermute | solution.py:516
  212.2 6.7 %collective-permute-start.25 = (f32[1,22,8,256]{3,2,1,0:T(8,128)S(1)}, f32[1,22,8,256]{3,2,1,0:T(8,128)S(1)}, u32[]{:S(2)}, u32[]{:S(2)}) collective-permute-start(f32[1,22,8,256]{3,2,1,0:T(8,128)S(1)} %pad_maximum_fusion.4), channel_id=1, source_target_pairs={{0,8},{8,16},{16,24},{24,32},{32,40},{40,48},{48,56},{1,9},{9,17},... | collective-permute-start | bytes 540680 | tf_op jit(solution)/shard_map/ppermute | solution.py:518
  216.5 6.8 %collective-permute-start.26 = (f32[1,22,8,256]{3,2,1,0:T(8,128)S(1)}, f32[1,22,8,256]{3,2,1,0:T(8,128)S(1)}, u32[]{:S(2)}, u32[]{:S(2)}) collective-permute-start(f32[1,22,8,256]{3,2,1,0:T(8,128)S(1)} %pad_maximum_fusion.4), channel_id=1, source_target_pairs={{8,0},{16,8},{24,16},{32,24},{40,32},{48,40},{56,48},{9,1},{17,9},... | collective-permute-start | bytes 540680 | tf_op jit(solution)/shard_map/ppermute | solution.py:519
  223.3 3.1 %copy-start.2 = (f32[22,24,256]{2,1,0:T(8,128)}, f32[22,24,256]{2,1,0:T(8,128)S(1)}, u32[]{:S(2)}) copy-start(f32[22,24,256]{2,1,0:T(8,128)S(1)} %maximum_bitcast_fusion.2.p) | copy-start | bytes 1622020
  226.5 0.8 copy-start.18
  227.3 0.8 copy-start.20
  228.8 14.4 %all-to-all-start.3 = ((f32[32,16,128]{2,1,0:T(8,128)}), f32[32,16,128]{2,1,0:T(8,128)}, u32[]{:S(2)}, u32[]{:S(2)}) async-start(f32[32,16,128]{2,1,0:T(8,128)} %broadcast_in_dim.58), calls=%async_computation.3 | async-start | bytes 524288 | tf_op jit(solution)/shard_map/all_to_all | solution.py:525
  243.2 1.0 copy-start.1
  244.2 0.9 copy-start.7
  245.1 0.9 copy-start.9
  246.0 0.9 copy-start.11
  246.9 0.9 copy-start.13
  247.7 1.0 copy-start.19
  248.8 1.0 copy-start.21
  249.8 0.7 copy-start.29
  250.5 9.5 %copy-start.5 = (f32[8,512,128]{2,1,0:T(8,128)S(1)}, f32[8,512,128]{2,1,0:T(8,128)}, u32[]{:S(2)}) copy-start(f32[8,512,128]{2,1,0:T(8,128)} %copy-done.4) | copy-start | bytes 6291460
  250.5 9.5 %copy-start.15 = (bf16[16,8,8,128]{3,2,1,0:T(8,128)(2,1)S(1)}, bf16[16,8,8,128]{3,2,1,0:T(8,128)(2,1)}, u32[]{:S(2)}) copy-start(bf16[16,8,8,128]{3,2,1,0:T(8,128)(2,1)} %features.3) | copy-start | bytes 786436
  250.5 9.5 %copy-start.17 = (bf16[8,512,128]{2,1,0:T(8,128)(2,1)S(1)}, bf16[8,512,128]{2,1,0:T(8,128)(2,1)}, u32[]{:S(2)}) copy-start(bf16[8,512,128]{2,1,0:T(8,128)(2,1)} %copy-done.16) | copy-start | bytes 3145732
  250.5 9.5 %copy-start.22 = (bf16[512,24]{1,0:T(8,128)(2,1)S(1)}, bf16[512,24]{1,0:T(8,128)(2,1)}, u32[]{:S(2)}) copy-start(bf16[512,24]{1,0:T(8,128)(2,1)} %copy.21.kback) | copy-start | bytes 73732
  250.5 9.5 %copy-start.27 = (f32[3,8,8,128]{3,2,1,0:T(8,128)S(1)}, f32[3,8,8,128]{3,2,1,0:T(8,128)}, u32[]{:S(2)}) copy-start(f32[3,8,8,128]{3,2,1,0:T(8,128)} %copy-done.26) | copy-start | bytes 294916
where the time goes:
time: 299 us; the launch traced here: 297 us
  starting transfers between devices  82.4 us (28%)
  blocking collectives  75.1 us (25%)
  Pallas kernels  65.8 us (22%)
  waiting for transfers between devices  50.1 us (17%)
  local copies, waits for them, and re-layouts  19.2 us (6%)
    pallas_call x13, Pallas kernels, call(): pl.pallas_call(body, out_shape=outs, in_specs=specs, out_specs=[pl.BlockS...  65.8 us
    all_to_all x3, blocking collectives, over_plane(): return lax.all_to_all(copies, XY, split_axis=0, concat_axis=0, tiled=True)  44.9 us
    all_to_all x2, blocking collectives, summed(): lax.all_to_all(copies, axis, split_axis=0, concat_axis=0, tiled=True)  30.2 us
    ppermute x4, starting transfers between devices, exchanged(): before = lax.ppermute(own, 'gz', ups('gz'))  19.5 us
    ppermute x4, waiting for transfers between devices, exchanged(): high = lax.ppermute(wide, GY, downs(GY))  17.6 us
    ppermute x4, starting transfers between devices, exchanged(): low = lax.ppermute(wide, GY, ups(GY))  17.2 us
    ppermute x4, waiting for transfers between devices, exchanged(): high = lax.ppermute(wide[:, 0:7], 'gx', downs('gx'))  15.2 us
    ppermute x4, starting transfers between devices, exchanged(): low = lax.ppermute(wide[:, 1:8], 'gx', ups('gx'))  10.5 us
  transfers between devices with their start and end apart: 28, of which 19 were waited for; matrix products, arithmetic and copies ran while one was open for 2% of the time, Pallas kernels for 0%

commit v1 on v0

--- a/solution.py
+++ b/solution.py
@@ -19,6 +19,7 @@
 REGION = (NXP, NYP, NZP)
 L1 = (20, 32, 128)
 L2 = (10, 16, 128)
+UNROLL = {24: 2, 32: 8, 16: 8}
 
 
 def shaped(shape, dtype=F32):
@@ -35,7 +36,7 @@
         in_specs=specs,
         out_specs=[pl.BlockSpec(memory_space=pltpu.VMEM)] * len(outs),
         scratch_shapes=list(scratch),
-        compiler_params=pltpu.CompilerParams(vmem_limit_bytes=48 << 20),
+        compiler_params=pltpu.CompilerParams(vmem_limit_bytes=20 << 20),
     )(*args)
 
 
@@ -49,6 +50,18 @@
 
 def exact_dot(a, b):
     return jnp.dot(a, b, precision=HIGHEST, preferred_element_type=F32)
+
+
+def chosen_dot(a, b):
+    high = a.astype(BF16)
+    rest = a - high.astype(F32)
+    middle = rest.astype(BF16)
+    low = (rest - middle.astype(F32)).astype(BF16)
+    count = a.shape[0]
+    parts = jnp.dot(
+        jnp.concatenate([high, middle, low], axis=0), b.astype(BF16), preferred_element_type=F32
+    )
+    return (parts[2 * count :] + parts[count : 2 * count]) + parts[:count]
 
 
 def planes(lo, hi, body, unroll=2):
@@ -72,14 +85,14 @@
         v, total = around(src, ax, ay, az, i)
         dst[i] = 0.2 * v + w[i] * (s[i] + total)
 
-    planes(lo, hi, one)
+    planes(lo, hi, one, UNROLL[src.shape[1]])
 
 
 def first_sweep(dst, s, w, lo, hi):
     def one(i):
         dst[i] = w[i] * s[i]
 
-    planes(lo, hi, one)
+    planes(lo, hi, one, UNROLL[s.shape[1]])
 
 
 def face(here, there, weight, low, high):
@@ -99,7 +112,7 @@
     def one_face(i):
         ax[i] = face(rho[i], rho[i + 1], weight, low[0], high[0])
 
-    planes(lo - 1, hi, one_face, 1)
+    planes(lo - 1, hi, one_face, 2)
 
     def one(i):
         r = rho[i]
@@ -118,7 +131,7 @@
         d[i] = diagonal
         w[i] = jnp.where(r > 0.0, 0.8 / diagonal, F32(0.0))
 
-    planes(lo, hi, one, 1)
+    planes(lo, hi, one, 2)
 
 
 def lane_pairs(cells, kept, repeat):
@@ -135,7 +148,7 @@
 
 def block_means(read, rows, out, out_row):
     pairs = [read(7 + 2 * k) + read(8 + 2 * k) for k in range(4)]
-    rows[...] = exact_dot(jnp.concatenate(pairs, axis=0), lane_pairs(256, 128, 128))
+    rows[...] = chosen_dot(jnp.concatenate(pairs, axis=0), lane_pairs(256, 128, 128))
     total = rows[pl.ds(0, 16, stride=2), :] + rows[pl.ds(1, 16, stride=2), :]
     out[out_row : out_row + 16, :] = 0.125 * total
 
@@ -202,7 +215,7 @@
 def restrict_whole(read, rows, dst):
     for k in range(8):
         rows[32 * k : 32 * k + 32, :] = read(2 + 2 * k) + read(3 + 2 * k)
-    rows[...] = exact_dot(rows[...], lane_pairs(128, 128, 64))
+    rows[...] = chosen_dot(rows[...], lane_pairs(128, 128, 64))
     for k in range(8):
         total = (
             rows[pl.ds(32 * k, 16, stride=2), :] + rows[pl.ds(32 * k + 1, 16, stride=2), :]
@@ -249,7 +262,7 @@
     for k in range(5):
         a, b = (v2, u2) if k % 2 == 0 else (u2, v2)
         sweep(a, b, s2, w2, ax2, ay2, az2, 1, 9)
-    spread = exact_dot(
+    spread = chosen_dot(
         jnp.concatenate([u2[1 + k] for k in range(8)], axis=0), lane_spread(128, 128)
     )
     rows[pl.ds(0, 128, stride=2), :] = spread
@@ -263,7 +276,7 @@
     sweep(v1, u1, s1, w1, ax1, ay1, az1, 2, 18)
     base = sc[0] * 4
     near = jnp.concatenate([u1[base + k] for k in range(8)], axis=0)
-    wide = exact_dot(near, lane_spread(128, 256))
+    wide = chosen_dot(near, lane_spread(128, 256))
     for lanes, ref in ((slice(0, 128), wide_a), (slice(128, 256), wide_b)):
         for k in range(8):
             ref[80 * k : 80 * k + 8, :] = jnp.zeros((8, 128), F32)
@@ -334,9 +347,51 @@
         out[i] = p[i + 6] + 0.2 * centre + w[i + 6] * (s[i + 6] + total)
 
 
+def members(count, groups):
+    r = lax.broadcasted_iota(jnp.int32, (count, groups), 0)
+    c = lax.broadcasted_iota(jnp.int32, (count, groups), 1)
+    return jnp.where(r // 8 == c, F32(1.0), F32(0.0)).astype(BF16)
+
+
+def same_row(x):
+    r = lax.broadcasted_iota(jnp.int32, x.shape, 0)
+    c = lax.broadcasted_iota(jnp.int32, x.shape, 1)
+    return jnp.where(r % 8 == c % 8, x, F32(0.0)).astype(BF16)
+
+
+ACROSS = (((1,), (1,)), ((), ()))
+
+
+def dot_across(a, b, precision=None):
+    return lax.dot_general(a, b, ACROSS, precision=precision, preferred_element_type=F32)
+
+
 def closure_body(
-    sc, features, kin, bias, kout, velocity, target, flux, slope, hidden, face_x, face_y, face_z
+    sc,
+    features,
+    weight_in,
+    bias_in,
+    weight_out,
+    velocity,
+    target,
+    flux,
+    slope,
+    hidden,
+    face_x,
+    face_y,
+    face_z,
+    kin,
+    bias,
+    kout,
 ):
+    units = members(512, 64)
+    narrow = dot_across(units, weight_in[...]).astype(BF16)
+    kin[...] = same_row(dot_across(narrow, members(128, 16)))
+    narrow = dot_across(members(24, 3), weight_out[...]).astype(BF16)
+    kout[...] = same_row(dot_across(narrow, units))
+    bias[...] = dot_across(
+        units.astype(F32), jnp.broadcast_to(bias_in[...], (128, 64)), HIGHEST
+    )
     _, high = opens_of(sc)
     high_x = jnp.where(sc[0] == 3, high[0], F32(1.0))
     high_y = jnp.where(sc[1] == 7, high[1], F32(1.0))
@@ -378,13 +433,14 @@
     return before_x, before_y, before_z
 
 
-def source_body(flux, low_x, low_y, low_z, out):
+def source_body(sc, flux, low_x, low_y, low_z, out):
+    inner = [jnp.where(sc[d] > 0, F32(1.0), F32(0.0)) for d in range(3)]
     for x in range(8):
         bx, by, bz = shifted(
             lambda d, i: flux[d, i],
-            lambda: low_x[0],
-            lambda i: jnp.broadcast_to(low_y[0, i : i + 1, :], (8, 128)),
-            lambda i: forth(low_z[0, i], 1),
+            lambda: low_x[0] * inner[0],
+            lambda i: jnp.broadcast_to(low_y[0, i : i + 1, :] * inner[1], (8, 128)),
+            lambda i: forth(low_z[0, i] * inner[2], 1),
             x,
         )
         out[x] = -((flux[0, x] - bx) + (flux[1, x] - by) + (flux[2, x] - bz))
@@ -435,7 +491,11 @@
         out[x] = (weighted(0, x) - bx) + (weighted(1, x) - by) + (weighted(2, x) - bz)
 
 
-def gradient_body(sc, near, misfit, features, slope, hidden, kback, out, acc_in, acc_bias, acc_out):
+def gradient_body(
+    sc, near, misfit, features, slope, hidden, weight_out, out, acc_in, acc_bias, acc_out, kback
+):
+    narrow = jnp.dot(members(512, 64), weight_out[...], preferred_element_type=F32).astype(BF16)
+    kback[...] = same_row(dot_across(narrow, members(24, 3)))
     _, high = opens_of(sc)
     high_x = jnp.where(sc[0] == 3, high[0], F32(1.0))
     high_y = jnp.where(sc[1] == 7, high[1], F32(1.0))
@@ -447,7 +507,7 @@
     acc_in[...] = jnp.zeros((128, 512), F32)
     acc_bias[...] = jnp.zeros((512, 128), F32)
     acc_out[...] = jnp.zeros((24, 512), F32)
-    across = (((1,), (1,)), ((), ()))
+    across = ACROSS
 
     def one(x):
         p = near[x + 1]
@@ -498,25 +558,28 @@
     out[8:16, 64:128] = folded[24:32]
 
 
-def ups(axis):
+def neighbours(up, down, axis):
     count = lax.axis_size(axis)
-    return [(i, i + 1) for i in range(count - 1)]
-
-
-def downs(axis):
-    return [(b, a) for a, b in ups(axis)]
+    ups = [(i, (i + 1) % count) for i in range(count)]
+    before = lax.ppermute(up, axis, ups)
+    after = lax.ppermute(down, axis, [(b, a) for a, b in ups])
+    place = lax.axis_index(axis)
+    zero = F32(0.0)
+    return jnp.where(place > 0, before, zero), jnp.where(place < count - 1, after, zero)
+
+
+def from_before(face, axis):
+    count = lax.axis_size(axis)
+    return lax.ppermute(face, axis, [(i, (i + 1) % count) for i in range(count)])
 
 
 def exchanged(own):
-    after = lax.ppermute(own, "gz", downs("gz"))
-    before = lax.ppermute(own, "gz", ups("gz"))
+    before, after = neighbours(own, own, "gz")
     lane = lax.broadcasted_iota(jnp.int32, own.shape, 3)
     wide = jnp.concatenate([own, jnp.where(lane < 64, after, before)], axis=3)
-    low = lax.ppermute(wide[:, 1:8], "gx", ups("gx"))
-    high = lax.ppermute(wide[:, 0:7], "gx", downs("gx"))
+    low, high = neighbours(wide[:, 1:8], wide[:, 0:7], "gx")
     wide = jnp.concatenate([low, wide, high], axis=1)
-    low = lax.ppermute(wide, GY, ups(GY))
-    high = lax.ppermute(wide, GY, downs(GY))
+    low, high = neighbours(wide, wide, GY)
     return jnp.concatenate([low, wide, high], axis=2)
 
 
@@ -535,11 +598,6 @@
 def per_device(velocity, features, density, target, weight_in, bias_in, weight_out, open_faces):
     place = jnp.stack([lax.axis_index("gx"), lax.axis_index(GY), lax.axis_index("gz")])
     sc = jnp.concatenate([place.astype(jnp.int32), open_faces])
-    eye = jnp.eye(8, dtype=BF16)
-    kin = jnp.kron(weight_in.T, eye)
-    kout = jnp.kron(weight_out.T, eye)
-    kback = jnp.kron(weight_out, eye)
-    bias = jnp.broadcast_to(bias_in[:, None, None], (64, 8, 128)).reshape(512, 128)
     block = (8, 8, 128)
     flux, slope, hidden, face_x, face_y, face_z = call(
         closure_body,
@@ -551,13 +609,16 @@
             shaped((2, 8, 128)),
             shaped((2, *block)),
         ],
-        (sc, features, kin, bias, kout, velocity, target),
+        (sc, features, weight_in, bias_in[None], weight_out, velocity, target),
+        [pltpu.VMEM((512, 128), BF16), pltpu.VMEM((512, 128), F32), pltpu.VMEM((24, 512), BF16)],
         smem=(0,),
     )
-    low_x = lax.ppermute(face_x, "gx", ups("gx"))
-    low_y = lax.ppermute(face_y, GY, ups(GY))
-    low_z = lax.ppermute(face_z, "gz", ups("gz"))
-    (source,) = call(source_body, [shaped(block)], (flux, low_x, low_y, low_z))
+    low_x = from_before(face_x, "gx")
+    low_y = from_before(face_y, GY)
+    low_z = from_before(face_z, "gz")
+    (source,) = call(
+        source_body, [shaped(block)], (sc, flux, low_x, low_y, low_z), smem=(0,)
+    )
     both = exchanged(jnp.stack([source, density]))
     region = shaped(REGION)
     one_region = [pltpu.VMEM(REGION, F32), pltpu.VMEM((32, 128), F32)]
@@ -612,11 +673,16 @@
     (packed,) = call(
         gradient_body,
         [shaped((16, 128))],
-        (sc, near, misfit, features, slope, hidden, kback),
-        [pltpu.VMEM((128, 512), F32), pltpu.VMEM((512, 128), F32), pltpu.VMEM((24, 512), F32)],
+        (sc, near, misfit, features, slope, hidden, weight_out),
+        [
+            pltpu.VMEM((128, 512), F32),
+            pltpu.VMEM((512, 128), F32),
+            pltpu.VMEM((24, 512), F32),
+            pltpu.VMEM((512, 24), BF16),
+        ],
         smem=(0,),
     )
-    total = summed(packed, (("gy_1", "gz"), ("gx", "gy_0")))
+    total = summed(packed, (XY, "gz"))
     grad_in = jnp.concatenate([total[0:8, 0:64], total[0:8, 64:128]], axis=0)
     return new_velocity, grad_in, total[8, 64:128], total[8:11, 0:64].T
 

time: 299 us -> 225 us (0.75)
  starting transfers between devices: 82.4 us -> 41.2 us
  Pallas kernels: 65.8 us -> 47.5 us
  waiting for transfers between devices: 50.1 us -> 32.5 us
  blocking collectives: 75.1 us -> 89.3 us
  local copies, waits for them, and re-layouts: 19.2 us -> 7.64 us
    ppermute x27, starting transfers between devices: 77 us -> 41.2 us  [the longest x12 25 us: neighbours(): after = lax.ppermute(down, axis, [(b, a) for a, b in ups])]
    all_to_all x3 -> x4, blocking collectives: 44.9 us -> 66.3 us  [over_plane(): return lax.all_to_all(copies, XY, split_axis=0, concat_axis=0, tiled=True)]
    pallas_call x13, Pallas kernels: 65.8 us -> 47.5 us  [call(): pl.pallas_call(body, out_shape=outs, in_specs=specs, out_specs=[pl.BlockS...]
    ppermute x27, waiting for transfers between devices: 46.3 us -> 32.5 us  [the longest x12 17.9 us: neighbours(): after = lax.ppermute(down, axis, [(b, a) for a, b in ups])]
    all_to_all x2, blocking collectives: 30.2 us -> 23.1 us  [summed(): lax.all_to_all(copies, axis, split_axis=0, concat_axis=0, tiled=True)]
    mul x4 -> x0, local copies, waits for them, and re-layouts: 6.36 us -> none  [the longest x2 3.57 us: per_device(): kback = jnp.kron(weight_out, eye)]
    all_to_all x1 -> x0, starting transfers between devices: 5.44 us -> none  [over_plane(): return lax.all_to_all(copies, XY, split_axis=0, concat_axis=0, tiled=True)]
    unnamed x70 -> x25, local copies, waits for them, and re-layouts: 9.5 us -> 5.48 us
  transfers between devices with their start and end apart: 28 -> 27, of which waited for: 19 -> 18; matrix products, arithmetic and copies ran while one was open for 2% -> 0% of each run, Pallas kernels for 0% -> 0%
where the time goes in v1:
time: 225 us
  blocking collectives  89.3 us (40%)
  Pallas kernels  47.5 us (21%)
  starting transfers between devices  41.2 us (18%)
  waiting for transfers between devices  32.5 us (14%)
  local copies, waits for them, and re-layouts  7.64 us (3%)
  other arithmetic  5.44 us (2%)
    all_to_all x4, blocking collectives, over_plane(): return lax.all_to_all(copies, XY, split_axis=0, concat_axis=0, tiled=True)  66.3 us
    pallas_call x13, Pallas kernels, call(): pl.pallas_call(body, out_shape=outs, in_specs=specs, out_specs=[pl.BlockS...  47.5 us
    ppermute x12, starting transfers between devices, neighbours(): after = lax.ppermute(down, axis, [(b, a) for a, b in ups])  25 us
    all_to_all x2, blocking collectives, summed(): lax.all_to_all(copies, axis, split_axis=0, concat_axis=0, tiled=True)  23.1 us
    ppermute x12, waiting for transfers between devices, neighbours(): after = lax.ppermute(down, axis, [(b, a) for a, b in ups])  17.9 us
    ppermute x12, waiting for transfers between devices, neighbours(): before = lax.ppermute(up, axis, ups)  12.6 us
    ppermute x12, starting transfers between devices, neighbours(): before = lax.ppermute(up, axis, ups)  10 us
    ppermute x3, starting transfers between devices, from_before(): lax.ppermute(face, axis, [(i, (i + 1) % count) for i in range(count)])  6.16 us
  transfers between devices with their start and end apart: 27, of which 18 were waited for; matrix products, arithmetic and copies ran while one was open for 0% of the time, Pallas kernels for 0%

profile of v1, /device:TPU:1, one launch (start us, length us, event | category | flops | bytes accessed | tf_op | source)
XLA Modules:
  0.0 224.6 jit_solution(7741114366667065920)
XLA Ops:
  0.7 0.8 copy.14.weight_out
  1.4 0.7 pad_add_fusion.sc
  2.2 0.9 copy-done
  3.1 0.9 copy-done.2
  4.0 0.9 copy-done.4
  4.9 0.7 copy-done.5
  6.3 4.4 %shard_map.111 = (f32[3,8,8,128]{3,2,1,0:T(8,128)S(1)}, f32[8,512,128]{2,1,0:T(8,128)S(1)}, bf16[8,512,128]{2,1,0:T(8,128)(2,1)S(1)}, f32[2,8,128]{2,1,0:T(8,128...) custom-call(s32[9]{0:T(128)S(1)} %pad_add_fusion.sc, bf16[16,8,8,128]{3,2,1,0:T(8,128)(2,1)S(1)} %copy-done, ...), custom_call_target="tpu_custom_call" | custom-call | tf_op jit(solution)/shard_map/pallas_call | solution.py:33
  10.6 2.5 %collective-permute-start.2 = (f32[2,8,8,128]{3,2,1,0:T(8,128)S(1)}, f32[2,8,8,128]{3,2,1,0:T(8,128)S(1)}, u32[]{:S(2)}, u32[]{:S(2)}) collective-permute-start(f32[2,8,8,128]{3,2,1,0:T(8,128)S(1)} %get-tuple-element.41), channel_id=1, source_target_pairs={{0,1},{1,2},{2,3},{3,4},{4,5},{5,6},{6,7},{7,0},{8,9},{9,10},{10,1... | collective-permute-start | bytes 196616 | tf_op jit(solution)/shard_map/ppermute | solution.py:573
  13.2 1.3 collective-permute-start
  14.5 2.3 %collective-permute-start.1 = (f32[2,8,128]{2,1,0:T(8,128)S(1)}, f32[2,8,128]{2,1,0:T(8,128)S(1)}, u32[]{:S(2)}, u32[]{:S(2)}) collective-permute-start(f32[2,8,128]{2,1,0:T(8,128)S(1)} %get-tuple-element.40), channel_id=1, source_target_pairs={{0,8},{8,16},{16,24},{24,32},{32,40},{40,48},{48,56},{56,0},{1,9},... | collective-permute-start | bytes 24584 | tf_op jit(solution)/shard_map/ppermute | solution.py:573
  17.6 1.2 collective-permute-done.2.low_z
  19.4 0.8 pad_maximum_fusion.6
  20.6 2.2 collective-permute-start.3
  22.8 1.6 collective-permute-done.4
  24.5 0.7 fusion.3
  25.2 1.3 collective-permute-start.5
  26.5 1.4 collective-permute-start.6
  28.0 2.5 %collective-permute-done.5 = f32[2,7,8,256]{3,2,1,0:T(8,128)} collective-permute-done((f32[2,7,8,256]{3,2,1,0:T(8,128)}, f32[2,7,8,256]{3,2,1,0:T(8,128)}, u32[]{:S(2)}, u32[]{:S(2)}) %collective-permute-start.5) | collective-permute-done | bytes 114720 | tf_op jit(solution)/shard_map/ppermute | solution.py:564
  31.1 0.8 pad_maximum_fusion.1
  31.9 4.3 %collective-permute-start.8 = (f32[2,22,8,256]{3,2,1,0:T(8,128)}, f32[2,22,8,256]{3,2,1,0:T(8,128)}, u32[]{:S(2)}, u32[]{:S(2)}) collective-permute-start(f32[2,22,8,256]{3,2,1,0:T(8,128)} %pad_maximum_fusion.1), channel_id=1, source_target_pairs={{8,0},{16,8},{24,16},{32,24},{40,32},{48,40},{56,48},{0,56},{9,1},... | collective-permute-start | bytes 1081352 | tf_op jit(solution)/shard_map/ppermute | solution.py:565
  36.8 5.7 %collective-permute-done.8 = f32[2,22,8,256]{3,2,1,0:T(8,128)} collective-permute-done((f32[2,22,8,256]{3,2,1,0:T(8,128)}, f32[2,22,8,256]{3,2,1,0:T(8,128)}, u32[]{:S(2)}, u32[]{:S(2)}) %collective-permute-start.8) | collective-permute-done | bytes 360480 | tf_op jit(solution)/shard_map/ppermute | solution.py:565
  42.5 1.0 broadcast_select_fusion
  43.5 1.0 broadcast_select_fusion.1
  44.7 4.6 %shard_map.113 = (f32[22,24,256]{2,1,0:T(8,128)S(1)}, f32[22,24,256]{2,1,0:T(8,128)S(1)}, f32[22,24,256]{2,1,0:T(8,128)S(1)}, f32[22,24,256]{2,1,0:T(8,128)S(1)}...) custom-call(s32[9]{0:T(128)S(1)} %pad_add_fusion.sc, ...), custom_call_target="tpu_custom_call" | custom-call | tf_op jit(solution)/shard_map/pallas_call | solution.py:33
  49.4 17.8 %all_to_all.30.parts = f32[32,32,128]{2,1,0:T(8,128)S(1)} all-to-all(f32[32,32,128]{2,1,0:T(8,128)S(1)} %broadcast_in_dim.76), channel_id=1, replica_groups=mesh['gx'=4,'gy_0'=4,'gy_1'=2,'gz'=8] {'gx','gy_0','gy_1'}, dimensions={0} | all-to-all | bytes 1048576 | tf_op jit(solution)/shard_map/all_to_all | solution.py:588
  67.2 3.1 %shard_map.114 = (f32[20,32,128]{2,1,0:T(8,128)S(1)}, f32[20,32,128]{2,1,0:T(8,128)S(1)}, f32[20,32,128]{2,1,0:T(8,128)S(1)}, f32[20,32,128]{2,1,0:T(8,128)S(1)}...) custom-call(s32[9]{0:T(128)S(1)} %pad_add_fusion.sc, ...), custom_call_target="tpu_custom_call" | custom-call | tf_op jit(solution)/shard_map/pallas_call | solution.py:33
  70.3 5.0 %shard_map.115 = f32[8,8,128]{2,1,0:T(8,128)S(1)} custom-call(s32[9]{0:T(128)S(1)} %pad_add_fusion.sc, f32[32,32,128]{2,1,0:T(8,128)S(1)} %all_to_all.30.parts, f32[20,32,128]{2,1,0:T(8,128)S(1)} %get-tuple-element.43.ax1, f32[20,32,128]{2,1,0:T(8,128)S(1)} %get-tuple-element.44.ay1, f32[20,32,128]{2,1,0:T(8,128)S(1)} %get-tuple-element.45.az1, ...), custom_call_target="tpu_custom_call" | custom-call | tf_op jit(solution)/shard_map/pallas_call | solution.py:33
  75.3 1.8 collective-permute-start.10
  77.1 1.3 collective-permute-start.9
  78.4 1.2 collective-permute-done.10
  79.6 0.8 collective-permute-done.9
  81.2 2.1 collective-permute-start.12
  83.2 1.6 collective-permute-done.11
  84.9 2.4 %collective-permute-start.14 = (f32[1,22,8,256]{3,2,1,0:T(8,128)S(1)}, f32[1,22,8,256]{3,2,1,0:T(8,128)S(1)}, u32[]{:S(2)}, u32[]{:S(2)}) collective-permute-start(f32[1,22,8,256]{3,2,1,0:T(8,128)S(1)} %pad_maximum_fusion.2), channel_id=1, source_target_pairs={{8,0},{16,8},{24,16},{32,24},{40,32},{48,40},{56,48},{0,56},{9,1},... | collective-permute-start | bytes 540680 | tf_op jit(solution)/shard_map/ppermute | solution.py:565
  87.5 3.2 %collective-permute-done.14 = f32[1,22,8,256]{3,2,1,0:T(8,128)S(1)} collective-permute-done((f32[1,22,8,256]{3,2,1,0:T(8,128)S(1)}, f32[1,22,8,256]{3,2,1,0:T(8,128)S(1)}, u32[]{:S(2)}, u32[]{:S(2)}) %collective-permute-start.14) | collective-permute-done | bytes 180256 | tf_op jit(solution)/shard_map/ppermute | solution.py:565
  90.7 3.1 %shard_map.116 = (f32[22,24,256]{2,1,0:T(8,128)S(1)}, f32[22,24,256]{2,1,0:T(8,128)S(1)}, f32[16,128]{1,0:T(8,128)S(1)}) custom-call(f32[22,24,256]{2,1,0:T(8,128)S(1)} %get-tuple-element.73.b.s, f32[22,24,256]{2,1,0:T(8,128)S(1)} %maximum_bitcast_fusion.p, f32[22,24,256]{2,1,0:T(8,128)S(1)} %get-tuple-element.54.ax, ...), custom_call_target="tpu_custom_call" | custom-call | tf_op jit(solution)/shard_map/pallas_call | solution.py:33
  93.8 16.1 %all_to_all.31.parts = f32[32,16,128]{2,1,0:T(8,128)S(1)} all-to-all(f32[32,16,128]{2,1,0:T(8,128)S(1)} %broadcast_in_dim.81), channel_id=1, replica_groups=mesh['gx'=4,'gy_0'=4,'gy_1'=2,'gz'=8] {'gx','gy_0','gy_1'}, dimensions={0} | all-to-all | bytes 524288 | tf_op jit(solution)/shard_map/all_to_all | solution.py:588
  109.9 5.1 %shard_map.117.near = f32[10,24,256]{2,1,0:T(8,128)S(1)} custom-call(s32[9]{0:T(128)S(1)} %pad_add_fusion.sc, f32[32,16,128]{2,1,0:T(8,128)S(1)} %all_to_all.31.parts, f32[20,32,128]{2,1,0:T(8,128)S(1)} %get-tuple-element.43.ax1, f32[20,32,128]{2,1,0:T(8,128)S(1)} %get-tuple-element.44.ay1, f32[20,32,128]{2,1,0:T(8,128)S(1)} %get-tuple-element.45.az1, ...), custom_call_target="tpu_custom_call" | custom-call | tf_op jit(solution)/shard_map/pallas_call | solution.py:33
  115.1 1.3 shard_map.118
  116.4 2.0 collective-permute-start.16
  118.3 0.7 collective-permute-start.15
  119.0 1.3 collective-permute-done.16
  120.3 1.0 collective-permute-done.15
  121.8 2.3 %collective-permute-start.18 = (f32[1,7,8,256]{3,2,1,0:T(8,128)S(1)}, f32[1,7,8,256]{3,2,1,0:T(8,128)S(1)}, u32[]{:S(2)}, u32[]{:S(2)}) collective-permute-start(f32[1,7,8,256]{3,2,1,0:T(8,128)S(1)} %get-tuple-element.79), channel_id=1, source_target_pairs={{64,0},{128,64},{192,128},{0,192},{65,1},{129,65},{193,129},{1,193... | collective-permute-start | bytes 172040 | tf_op jit(solution)/shard_map/ppermute | solution.py:565
  124.1 1.6 collective-permute-done.17
  125.7 2.4 %collective-permute-start.20 = (f32[1,22,8,256]{3,2,1,0:T(8,128)S(1)}, f32[1,22,8,256]{3,2,1,0:T(8,128)S(1)}, u32[]{:S(2)}, u32[]{:S(2)}) collective-permute-start(f32[1,22,8,256]{3,2,1,0:T(8,128)S(1)} %pad_maximum_fusion.3), channel_id=1, source_target_pairs={{8,0},{16,8},{24,16},{32,24},{40,32},{48,40},{56,48},{0,56},{9,1},... | collective-permute-start | bytes 540680 | tf_op jit(solution)/shard_map/ppermute | solution.py:565
  128.4 3.2 %collective-permute-done.20 = f32[1,22,8,256]{3,2,1,0:T(8,128)S(1)} collective-permute-done((f32[1,22,8,256]{3,2,1,0:T(8,128)S(1)}, f32[1,22,8,256]{3,2,1,0:T(8,128)S(1)}, u32[]{:S(2)}, u32[]{:S(2)}) %collective-permute-start.20) | collective-permute-done | bytes 180256 | tf_op jit(solution)/shard_map/ppermute | solution.py:565
  131.7 2.0 shard_map.119
  133.7 16.1 %all_to_all.32.parts = f32[32,16,128]{2,1,0:T(8,128)S(1)} all-to-all(f32[32,16,128]{2,1,0:T(8,128)S(1)} %broadcast_in_dim.83), channel_id=1, replica_groups=mesh['gx'=4,'gy_0'=4,'gy_1'=2,'gz'=8] {'gx','gy_0','gy_1'}, dimensions={0} | all-to-all | bytes 524288 | tf_op jit(solution)/shard_map/all_to_all | solution.py:588
  149.8 5.0 %shard_map.120 = f32[8,8,128]{2,1,0:T(8,128)S(1)} custom-call(s32[9]{0:T(128)S(1)} %pad_add_fusion.sc, f32[32,16,128]{2,1,0:T(8,128)S(1)} %all_to_all.32.parts, f32[20,32,128]{2,1,0:T(8,128)S(1)} %get-tuple-element.43.ax1, f32[20,32,128]{2,1,0:T(8,128)S(1)} %get-tuple-element.44.ay1, f32[20,32,128]{2,1,0:T(8,128)S(1)} %get-tuple-element.45.az1, ...), custom_call_target="tpu_custom_call" | custom-call | tf_op jit(solution)/shard_map/pallas_call | solution.py:33
  154.8 1.8 collective-permute-start.22
  156.6 0.9 collective-permute-start.21
  157.6 1.3 collective-permute-done.22
  158.9 0.8 collective-permute-done.21
  160.0 2.4 %collective-permute-start.24 = (f32[1,7,8,256]{3,2,1,0:T(8,128)S(1)}, f32[1,7,8,256]{3,2,1,0:T(8,128)S(1)}, u32[]{:S(2)}, u32[]{:S(2)}) collective-permute-start(f32[1,7,8,256]{3,2,1,0:T(8,128)S(1)} %get-tuple-element.77), channel_id=1, source_target_pairs={{64,0},{128,64},{192,128},{0,192},{65,1},{129,65},{193,129},{1,193... | collective-permute-start | bytes 172040 | tf_op jit(solution)/shard_map/ppermute | solution.py:565
  162.5 1.6 collective-permute-done.23
  164.1 2.4 %collective-permute-start.26 = (f32[1,22,8,256]{3,2,1,0:T(8,128)S(1)}, f32[1,22,8,256]{3,2,1,0:T(8,128)S(1)}, u32[]{:S(2)}, u32[]{:S(2)}) collective-permute-start(f32[1,22,8,256]{3,2,1,0:T(8,128)S(1)} %pad_maximum_fusion.4), channel_id=1, source_target_pairs={{8,0},{16,8},{24,16},{32,24},{40,32},{48,40},{56,48},{0,56},{9,1},... | collective-permute-start | bytes 540680 | tf_op jit(solution)/shard_map/ppermute | solution.py:565
  166.7 3.2 %collective-permute-done.26 = f32[1,22,8,256]{3,2,1,0:T(8,128)S(1)} collective-permute-done((f32[1,22,8,256]{3,2,1,0:T(8,128)S(1)}, f32[1,22,8,256]{3,2,1,0:T(8,128)S(1)}, u32[]{:S(2)}, u32[]{:S(2)}) %collective-permute-start.26) | collective-permute-done | bytes 180256 | tf_op jit(solution)/shard_map/ppermute | solution.py:565
  170.0 3.0 %shard_map.121 = (f32[22,24,256]{2,1,0:T(8,128)S(1)}, f32[22,24,256]{2,1,0:T(8,128)S(1)}, f32[16,128]{1,0:T(8,128)S(1)}) custom-call(f32[22,24,256]{2,1,0:T(8,128)S(1)} %maximum_bitcast_fusion.1.b.s, f32[22,24,256]{2,1,0:T(8,128)S(1)} %maximum_bitcast_fusion.2.p, f32[22,24,256]{2,1,0:T(8,128)S(1)} %get-tuple-element.54.ax, ...), custom_call_target="tpu_custom_call" | custom-call | tf_op jit(solution)/shard_map/pallas_call | solution.py:33
  173.0 16.3 %all_to_all.33.parts = f32[32,16,128]{2,1,0:T(8,128)S(1)} all-to-all(f32[32,16,128]{2,1,0:T(8,128)S(1)} %broadcast_in_dim.85), channel_id=1, replica_groups=mesh['gx'=4,'gy_0'=4,'gy_1'=2,'gz'=8] {'gx','gy_0','gy_1'}, dimensions={0} | all-to-all | bytes 524288 | tf_op jit(solution)/shard_map/all_to_all | solution.py:588
  189.3 5.1 %shard_map.122.near = f32[10,24,256]{2,1,0:T(8,128)S(1)} custom-call(s32[9]{0:T(128)S(1)} %pad_add_fusion.sc, f32[32,16,128]{2,1,0:T(8,128)S(1)} %all_to_all.33.parts, f32[20,32,128]{2,1,0:T(8,128)S(1)} %get-tuple-element.43.ax1, f32[20,32,128]{2,1,0:T(8,128)S(1)} %get-tuple-element.44.ay1, f32[20,32,128]{2,1,0:T(8,128)S(1)} %get-tuple-element.45.az1, ...), custom_call_target="tpu_custom_call" | custom-call | tf_op jit(solution)/shard_map/pallas_call | solution.py:33
  194.5 5.1 %shard_map.123 = f32[16,128]{1,0:T(8,128)S(1)} custom-call(s32[9]{0:T(128)S(1)} %pad_add_fusion.sc, f32[10,24,256]{2,1,0:T(8,128)S(1)} %shard_map.122.near, f32[3,8,8,128]{3,2,1,0:T(8,128)S(1)} %get-tuple-element.69.misfit, bf16[16,8,8,128]{3,2,1,0:T(8,128)(2,1)S(1)} %copy-done.1, f32[8,512,128]{2,1,0:T(8,128)S(1)} %get-tuple-element.70.slope, ...), custom_call_target="tpu_custom_call" | custom-call | tf_op jit(solution)/shard_map/pallas_call | solution.py:33
  199.7 12.4 %all_to_all.34 = f32[32,16,128]{2,1,0:T(8,128)S(1)} all-to-all(f32[32,16,128]{2,1,0:T(8,128)S(1)} %broadcast_in_dim.86), channel_id=1, replica_groups=mesh['gx'=4,'gy_0'=4,'gy_1'=2,'gz'=8] {'gx','gy_0','gy_1'}, dimensions={0} | all-to-all | bytes 524288 | tf_op jit(solution)/shard_map/all_to_all | solution.py:594
  212.2 10.6 %all_to_all.35 = f32[8,16,128]{2,1,0:T(8,128)S(1)} all-to-all(f32[8,16,128]{2,1,0:T(8,128)S(1)} %broadcast_in_dim.87), channel_id=1, replica_groups=mesh['gx'=4,'gy_0'=4,'gy_1'=2,'gz'=8] {'gz'}, dimensions={0} | all-to-all | bytes 131072 | tf_op jit(solution)/shard_map/all_to_all | solution.py:594
  (83 shorter events, 8.4 us)
Async XLA Ops:
  0.6 23.9 %copy-start.11 = (f32[8,8,128]{2,1,0:T(8,128)S(1)}, f32[8,8,128]{2,1,0:T(8,128)}, u32[]{:S(2)}) copy-start(f32[8,8,128]{2,1,0:T(8,128)} %param.10) | copy-start | bytes 98308
  2.2 1.0 copy-start
  3.1 0.9 copy-start.2
  4.0 0.9 copy-start.4
  4.9 0.7 copy-start.5
  5.6 0.7 copy-start.6
  10.6 8.1 %collective-permute-start.2 = (f32[2,8,8,128]{3,2,1,0:T(8,128)S(1)}, f32[2,8,8,128]{3,2,1,0:T(8,128)S(1)}, u32[]{:S(2)}, u32[]{:S(2)}) collective-permute-start(f32[2,8,8,128]{3,2,1,0:T(8,128)S(1)} %get-tuple-element.41), channel_id=1, source_target_pairs={{0,1},{1,2},{2,3},{3,4},{4,5},{5,6},{6,7},{7,0},{8,9},{9,10},{10,1... | collective-permute-start | bytes 196616 | tf_op jit(solution)/shard_map/ppermute | solution.py:573
  13.2 3.8 %collective-permute-start = (f32[2,8,128]{2,1,0:T(8,128)S(1)}, f32[2,8,128]{2,1,0:T(8,128)S(1)}, u32[]{:S(2)}, u32[]{:S(2)}) collective-permute-start(f32[2,8,128]{2,1,0:T(8,128)S(1)} %get-tuple-element.39), channel_id=1, source_target_pairs={{0,64},{64,128},{128,192},{192,0},{1,65},{65,129},{129,193},{193,1... | collective-permute-start | bytes 24584 | tf_op jit(solution)/shard_map/ppermute | solution.py:573
  14.5 3.1 %collective-permute-start.1 = (f32[2,8,128]{2,1,0:T(8,128)S(1)}, f32[2,8,128]{2,1,0:T(8,128)S(1)}, u32[]{:S(2)}, u32[]{:S(2)}) collective-permute-start(f32[2,8,128]{2,1,0:T(8,128)S(1)} %get-tuple-element.40), channel_id=1, source_target_pairs={{0,8},{8,16},{16,24},{24,32},{32,40},{40,48},{48,56},{56,0},{1,9},... | collective-permute-start | bytes 24584 | tf_op jit(solution)/shard_map/ppermute | solution.py:573
  20.2 4.3 %collective-permute-start.4 = (f32[2,8,8,128]{3,2,1,0:T(8,128)S(1)}, f32[2,8,8,128]{3,2,1,0:T(8,128)S(1)}, u32[]{:S(2)}, u32[]{:S(2)}) collective-permute-start(f32[2,8,8,128]{3,2,1,0:T(8,128)S(1)} %pad_maximum_fusion.6), channel_id=1, source_target_pairs={{0,1},{1,2},{2,3},{3,4},{4,5},{5,6},{6,7},{7,0},{8,9},{9,10},{10,1... | collective-permute-start | bytes 196616 | tf_op jit(solution)/shard_map/ppermute | solution.py:564
  20.6 3.9 %collective-permute-start.3 = (f32[2,8,8,128]{3,2,1,0:T(8,128)S(1)}, f32[2,8,8,128]{3,2,1,0:T(8,128)S(1)}, u32[]{:S(2)}, u32[]{:S(2)}) collective-permute-start(f32[2,8,8,128]{3,2,1,0:T(8,128)S(1)} %pad_maximum_fusion.6), channel_id=1, source_target_pairs={{1,0},{2,1},{3,2},{4,3},{5,4},{6,5},{7,6},{0,7},{9,8},{10,9},{11,1... | collective-permute-start | bytes 196616 | tf_op jit(solution)/shard_map/ppermute | solution.py:565
  25.2 5.2 %collective-permute-start.5 = (f32[2,7,8,256]{3,2,1,0:T(8,128)}, f32[2,7,8,256]{3,2,1,0:T(8,128)}, u32[]{:S(2)}, u32[]{:S(2)}) collective-permute-start(f32[2,7,8,256]{3,2,1,0:T(8,128)} %get-tuple-element.74), channel_id=1, source_target_pairs={{0,64},{64,128},{128,192},{192,0},{1,65},{65,129},{129,193},{193,1... | collective-permute-start | bytes 344072 | tf_op jit(solution)/shard_map/ppermute | solution.py:564
  26.5 4.0 %collective-permute-start.6 = (f32[2,7,8,256]{3,2,1,0:T(8,128)}, f32[2,7,8,256]{3,2,1,0:T(8,128)S(1)}, u32[]{:S(2)}, u32[]{:S(2)}) collective-permute-start(f32[2,7,8,256]{3,2,1,0:T(8,128)} %get-tuple-element.75), channel_id=1, source_target_pairs={{64,0},{128,64},{192,128},{0,192},{65,1},{129,65},{193,129},{1,193... | collective-permute-start | bytes 344072 | tf_op jit(solution)/shard_map/ppermute | solution.py:565
  30.5 0.6 copy-start.7
  31.1 0.8 copy-start.9
  31.9 10.6 %collective-permute-start.8 = (f32[2,22,8,256]{3,2,1,0:T(8,128)}, f32[2,22,8,256]{3,2,1,0:T(8,128)}, u32[]{:S(2)}, u32[]{:S(2)}) collective-permute-start(f32[2,22,8,256]{3,2,1,0:T(8,128)} %pad_maximum_fusion.1), channel_id=1, source_target_pairs={{8,0},{16,8},{24,16},{32,24},{40,32},{48,40},{56,48},{0,56},{9,1},... | collective-permute-start | bytes 1081352 | tf_op jit(solution)/shard_map/ppermute | solution.py:565
  36.1 7.4 %collective-permute-start.7 = (f32[2,22,8,256]{3,2,1,0:T(8,128)}, f32[2,22,8,256]{3,2,1,0:T(8,128)}, u32[]{:S(2)}, u32[]{:S(2)}) collective-permute-start(f32[2,22,8,256]{3,2,1,0:T(8,128)} %pad_maximum_fusion.1), channel_id=1, source_target_pairs={{0,8},{8,16},{16,24},{24,32},{32,40},{40,48},{48,56},{56,0},{1,9},... | collective-permute-start | bytes 1081352 | tf_op jit(solution)/shard_map/ppermute | solution.py:564
  36.8 7.8 %copy-start.8 = (f32[2,7,8,256]{3,2,1,0:T(8,128)S(1)}, f32[2,7,8,256]{3,2,1,0:T(8,128)}, u32[]{:S(2)}) copy-start(f32[2,7,8,256]{3,2,1,0:T(8,128)} %copy-done.7) | copy-start | bytes 344068
  36.8 7.8 %copy-start.10 = (f32[2,7,8,256]{3,2,1,0:T(8,128)S(1)}, f32[2,7,8,256]{3,2,1,0:T(8,128)}, u32[]{:S(2)}) copy-start(f32[2,7,8,256]{3,2,1,0:T(8,128)} %copy-done.9) | copy-start | bytes 344068
  75.3 4.3 %collective-permute-start.10 = (f32[1,8,8,128]{3,2,1,0:T(8,128)S(1)}, f32[1,8,8,128]{3,2,1,0:T(8,128)S(1)}, u32[]{:S(2)}, u32[]{:S(2)}) collective-permute-start(f32[1,8,8,128]{3,2,1,0:T(8,128)S(1)} %bitcast.32), channel_id=1, source_target_pairs={{0,1},{1,2},{2,3},{3,4},{4,5},{5,6},{6,7},{7,0},{8,9},{9,10},{10,1... | collective-permute-start | bytes 98312 | tf_op jit(solution)/shard_map/ppermute | solution.py:564
  77.1 3.3 %collective-permute-start.9 = (f32[1,8,8,128]{3,2,1,0:T(8,128)S(1)}, f32[1,8,8,128]{3,2,1,0:T(8,128)S(1)}, u32[]{:S(2)}, u32[]{:S(2)}) collective-permute-start(f32[1,8,8,128]{3,2,1,0:T(8,128)S(1)} %bitcast.33), channel_id=1, source_target_pairs={{1,0},{2,1},{3,2},{4,3},{5,4},{6,5},{7,6},{0,7},{9,8},{10,9},{11,1... | collective-permute-start | bytes 98312 | tf_op jit(solution)/shard_map/ppermute | solution.py:565
  80.5 4.3 %collective-permute-start.11 = (f32[1,7,8,256]{3,2,1,0:T(8,128)S(1)}, f32[1,7,8,256]{3,2,1,0:T(8,128)S(1)}, u32[]{:S(2)}, u32[]{:S(2)}) collective-permute-start(f32[1,7,8,256]{3,2,1,0:T(8,128)S(1)} %get-tuple-element.80), channel_id=1, source_target_pairs={{0,64},{64,128},{128,192},{192,0},{1,65},{65,129},{129,193},{193,1... | collective-permute-start | bytes 172040 | tf_op jit(solution)/shard_map/ppermute | solution.py:564
  81.2 3.7 %collective-permute-start.12 = (f32[1,7,8,256]{3,2,1,0:T(8,128)S(1)}, f32[1,7,8,256]{3,2,1,0:T(8,128)S(1)}, u32[]{:S(2)}, u32[]{:S(2)}) collective-permute-start(f32[1,7,8,256]{3,2,1,0:T(8,128)S(1)} %get-tuple-element.81), channel_id=1, source_target_pairs={{64,0},{128,64},{192,128},{0,192},{65,1},{129,65},{193,129},{1,193... | collective-permute-start | bytes 172040 | tf_op jit(solution)/shard_map/ppermute | solution.py:565
  84.9 5.8 %collective-permute-start.14 = (f32[1,22,8,256]{3,2,1,0:T(8,128)S(1)}, f32[1,22,8,256]{3,2,1,0:T(8,128)S(1)}, u32[]{:S(2)}, u32[]{:S(2)}) collective-permute-start(f32[1,22,8,256]{3,2,1,0:T(8,128)S(1)} %pad_maximum_fusion.2), channel_id=1, source_target_pairs={{8,0},{16,8},{24,16},{32,24},{40,32},{48,40},{56,48},{0,56},{9,1},... | collective-permute-start | bytes 540680 | tf_op jit(solution)/shard_map/ppermute | solution.py:565
  87.3 3.4 %collective-permute-start.13 = (f32[1,22,8,256]{3,2,1,0:T(8,128)S(1)}, f32[1,22,8,256]{3,2,1,0:T(8,128)S(1)}, u32[]{:S(2)}, u32[]{:S(2)}) collective-permute-start(f32[1,22,8,256]{3,2,1,0:T(8,128)S(1)} %pad_maximum_fusion.2), channel_id=1, source_target_pairs={{0,8},{8,16},{16,24},{24,32},{32,40},{40,48},{48,56},{56,0},{1,9},... | collective-permute-start | bytes 540680 | tf_op jit(solution)/shard_map/ppermute | solution.py:564
  109.9 5.2 %copy-start.3 = (f32[3,8,8,128]{3,2,1,0:T(8,128)S(1)}, f32[3,8,8,128]{3,2,1,0:T(8,128)}, u32[]{:S(2)}) copy-start(f32[3,8,8,128]{3,2,1,0:T(8,128)} %target.3) | copy-start | bytes 294916
  116.4 4.0 %collective-permute-start.16 = (f32[1,8,8,128]{3,2,1,0:T(8,128)S(1)}, f32[1,8,8,128]{3,2,1,0:T(8,128)S(1)}, u32[]{:S(2)}, u32[]{:S(2)}) collective-permute-start(f32[1,8,8,128]{3,2,1,0:T(8,128)S(1)} %bitcast.37), channel_id=1, source_target_pairs={{0,1},{1,2},{2,3},{3,4},{4,5},{5,6},{6,7},{7,0},{8,9},{9,10},{10,1... | collective-permute-start | bytes 98312 | tf_op jit(solution)/shard_map/ppermute | solution.py:564
  118.3 3.0 %collective-permute-start.15 = (f32[1,8,8,128]{3,2,1,0:T(8,128)S(1)}, f32[1,8,8,128]{3,2,1,0:T(8,128)S(1)}, u32[]{:S(2)}, u32[]{:S(2)}) collective-permute-start(f32[1,8,8,128]{3,2,1,0:T(8,128)S(1)} %bitcast.38), channel_id=1, source_target_pairs={{1,0},{2,1},{3,2},{4,3},{5,4},{6,5},{7,6},{0,7},{9,8},{10,9},{11,1... | collective-permute-start | bytes 98312 | tf_op jit(solution)/shard_map/ppermute | solution.py:565
  121.4 4.3 %collective-permute-start.17 = (f32[1,7,8,256]{3,2,1,0:T(8,128)S(1)}, f32[1,7,8,256]{3,2,1,0:T(8,128)S(1)}, u32[]{:S(2)}, u32[]{:S(2)}) collective-permute-start(f32[1,7,8,256]{3,2,1,0:T(8,128)S(1)} %get-tuple-element.78), channel_id=1, source_target_pairs={{0,64},{64,128},{128,192},{192,0},{1,65},{65,129},{129,193},{193,1... | collective-permute-start | bytes 172040 | tf_op jit(solution)/shard_map/ppermute | solution.py:564
  121.8 3.9 %collective-permute-start.18 = (f32[1,7,8,256]{3,2,1,0:T(8,128)S(1)}, f32[1,7,8,256]{3,2,1,0:T(8,128)S(1)}, u32[]{:S(2)}, u32[]{:S(2)}) collective-permute-start(f32[1,7,8,256]{3,2,1,0:T(8,128)S(1)} %get-tuple-element.79), channel_id=1, source_target_pairs={{64,0},{128,64},{192,128},{0,192},{65,1},{129,65},{193,129},{1,193... | collective-permute-start | bytes 172040 | tf_op jit(solution)/shard_map/ppermute | solution.py:565
  125.7 5.8 %collective-permute-start.20 = (f32[1,22,8,256]{3,2,1,0:T(8,128)S(1)}, f32[1,22,8,256]{3,2,1,0:T(8,128)S(1)}, u32[]{:S(2)}, u32[]{:S(2)}) collective-permute-start(f32[1,22,8,256]{3,2,1,0:T(8,128)S(1)} %pad_maximum_fusion.3), channel_id=1, source_target_pairs={{8,0},{16,8},{24,16},{32,24},{40,32},{48,40},{56,48},{0,56},{9,1},... | collective-permute-start | bytes 540680 | tf_op jit(solution)/shard_map/ppermute | solution.py:565
  128.2 3.4 %collective-permute-start.19 = (f32[1,22,8,256]{3,2,1,0:T(8,128)S(1)}, f32[1,22,8,256]{3,2,1,0:T(8,128)S(1)}, u32[]{:S(2)}, u32[]{:S(2)}) collective-permute-start(f32[1,22,8,256]{3,2,1,0:T(8,128)S(1)} %pad_maximum_fusion.3), channel_id=1, source_target_pairs={{0,8},{8,16},{16,24},{24,32},{32,40},{40,48},{48,56},{56,0},{1,9},... | collective-permute-start | bytes 540680 | tf_op jit(solution)/shard_map/ppermute | solution.py:564
  154.8 4.1 %collective-permute-start.22 = (f32[1,8,8,128]{3,2,1,0:T(8,128)S(1)}, f32[1,8,8,128]{3,2,1,0:T(8,128)S(1)}, u32[]{:S(2)}, u32[]{:S(2)}) collective-permute-start(f32[1,8,8,128]{3,2,1,0:T(8,128)S(1)} %bitcast.27), channel_id=1, source_target_pairs={{0,1},{1,2},{2,3},{3,4},{4,5},{5,6},{6,7},{7,0},{8,9},{9,10},{10,1... | collective-permute-start | bytes 98312 | tf_op jit(solution)/shard_map/ppermute | solution.py:564
  156.6 3.1 %collective-permute-start.21 = (f32[1,8,8,128]{3,2,1,0:T(8,128)S(1)}, f32[1,8,8,128]{3,2,1,0:T(8,128)S(1)}, u32[]{:S(2)}, u32[]{:S(2)}) collective-permute-start(f32[1,8,8,128]{3,2,1,0:T(8,128)S(1)} %bitcast.28), channel_id=1, source_target_pairs={{1,0},{2,1},{3,2},{4,3},{5,4},{6,5},{7,6},{0,7},{9,8},{10,9},{11,1... | collective-permute-start | bytes 98312 | tf_op jit(solution)/shard_map/ppermute | solution.py:565
  159.7 4.3 %collective-permute-start.23 = (f32[1,7,8,256]{3,2,1,0:T(8,128)S(1)}, f32[1,7,8,256]{3,2,1,0:T(8,128)S(1)}, u32[]{:S(2)}, u32[]{:S(2)}) collective-permute-start(f32[1,7,8,256]{3,2,1,0:T(8,128)S(1)} %get-tuple-element.76), channel_id=1, source_target_pairs={{0,64},{64,128},{128,192},{192,0},{1,65},{65,129},{129,193},{193,1... | collective-permute-start | bytes 172040 | tf_op jit(solution)/shard_map/ppermute | solution.py:564
  160.0 4.0 %collective-permute-start.24 = (f32[1,7,8,256]{3,2,1,0:T(8,128)S(1)}, f32[1,7,8,256]{3,2,1,0:T(8,128)S(1)}, u32[]{:S(2)}, u32[]{:S(2)}) collective-permute-start(f32[1,7,8,256]{3,2,1,0:T(8,128)S(1)} %get-tuple-element.77), channel_id=1, source_target_pairs={{64,0},{128,64},{192,128},{0,192},{65,1},{129,65},{193,129},{1,193... | collective-permute-start | bytes 172040 | tf_op jit(solution)/shard_map/ppermute | solution.py:565
  164.1 5.8 %collective-permute-start.26 = (f32[1,22,8,256]{3,2,1,0:T(8,128)S(1)}, f32[1,22,8,256]{3,2,1,0:T(8,128)S(1)}, u32[]{:S(2)}, u32[]{:S(2)}) collective-permute-start(f32[1,22,8,256]{3,2,1,0:T(8,128)S(1)} %pad_maximum_fusion.4), channel_id=1, source_target_pairs={{8,0},{16,8},{24,16},{32,24},{40,32},{48,40},{56,48},{0,56},{9,1},... | collective-permute-start | bytes 540680 | tf_op jit(solution)/shard_map/ppermute | solution.py:565
  166.5 3.4 %collective-permute-start.25 = (f32[1,22,8,256]{3,2,1,0:T(8,128)S(1)}, f32[1,22,8,256]{3,2,1,0:T(8,128)S(1)}, u32[]{:S(2)}, u32[]{:S(2)}) collective-permute-start(f32[1,22,8,256]{3,2,1,0:T(8,128)S(1)} %pad_maximum_fusion.4), channel_id=1, source_target_pairs={{0,8},{8,16},{16,24},{24,32},{32,40},{40,48},{48,56},{56,0},{1,9},... | collective-permute-start | bytes 540680 | tf_op jit(solution)/shard_map/ppermute | solution.py:564
  189.3 5.2 %copy-start.1 = (bf16[16,8,8,128]{3,2,1,0:T(8,128)(2,1)S(1)}, bf16[16,8,8,128]{3,2,1,0:T(8,128)(2,1)}, u32[]{:S(2)}) copy-start(bf16[16,8,8,128]{3,2,1,0:T(8,128)(2,1)} %features.3) | copy-start | bytes 786436

commit v2 on v1

--- a/solution.py
+++ b/solution.py
@@ -7,6 +7,7 @@
 from jax.sharding import PartitionSpec as P
 
 GY = ("gy_0", "gy_1")
+GRANT = 12
 XY = ("gx", "gy_0", "gy_1")
 ALL = ("gx", "gy_0", "gy_1", "gz")
 F32 = jnp.float32
@@ -26,17 +27,18 @@
     return jax.ShapeDtypeStruct(shape, dtype)
 
 
-def call(body, outs, args, scratch=(), smem=()):
-    specs = [
-        pl.BlockSpec(memory_space=pltpu.SMEM if i in smem else pltpu.VMEM) for i in range(len(args))
+def call(body, outs, args, scratch=(), smem=(), left=(), grant=12):
+    spaces = [
+        pltpu.SMEM if i in smem else pltpu.HBM if i in left else pltpu.VMEM for i in range(len(args))
     ]
+    specs = [pl.BlockSpec(memory_space=space) for space in spaces]
     return pl.pallas_call(
         body,
         out_shape=outs,
         in_specs=specs,
         out_specs=[pl.BlockSpec(memory_space=pltpu.VMEM)] * len(outs),
         scratch_shapes=list(scratch),
-        compiler_params=pltpu.CompilerParams(vmem_limit_bytes=20 << 20),
+        compiler_params=pltpu.CompilerParams(vmem_limit_bytes=grant << 20),
     )(*args)
 
 
@@ -117,13 +119,15 @@
     def one(i):
         r = rho[i]
         after = back(r, 0)
-        before = forth(r, 0)
         row = lax.broadcasted_iota(jnp.int32, r.shape, 0)
         if whole_y:
             after = jnp.where(row == count - 1, F32(0.0), after)
-            before = jnp.where(row == 0, F32(0.0), before)
         up_y = face(r, after, weight, low[1], high[1])
-        down_y = face(before, r, weight, low[1], high[1])
+        if whole_y:
+            first = jnp.where(r > 0.0, weight * 2.0 / jnp.where(r > 0.0, r, F32(1.0)), F32(0.0))
+            down_y = jnp.where(row == 0, first * low[1], forth(up_y, 0))
+        else:
+            down_y = forth(up_y, 0)
         up_z = face(r, back(r, 1), weight, low[2], high[2])
         diagonal = MASS_SHIFT + ax[i] + ax[i - 1] + up_y + down_y + up_z + forth(up_z, 1)
         ay[i] = jnp.where(row == count - 1, F32(0.0), up_y) if whole_y else up_y
@@ -149,8 +153,9 @@
 def block_means(read, rows, out, out_row):
     pairs = [read(7 + 2 * k) + read(8 + 2 * k) for k in range(4)]
     rows[...] = chosen_dot(jnp.concatenate(pairs, axis=0), lane_pairs(256, 128, 128))
-    total = rows[pl.ds(0, 16, stride=2), :] + rows[pl.ds(1, 16, stride=2), :]
-    out[out_row : out_row + 16, :] = 0.125 * total
+    total = 0.125 * (rows[pl.ds(0, 16, stride=2), :] + rows[pl.ds(1, 16, stride=2), :])
+    for k in range(32):
+        out[k, out_row : out_row + 16, :] = total
 
 
 def presmooth(s, v, va, coefs, rows, out):
@@ -171,7 +176,10 @@
     return values[0::2], values[1::2]
 
 
-def start_body(sc, b, rho, ax, ay, az, w, d, v, out, va, rows):
+def start_body(
+    sc, own, low, high, b, ax, ay, az, w, d, v, out, low_faces, rho, va, rows
+):
+    along_y(sc, own, low, high, b, rho, low_faces)
     coefs = (ax, ay, az, w, d)
     for ref in (ax, ay, az, w, d, v):
         ref[0] = jnp.zeros((NYP, NZP), F32)
@@ -368,26 +376,44 @@
 
 def closure_body(
     sc,
-    features,
+    features_far,
+    velocity_far,
+    target_far,
+    density_far,
     weight_in,
     bias_in,
     weight_out,
-    velocity,
-    target,
     flux,
     slope,
     hidden,
-    face_x,
-    face_y,
-    face_z,
+    message,
+    target_faces,
+    marks,
+    features,
+    velocity,
+    target,
     kin,
     bias,
     kout,
+    sems,
 ):
+    copies = [
+        pltpu.make_async_copy(source, place, sems.at[k])
+        for k, (source, place) in enumerate(
+            (
+                (features_far, features),
+                (velocity_far, velocity),
+                (target_far, target),
+                (density_far, message.at[8:16]),
+            )
+        )
+    ]
+    for copy in copies:
+        copy.start()
     units = members(512, 64)
     narrow = dot_across(units, weight_in[...]).astype(BF16)
     kin[...] = same_row(dot_across(narrow, members(128, 16)))
-    narrow = dot_across(members(24, 3), weight_out[...]).astype(BF16)
+    narrow = jnp.dot(members(24, 3), weight_out[...], preferred_element_type=F32).astype(BF16)
     kout[...] = same_row(dot_across(narrow, units))
     bias[...] = dot_across(
         units.astype(F32), jnp.broadcast_to(bias_in[...], (128, 64)), HIGHEST
@@ -400,6 +426,8 @@
     col = lax.broadcasted_iota(jnp.int32, (8, 128), 1)
     factor_y = jnp.where(row == 7, high_y, F32(1.0))
     factor_z = jnp.where(col == 127, high_z, F32(1.0))
+    for copy in copies:
+        copy.wait()
 
     def one(x):
         columns = features[:, x, :, :].astype(F32).reshape(128, 128).astype(BF16)
@@ -415,13 +443,29 @@
         flux[2, x] = (velocity[2, x] + shift[16:24]) * factor_z
 
     planes(0, 8, one, 1)
-    face_x[0] = flux[0, 7]
-    face_x[1] = target[0, 7]
+    zero = jnp.zeros((8, 128), F32)
+    ends = zero
     for x in range(8):
-        face_y[0, x : x + 1, :] = flux[1, x, 7:8, :]
-        face_y[1, x : x + 1, :] = target[1, x, 7:8, :]
-    face_z[0] = flux[2]
-    face_z[1] = target[2]
+        bx, by, bz = shifted(
+            lambda d, i: flux[d, i], lambda: zero, lambda i: zero, lambda i: zero, x
+        )
+        message[x] = -((flux[0, x] - bx) + (flux[1, x] - by) + (flux[2, x] - bz))
+        message[17, x : x + 1, :] = flux[1, x, 7:8, :]
+        target_faces[1, x : x + 1, :] = target[1, x, 7:8, :]
+        ends = jnp.where(col == x, pltpu.roll(flux[2, x], x + 1, 1), ends)
+        ends = jnp.where(col == x + 8, pltpu.roll(target[2, x], x + 9, 1), ends)
+    message[16] = flux[0, 7]
+    message[18] = ends
+    target_faces[0] = target[0, 7]
+    inside = inside_of(sc)
+    wide_col = lax.broadcasted_iota(jnp.int32, (1, 256), 1)
+    one_row = jnp.ones((1, 256), F32)
+    marks[0:1, :] = jnp.where(wide_col < 64, inside[2][1], F32(0.0))
+    marks[1:2, :] = jnp.where(wide_col < 64, F32(0.0), inside[2][0])
+    for d in range(2):
+        marks[2 + 2 * d : 3 + 2 * d, :] = one_row * inside[d][0]
+        marks[3 + 2 * d : 4 + 2 * d, :] = one_row * inside[d][1]
+    marks[6:8, :] = jnp.zeros((2, 256), F32)
 
 
 def shifted(field, low_x, low_y, low_z, x):
@@ -433,20 +477,82 @@
     return before_x, before_y, before_z
 
 
-def source_body(sc, flux, low_x, low_y, low_z, out):
-    inner = [jnp.where(sc[d] > 0, F32(1.0), F32(0.0)) for d in range(3)]
-    for x in range(8):
-        bx, by, bz = shifted(
-            lambda d, i: flux[d, i],
-            lambda: low_x[0] * inner[0],
-            lambda i: jnp.broadcast_to(low_y[0, i : i + 1, :] * inner[1], (8, 128)),
-            lambda i: forth(low_z[0, i] * inner[2], 1),
-            x,
+def inside_of(sc):
+    last = (3, 7, 7)
+    return [
+        (
+            jnp.where(sc[d] > 0, F32(1.0), F32(0.0)),
+            jnp.where(sc[d] < last[d], F32(1.0), F32(0.0)),
         )
-        out[x] = -((flux[0, x] - bx) + (flux[1, x] - by) + (flux[2, x] - bz))
-
-
-def middle_body(sc, near, flux, target, low_x, low_y, low_z, ax, ay, az, new, misfit, out):
+        for d in range(3)
+    ]
+
+
+def along_z_body(sc, own, before, after, target_faces, wide, up, down):
+    has_before, has_after = inside_of(sc)[2]
+    col = lax.broadcasted_iota(jnp.int32, (8, 128), 1)
+
+    def around_z(k):
+        return jnp.where(col < 64, after[k] * has_after, before[k] * has_before)
+
+    for k in range(18):
+        here, there = own[k], around_z(k)
+        if k < 8:
+            turn = (128 - k) % 128
+            low = pltpu.roll(before[18], turn, 1) if turn else before[18]
+            high = pltpu.roll(own[18], turn, 1) if turn else own[18]
+            here = jnp.where(col == 0, here + low * has_before, here)
+            there = jnp.where(col == 0, there + high * has_after, there)
+        wide[k, :, 0:128] = here
+        wide[k, :, 128:256] = there
+    for k in range(7):
+        up[k] = wide[k + 1]
+        up[k + 7] = wide[k + 9]
+        down[k] = wide[k]
+        down[k + 7] = wide[k + 8]
+    up[14] = wide[17]
+    down[14] = wide[17]
+    up[15] = wide[16]
+    up[16, :, 0:128] = target_faces[0]
+    up[16, :, 128:256] = jnp.zeros((8, 128), F32)
+
+
+def along_x_body(sc, wide, low, high, target_faces, out):
+    has_before, has_after = inside_of(sc)[0]
+    for k in range(7):
+        out[k] = low[k] * has_before
+        out[k + 22] = low[k + 7] * has_before
+        more = wide[16] if k == 0 else jnp.zeros((8, 256), F32)
+        out[k + 15] = (high[k] + more) * has_after
+        out[k + 37] = high[k + 7] * has_after
+    for k in range(8):
+        out[k + 7] = wide[k] + low[15] * has_before if k == 0 else wide[k]
+        out[k + 29] = wide[k + 8]
+    out[44] = low[14] * has_before
+    out[45] = wide[17]
+    out[46] = high[14] * has_after
+    out[47, :, 0:128] = target_faces[1]
+    out[47, :, 128:256] = jnp.zeros((8, 128), F32)
+
+
+def along_y(sc, own, low, high, b, rho, low_faces):
+    has_before, has_after = inside_of(sc)[1]
+    row = lax.broadcasted_iota(jnp.int32, (8, 256), 0)
+    for i in range(22):
+        k, r = divmod(i + 1, 8)
+        more = jnp.broadcast_to(low[44 + k, r : r + 1, :] * has_before, (8, 256))
+        next_more = jnp.broadcast_to(own[44 + k, r : r + 1, :], (8, 256))
+        b[i, 0:8, :] = low[i] * has_before
+        b[i, 8:16, :] = jnp.where(row == 0, own[i] + more, own[i])
+        b[i, 16:24, :] = jnp.where(row == 0, high[i] + next_more, high[i]) * has_after
+        rho[i, 0:8, :] = low[i + 22] * has_before
+        rho[i, 8:16, :] = own[i + 22]
+        rho[i, 16:24, :] = high[i + 22] * has_after
+    low_faces[0] = low[45, :, 0:128]
+    low_faces[1] = low[47, :, 0:128]
+
+
+def middle_body(sc, near, flux, target, from_x, low_y, from_z, ax, ay, az, new, misfit, out):
     scale = F32(1.0 / CELLS)
     inner = [jnp.where(sc[d] > 0, F32(1.0), F32(0.0)) for d in range(3)]
 
@@ -466,7 +572,8 @@
     def low_weighted_x():
         up = ax[6, 8:16, 0:128]
         rise = (near[1] - near[0])[8:16, 0:128]
-        return up * ((low_x[0] - up * rise - low_x[1]) * (scale * inner[0]))
+        value = from_x[15, :, 0:128] - up * rise - from_x[16, :, 0:128]
+        return up * (value * (scale * inner[0]))
 
     def low_weighted_y(x):
         up = ay[x + 7, 7:8, 0:128]
@@ -478,7 +585,9 @@
         p = near[x + 1, 8:16, :]
         rise = (back(p, 1) - p)[:, 128:256]
         up = az[x + 7, 8:16, 128:256]
-        value = up * ((low_z[0, x] - up * rise - low_z[1, x]) * (scale * inner[2]))
+        low_flux = pltpu.roll(from_z[18], 127 - x, 1)
+        low_target = pltpu.roll(from_z[18], 119 - x, 1)
+        value = up * ((low_flux - up * rise - low_target) * (scale * inner[2]))
         return forth(value, 1)
 
     refs = (ax, ay, az)
@@ -494,7 +603,7 @@
 def gradient_body(
     sc, near, misfit, features, slope, hidden, weight_out, out, acc_in, acc_bias, acc_out, kback
 ):
-    narrow = jnp.dot(members(512, 64), weight_out[...], preferred_element_type=F32).astype(BF16)
+    narrow = dot_across(members(512, 64), weight_out[...]).astype(BF16)
     kback[...] = same_row(dot_across(narrow, members(24, 3)))
     _, high = opens_of(sc)
     high_x = jnp.where(sc[0] == 3, high[0], F32(1.0))
@@ -552,85 +661,106 @@
         jnp.ones((8, 128), F32), acc_bias[...], across, precision=HIGHEST, preferred_element_type=F32
     )
     folded = exact_dot(jnp.concatenate([in_part, out_part, bias_part], axis=0), fold)
-    out[0:8, 0:64] = folded[0:8]
-    out[0:8, 64:128] = folded[8:16]
-    out[8:16, 0:64] = folded[16:24]
-    out[8:16, 64:128] = folded[24:32]
-
-
-def neighbours(up, down, axis):
+    packed = jnp.concatenate(
+        [
+            jnp.concatenate([folded[0:8], folded[8:16]], axis=1),
+            jnp.concatenate([folded[16:24], folded[24:32]], axis=1),
+        ],
+        axis=0,
+    )
+    for k in range(32):
+        out[k] = packed
+
+
+def plane_sum_body(parts, out):
+    total = parts[0]
+    for k in range(1, 32):
+        total = total + parts[k]
+    for k in range(8):
+        out[k] = total
+
+
+def ring(up, down, axis):
     count = lax.axis_size(axis)
     ups = [(i, (i + 1) % count) for i in range(count)]
-    before = lax.ppermute(up, axis, ups)
-    after = lax.ppermute(down, axis, [(b, a) for a, b in ups])
-    place = lax.axis_index(axis)
-    zero = F32(0.0)
-    return jnp.where(place > 0, before, zero), jnp.where(place < count - 1, after, zero)
-
-
-def from_before(face, axis):
-    count = lax.axis_size(axis)
-    return lax.ppermute(face, axis, [(i, (i + 1) % count) for i in range(count)])
-
-
-def exchanged(own):
-    before, after = neighbours(own, own, "gz")
-    lane = lax.broadcasted_iota(jnp.int32, own.shape, 3)
-    wide = jnp.concatenate([own, jnp.where(lane < 64, after, before)], axis=3)
-    low, high = neighbours(wide[:, 1:8], wide[:, 0:7], "gx")
-    wide = jnp.concatenate([low, wide, high], axis=1)
-    low, high = neighbours(wide, wide, GY)
-    return jnp.concatenate([low, wide, high], axis=2)
-
-
-def over_plane(part):
-    copies = jnp.broadcast_to(part, (32, *part.shape))
-    return lax.all_to_all(copies, XY, split_axis=0, concat_axis=0, tiled=True)
-
-
-def summed(part, axes):
-    for axis in axes:
-        copies = jnp.broadcast_to(part, (lax.axis_size(axis), *part.shape))
-        part = jnp.sum(lax.all_to_all(copies, axis, split_axis=0, concat_axis=0, tiled=True), axis=0)
-    return part
+    return lax.ppermute(up, axis, ups), lax.ppermute(down, axis, [(b, a) for a, b in ups])
+
+
+def exchanged(own, marks):
+    before, after = ring(own, own, "gz")
+    wide = jnp.concatenate([own, after * marks[0, :128] + before * marks[1, :128]], axis=2)
+    low, high = ring(wide[1:8], wide[0:7], "gx")
+    wide = jnp.concatenate([low * marks[2], wide, high * marks[3]], axis=0)
+    low, high = ring(wide, wide, GY)
+    return jnp.concatenate([low * marks[4], wide, high * marks[5]], axis=1)
+
+
+def unpack_body(parts, grad_in, grad_bias, grad_out):
+    total = parts[0]
+    for k in range(1, 8):
+        total = total + parts[k]
+    grad_in[0:8, :] = total[0:8, 0:64]
+    grad_in[8:16, :] = total[0:8, 64:128]
+    grad_bias[...] = total[8:9, 64:128]
+    grad_out[...] = total[8:11, 0:64]
+
+
+def sent_to_all(copies, axis):
+    return lax.all_to_all(copies, axis, split_axis=0, concat_axis=0, tiled=True)
 
 
 def per_device(velocity, features, density, target, weight_in, bias_in, weight_out, open_faces):
     place = jnp.stack([lax.axis_index("gx"), lax.axis_index(GY), lax.axis_index("gz")])
     sc = jnp.concatenate([place.astype(jnp.int32), open_faces])
     block = (8, 8, 128)
-    flux, slope, hidden, face_x, face_y, face_z = call(
+    narrow_out = weight_out.T
+    flux, slope, hidden, message, target_faces, marks = call(
         closure_body,
         [
             shaped((3, *block)),
             shaped((8, 512, 128)),
             shaped((8, 512, 128), BF16),
+            shaped((19, 8, 128)),
             shaped((2, 8, 128)),
-            shaped((2, 8, 128)),
-            shaped((2, *block)),
+            shaped((8, 256)),
         ],
-        (sc, features, weight_in, bias_in[None], weight_out, velocity, target),
-        [pltpu.VMEM((512, 128), BF16), pltpu.VMEM((512, 128), F32), pltpu.VMEM((24, 512), BF16)],
+        (sc, features, velocity, target, density, weight_in, bias_in[None], narrow_out),
+        [
+            pltpu.VMEM((16, *block), BF16),
+            pltpu.VMEM((3, *block), F32),
+            pltpu.VMEM((3, *block), F32),
+            pltpu.VMEM((512, 128), BF16),
+            pltpu.VMEM((512, 128), F32),
+            pltpu.VMEM((24, 512), BF16),
+            pltpu.SemaphoreType.DMA((4,)),
+        ],
         smem=(0,),
-    )
-    low_x = from_before(face_x, "gx")
-    low_y = from_before(face_y, GY)
-    low_z = from_before(face_z, "gz")
-    (source,) = call(
-        source_body, [shaped(block)], (sc, flux, low_x, low_y, low_z), smem=(0,)
-    )
-    both = exchanged(jnp.stack([source, density]))
-    region = shaped(REGION)
+        left=(1, 2, 3, 4),
+        grant=GRANT,
+    )
+    from_z, after = ring(message, message, "gz")
+    wide, up, down = call(
+        along_z_body,
+        [shaped((18, 8, 256)), shaped((17, 8, 256)), shaped((15, 8, 256))],
+        (sc, message, from_z, after, target_faces),
+        smem=(0,),
+    )
+    from_x, after = ring(up, down, "gx")
+    (message,) = call(
+        along_x_body, [shaped((48, 8, 256))], (sc, wide, from_x, after, target_faces), smem=(0,)
+    )
+    before, after = ring(message, message, GY)
+    region, to_plane = shaped(REGION), shaped((32, 16, 128))
     one_region = [pltpu.VMEM(REGION, F32), pltpu.VMEM((32, 128), F32)]
-    *coefs, v, part = call(
+    source, *coefs, v, part, low_y = call(
         start_body,
-        [region] * 6 + [shaped((32, 128))],
-        (sc, both[0], both[1]),
-        one_region,
+        [region] * 7 + [shaped((32, 32, 128)), shaped((2, 8, 128))],
+        (sc, message, before, after),
+        [pltpu.VMEM(REGION, F32), *one_region],
         smem=(0,),
     )
     ax, ay, az, w, d = coefs
-    parts = over_plane(part)
+    parts = sent_to_all(part, XY)
     coarse = call(
         coarse_body,
         [shaped(L1)] * 5 + [shaped(L2)] * 5,
@@ -647,33 +777,33 @@
             POST_SCRATCH,
             smem=(0,),
         )
-        p = exchanged(own[None])[0]
+        p = exchanged(own, marks)
         s, v, part = call(
-            again_body, [region, region, shaped((16, 128))], (b, p, *coefs), one_region
+            again_body, [region, region, to_plane], (b, p, *coefs), one_region
         )
         (near,) = call(
             post_near_body,
             [shaped((10, NYP, NZP))],
-            (sc, over_plane(part), *coarse, s, v, ax, ay, az, w, p),
+            (sc, sent_to_all(part, XY), *coarse, s, v, ax, ay, az, w, p),
             POST_SCRATCH,
             smem=(0,),
         )
         return near
 
-    near = finish_solve(both[0], v, parts)
+    near = finish_solve(source, v, parts)
     new_velocity, misfit, grad_pressure = call(
         middle_body,
         [shaped((3, *block)), shaped((3, *block)), shaped(block)],
-        (sc, near, flux, target, low_x, low_y, low_z, ax, ay, az),
+        (sc, near, flux, target, from_x, low_y, from_z, ax, ay, az),
         smem=(0,),
     )
-    b = exchanged(grad_pressure[None])[0]
-    v, part = call(pre_body, [region, shaped((16, 128))], (b, *coefs), one_region)
-    near = finish_solve(b, v, over_plane(part))
+    b = exchanged(grad_pressure, marks)
+    v, part = call(pre_body, [region, to_plane], (b, *coefs), one_region)
+    near = finish_solve(b, v, sent_to_all(part, XY))
     (packed,) = call(
         gradient_body,
-        [shaped((16, 128))],
-        (sc, near, misfit, features, slope, hidden, weight_out),
+        [to_plane],
+        (sc, near, misfit, features, slope, hidden, narrow_out),
         [
             pltpu.VMEM((128, 512), F32),
             pltpu.VMEM((512, 128), F32),
@@ -682,9 +812,13 @@
         ],
         smem=(0,),
     )
-    total = summed(packed, (XY, "gz"))
-    grad_in = jnp.concatenate([total[0:8, 0:64], total[0:8, 64:128]], axis=0)
-    return new_velocity, grad_in, total[8, 64:128], total[8:11, 0:64].T
+    (plane,) = call(plane_sum_body, [shaped((8, 16, 128))], (sent_to_all(packed, XY),))
+    grad_in, grad_bias, grad_out = call(
+        unpack_body,
+        [shaped((16, 64)), shaped((1, 64)), shaped((3, 64))],
+        (sent_to_all(plane, "gz"),),
+    )
+    return new_velocity, grad_in, grad_bias[0], grad_out.T
 
 
 def solution(mesh):

time: 225 us -> 218 us (0.969)
  other arithmetic: 5.44 us -> 1.1 us
  starting transfers between devices: 41.2 us -> 38.7 us
    ppermute x27 -> x24, starting transfers between devices: 41.2 us -> 38.7 us  [the longest x12 32.6 us: ring(): lax.ppermute(down, axis, [(b, a) for a, b in ups])]
    pallas_call x13 -> x16, Pallas kernels: 47.5 us -> 49.5 us  [call(): pl.pallas_call(body, out_shape=outs, in_specs=specs, out_specs=[pl.BlockS...]
    ppermute x27 -> x24, waiting for transfers between devices: 32.5 us -> 31.1 us  [the longest x12 19.2 us: ring(): lax.ppermute(down, axis, [(b, a) for a, b in ups])]
    unnamed x25 -> x20, local copies, waits for them, and re-layouts: 5.48 us -> 5.52 us
  transfers between devices with their start and end apart: 27 -> 24, of which waited for: 18 -> 14; matrix products, arithmetic and copies ran while one was open for 0% -> 0% of each run, Pallas kernels for 0% -> 0%
where the time goes in v2:
time: 218 us; the launch traced here: 217 us
  blocking collectives  90 us (41%)
  Pallas kernels  49.5 us (23%)
  starting transfers between devices  38.7 us (18%)
  waiting for transfers between devices  31.1 us (14%)
  local copies, waits for them, and re-layouts  5.53 us (3%)
    all_to_all x6, blocking collectives, sent_to_all(): return lax.all_to_all(copies, axis, split_axis=0, concat_axis=0, tiled=True)  90 us
    pallas_call x16, Pallas kernels, call(): pl.pallas_call(body, out_shape=outs, in_specs=specs, out_specs=[pl.BlockS...  49.5 us
    ppermute x12, starting transfers between devices, ring(): lax.ppermute(down, axis, [(b, a) for a, b in ups])  32.6 us
    ppermute x12, waiting for transfers between devices, ring(): lax.ppermute(down, axis, [(b, a) for a, b in ups])  19.2 us
    ppermute x12, waiting for transfers between devices, ring(): lax.ppermute(up, axis, ups)  12 us
    ppermute x12, starting transfers between devices, ring(): lax.ppermute(up, axis, ups)  6.05 us
    unnamed x20, local copies, waits for them, and re-layouts  5.52 us
  transfers between devices with their start and end apart: 24, of which 14 were waited for; matrix products, arithmetic and copies ran while one was open for 0% of the time, Pallas kernels for 0%

profile of v2, /device:TPU:1, one launch (start us, length us, event | category | flops | bytes accessed | tf_op | source)
XLA Modules:
  0.0 217.0 jit_solution(7660351164389340433)
XLA Ops:
  0.6 0.7 pad_add_fusion.sc
  1.4 0.9 copy-done
  2.3 0.9 copy-done.2
  3.2 0.9 copy-done.4
  4.1 0.8 copy-done.5
  4.9 0.7 copy-done.6
  5.6 0.7 copy-done.7
  6.2 0.7 copy-done.9
  6.9 4.8 %shard_map.111 = (f32[3,8,8,128]{3,2,1,0:T(8,128)S(1)}, f32[8,512,128]{2,1,0:T(8,128)S(1)}, bf16[8,512,128]{2,1,0:T(8,128)(2,1)S(1)}, f32[19,8,128]{2,1,0:T(8,12...) custom-call(s32[9]{0:T(128)S(1)} %pad_add_fusion.sc, bf16[16,8,8,128]{3,2,1,0:T(8,128)(2,1)S(1)} %copy-done, ...), custom_call_target="tpu_custom_call" | custom-call | tf_op jit(solution)/shard_map/pallas_call | solution.py:35
  11.7 6.5 %collective-permute-start.1 = (f32[19,8,128]{2,1,0:T(8,128)S(1)}, f32[19,8,128]{2,1,0:T(8,128)S(1)}, u32[]{:S(2)}, u32[]{:S(2)}) collective-permute-start(f32[19,8,128]{2,1,0:T(8,128)S(1)} %get-tuple-element.46.own), channel_id=1, source_target_pairs={{1,0},{2,1},{3,2},{4,3},{5,4},{6,5},{7,6},{0,7},{9,8},{10,9},{11,1... | collective-permute-start | bytes 233480 | tf_op jit(solution)/shard_map/ppermute | solution.py:686
  18.2 1.4 collective-permute-done.1.after
  19.6 3.0 %collective-permute-done.before.from_z = f32[19,8,128]{2,1,0:T(8,128)S(1)} collective-permute-done((f32[19,8,128]{2,1,0:T(8,128)S(1)}, f32[19,8,128]{2,1,0:T(8,128)S(1)}, u32[]{:S(2)}, u32[]{:S(2)}) %collective-permute-start) | collective-permute-done | bytes 77856 | tf_op jit(solution)/shard_map/ppermute | solution.py:686
  22.7 0.6 shard_map.112
  23.3 1.4 collective-permute-start.2
  24.7 1.5 collective-permute-start.3
  26.2 2.2 %collective-permute-done.3.high = f32[15,8,256]{2,1,0:T(8,128)S(1)} collective-permute-done((f32[15,8,256]{2,1,0:T(8,128)S(1)}, f32[15,8,256]{2,1,0:T(8,128)S(1)}, u32[]{:S(2)}, u32[]{:S(2)}) %collective-permute-start.3) | collective-permute-done | bytes 122912 | tf_op jit(solution)/shard_map/ppermute | solution.py:686
  28.4 0.1 collective-permute-done.2.low.from_x
  28.5 0.6 shard_map.113.own
  29.1 3.4 %collective-permute-start.5 = (f32[48,8,256]{2,1,0:T(8,128)S(1)}, f32[48,8,256]{2,1,0:T(8,128)S(1)}, u32[]{:S(2)}, u32[]{:S(2)}) collective-permute-start(f32[48,8,256]{2,1,0:T(8,128)S(1)} %shard_map.113.own), channel_id=1, source_target_pairs={{8,0},{16,8},{24,16},{32,24},{40,32},{48,40},{56,48},{0,56},{9,1},... | collective-permute-start | bytes 1179656 | tf_op jit(solution)/shard_map/ppermute | solution.py:686
  32.5 1.1 collective-permute-start.4
  33.6 5.7 %collective-permute-done.5.high = f32[48,8,256]{2,1,0:T(8,128)S(1)} collective-permute-done((f32[48,8,256]{2,1,0:T(8,128)S(1)}, f32[48,8,256]{2,1,0:T(8,128)S(1)}, u32[]{:S(2)}, u32[]{:S(2)}) %collective-permute-start.5) | collective-permute-done | bytes 393248 | tf_op jit(solution)/shard_map/ppermute | solution.py:686
  39.4 4.7 %shard_map.114 = (f32[22,24,256]{2,1,0:T(8,128)S(1)}, f32[22,24,256]{2,1,0:T(8,128)S(1)}, f32[22,24,256]{2,1,0:T(8,128)S(1)}, f32[22,24,256]{2,1,0:T(8,128)S(1)}...) custom-call(s32[9]{0:T(128)S(1)} %pad_add_fusion.sc, ...), custom_call_target="tpu_custom_call" | custom-call | tf_op jit(solution)/shard_map/pallas_call | solution.py:35
  44.1 18.4 %all_to_all.30.parts = f32[32,32,128]{2,1,0:T(8,128)S(1)} all-to-all(f32[32,32,128]{2,1,0:T(8,128)S(1)} %get-tuple-element.52), channel_id=1, replica_groups=mesh['gx'=4,'gy_0'=4,'gy_1'=2,'gz'=8] {'gx','gy_0','gy_1'}, dimensions={0} | all-to-all | bytes 1048576 | tf_op jit(solution)/shard_map/all_to_all | solution.py:709
  62.5 3.1 %shard_map.115 = (f32[20,32,128]{2,1,0:T(8,128)S(1)}, f32[20,32,128]{2,1,0:T(8,128)S(1)}, f32[20,32,128]{2,1,0:T(8,128)S(1)}, f32[20,32,128]{2,1,0:T(8,128)S(1)}...) custom-call(s32[9]{0:T(128)S(1)} %pad_add_fusion.sc, ...), custom_call_target="tpu_custom_call" | custom-call | tf_op jit(solution)/shard_map/pallas_call | solution.py:35
  65.6 5.0 %shard_map.116 = f32[8,8,128]{2,1,0:T(8,128)S(1)} custom-call(s32[9]{0:T(128)S(1)} %pad_add_fusion.sc, f32[32,32,128]{2,1,0:T(8,128)S(1)} %all_to_all.30.parts, f32[20,32,128]{2,1,0:T(8,128)S(1)} %get-tuple-element.53.ax1, f32[20,32,128]{2,1,0:T(8,128)S(1)} %get-tuple-element.54.ay1, f32[20,32,128]{2,1,0:T(8,128)S(1)} %get-tuple-element.55.az1, ...), custom_call_target="tpu_custom_call" | custom-call | tf_op jit(solution)/shard_map/pallas_call | solution.py:35
  70.6 0.1 collective-permute-start.7
  70.7 2.7 %collective-permute-start.6 = (f32[8,8,128]{2,1,0:T(8,128)S(1)}, f32[8,8,128]{2,1,0:T(8,128)S(1)}, u32[]{:S(2)}, u32[]{:S(2)}) collective-permute-start(f32[8,8,128]{2,1,0:T(8,128)S(1)} %shard_map.116), channel_id=1, source_target_pairs={{1,0},{2,1},{3,2},{4,3},{5,4},{6,5},{7,6},{0,7},{9,8},{10,9},{11,1... | collective-permute-start | bytes 98312 | tf_op jit(solution)/shard_map/ppermute | solution.py:686
  73.4 1.3 collective-permute-done.7
  74.7 1.0 collective-permute-start.8
  75.7 1.8 collective-permute-start.9
  77.4 1.6 collective-permute-done.8
  79.1 2.7 %collective-permute-start.11 = (f32[22,8,256]{2,1,0:T(8,128)S(1)}, f32[22,8,256]{2,1,0:T(8,128)S(1)}, u32[]{:S(2)}, u32[]{:S(2)}) collective-permute-start(f32[22,8,256]{2,1,0:T(8,128)S(1)} %pad_maximum_fusion.3), channel_id=1, source_target_pairs={{8,0},{16,8},{24,16},{32,24},{40,32},{48,40},{56,48},{0,56},{9,1},... | collective-permute-start | bytes 540680 | tf_op jit(solution)/shard_map/ppermute | solution.py:686
  81.8 0.2 collective-permute-start.10
  82.0 3.2 %collective-permute-done.11 = f32[22,8,256]{2,1,0:T(8,128)S(1)} collective-permute-done((f32[22,8,256]{2,1,0:T(8,128)S(1)}, f32[22,8,256]{2,1,0:T(8,128)S(1)}, u32[]{:S(2)}, u32[]{:S(2)}) %collective-permute-start.11) | collective-permute-done | bytes 180256 | tf_op jit(solution)/shard_map/ppermute | solution.py:686
  85.2 3.1 %shard_map.117 = (f32[22,24,256]{2,1,0:T(8,128)S(1)}, f32[22,24,256]{2,1,0:T(8,128)S(1)}, f32[32,16,128]{2,1,0:T(8,128)S(1)}) custom-call(f32[22,24,256]{2,1,0:T(8,128)S(1)} %get-tuple-element.51.s.b, f32[22,24,256]{2,1,0:T(8,128)S(1)} %pad_maximum_fusion.p, f32[22,24,256]{2,1,0:T(8,128)S(1)} %get-tuple-element.64.ax, ...), custom_call_target="tpu_custom_call" | custom-call | tf_op jit(solution)/shard_map/pallas_call | solution.py:35
  88.3 16.1 %all_to_all.31.parts = f32[32,16,128]{2,1,0:T(8,128)S(1)} all-to-all(f32[32,16,128]{2,1,0:T(8,128)S(1)} %get-tuple-element.70), channel_id=1, replica_groups=mesh['gx'=4,'gy_0'=4,'gy_1'=2,'gz'=8] {'gx','gy_0','gy_1'}, dimensions={0} | all-to-all | bytes 524288 | tf_op jit(solution)/shard_map/all_to_all | solution.py:709
  104.4 5.1 %shard_map.118.near = f32[10,24,256]{2,1,0:T(8,128)S(1)} custom-call(s32[9]{0:T(128)S(1)} %pad_add_fusion.sc, f32[32,16,128]{2,1,0:T(8,128)S(1)} %all_to_all.31.parts, f32[20,32,128]{2,1,0:T(8,128)S(1)} %get-tuple-element.53.ax1, f32[20,32,128]{2,1,0:T(8,128)S(1)} %get-tuple-element.54.ay1, f32[20,32,128]{2,1,0:T(8,128)S(1)} %get-tuple-element.55.az1, ...), custom_call_target="tpu_custom_call" | custom-call | tf_op jit(solution)/shard_map/pallas_call | solution.py:35
  109.6 1.3 shard_map.119
  110.9 2.9 %collective-permute-start.12 = (f32[8,8,128]{2,1,0:T(8,128)S(1)}, f32[8,8,128]{2,1,0:T(8,128)S(1)}, u32[]{:S(2)}, u32[]{:S(2)}) collective-permute-start(f32[8,8,128]{2,1,0:T(8,128)S(1)} %get-tuple-element.76), channel_id=1, source_target_pairs={{1,0},{2,1},{3,2},{4,3},{5,4},{6,5},{7,6},{0,7},{9,8},{10,9},{11,1... | collective-permute-start | bytes 98312 | tf_op jit(solution)/shard_map/ppermute | solution.py:686
  113.8 1.6 collective-permute-done.13
  115.4 0.6 collective-permute-start.14
  116.0 2.2 collective-permute-start.15
  118.2 1.6 collective-permute-done.14
  119.8 1.9 collective-permute-start.17
  121.7 0.4 collective-permute-start.16
  122.1 3.5 %collective-permute-done.17 = f32[22,8,256]{2,1,0:T(8,128)S(1)} collective-permute-done((f32[22,8,256]{2,1,0:T(8,128)S(1)}, f32[22,8,256]{2,1,0:T(8,128)S(1)}, u32[]{:S(2)}, u32[]{:S(2)}) %collective-permute-start.17) | collective-permute-done | bytes 180256 | tf_op jit(solution)/shard_map/ppermute | solution.py:686
  125.6 2.1 shard_map.120
  127.7 15.6 %all_to_all.32.parts = f32[32,16,128]{2,1,0:T(8,128)S(1)} all-to-all(f32[32,16,128]{2,1,0:T(8,128)S(1)} %get-tuple-element.77), channel_id=1, replica_groups=mesh['gx'=4,'gy_0'=4,'gy_1'=2,'gz'=8] {'gx','gy_0','gy_1'}, dimensions={0} | all-to-all | bytes 524288 | tf_op jit(solution)/shard_map/all_to_all | solution.py:709
  143.3 5.0 %shard_map.121 = f32[8,8,128]{2,1,0:T(8,128)S(1)} custom-call(s32[9]{0:T(128)S(1)} %pad_add_fusion.sc, f32[32,16,128]{2,1,0:T(8,128)S(1)} %all_to_all.32.parts, f32[20,32,128]{2,1,0:T(8,128)S(1)} %get-tuple-element.53.ax1, f32[20,32,128]{2,1,0:T(8,128)S(1)} %get-tuple-element.54.ay1, f32[20,32,128]{2,1,0:T(8,128)S(1)} %get-tuple-element.55.az1, ...), custom_call_target="tpu_custom_call" | custom-call | tf_op jit(solution)/shard_map/pallas_call | solution.py:35
  148.4 3.0 %collective-permute-start.18 = (f32[8,8,128]{2,1,0:T(8,128)S(1)}, f32[8,8,128]{2,1,0:T(8,128)S(1)}, u32[]{:S(2)}, u32[]{:S(2)}) collective-permute-start(f32[8,8,128]{2,1,0:T(8,128)S(1)} %shard_map.121), channel_id=1, source_target_pairs={{1,0},{2,1},{3,2},{4,3},{5,4},{6,5},{7,6},{0,7},{9,8},{10,9},{11,1... | collective-permute-start | bytes 98312 | tf_op jit(solution)/shard_map/ppermute | solution.py:686
  151.4 1.2 collective-permute-done.19
  152.6 0.9 collective-permute-start.20
  153.5 1.9 collective-permute-start.21
  155.4 1.6 collective-permute-done.20
  157.0 2.2 %collective-permute-start.23 = (f32[22,8,256]{2,1,0:T(8,128)S(1)}, f32[22,8,256]{2,1,0:T(8,128)S(1)}, u32[]{:S(2)}, u32[]{:S(2)}) collective-permute-start(f32[22,8,256]{2,1,0:T(8,128)S(1)} %pad_maximum_fusion.5), channel_id=1, source_target_pairs={{8,0},{16,8},{24,16},{32,24},{40,32},{48,40},{56,48},{0,56},{9,1},... | collective-permute-start | bytes 540680 | tf_op jit(solution)/shard_map/ppermute | solution.py:686
  159.2 0.4 collective-permute-start.22
  159.6 3.2 %collective-permute-done.23 = f32[22,8,256]{2,1,0:T(8,128)S(1)} collective-permute-done((f32[22,8,256]{2,1,0:T(8,128)S(1)}, f32[22,8,256]{2,1,0:T(8,128)S(1)}, u32[]{:S(2)}, u32[]{:S(2)}) %collective-permute-start.23) | collective-permute-done | bytes 180256 | tf_op jit(solution)/shard_map/ppermute | solution.py:686
  162.8 3.1 %shard_map.122 = (f32[22,24,256]{2,1,0:T(8,128)S(1)}, f32[22,24,256]{2,1,0:T(8,128)S(1)}, f32[32,16,128]{2,1,0:T(8,128)S(1)}) custom-call(f32[22,24,256]{2,1,0:T(8,128)S(1)} %pad_maximum_fusion.1.b.s, f32[22,24,256]{2,1,0:T(8,128)S(1)} %pad_maximum_fusion.2.p, f32[22,24,256]{2,1,0:T(8,128)S(1)} %get-tuple-element.64.ax, ...), custom_call_target="tpu_custom_call" | custom-call | tf_op jit(solution)/shard_map/pallas_call | solution.py:35
  165.9 15.9 %all_to_all.33.parts = f32[32,16,128]{2,1,0:T(8,128)S(1)} all-to-all(f32[32,16,128]{2,1,0:T(8,128)S(1)} %get-tuple-element.79), channel_id=1, replica_groups=mesh['gx'=4,'gy_0'=4,'gy_1'=2,'gz'=8] {'gx','gy_0','gy_1'}, dimensions={0} | all-to-all | bytes 524288 | tf_op jit(solution)/shard_map/all_to_all | solution.py:709
  181.8 5.1 %shard_map.123.near = f32[10,24,256]{2,1,0:T(8,128)S(1)} custom-call(s32[9]{0:T(128)S(1)} %pad_add_fusion.sc, f32[32,16,128]{2,1,0:T(8,128)S(1)} %all_to_all.33.parts, f32[20,32,128]{2,1,0:T(8,128)S(1)} %get-tuple-element.53.ax1, f32[20,32,128]{2,1,0:T(8,128)S(1)} %get-tuple-element.54.ay1, f32[20,32,128]{2,1,0:T(8,128)S(1)} %get-tuple-element.55.az1, ...), custom_call_target="tpu_custom_call" | custom-call | tf_op jit(solution)/shard_map/pallas_call | solution.py:35
  187.0 5.2 %shard_map.124 = f32[32,16,128]{2,1,0:T(8,128)S(1)} custom-call(s32[9]{0:T(128)S(1)} %pad_add_fusion.sc, f32[10,24,256]{2,1,0:T(8,128)S(1)} %shard_map.123.near, f32[3,8,8,128]{3,2,1,0:T(8,128)S(1)} %get-tuple-element.82.misfit, bf16[16,8,8,128]{3,2,1,0:T(8,128)(2,1)S(1)} %copy-done.1, f32[8,512,128]{2,1,0:T(8,128)S(1)} %get-tuple-element.83.slope, ...), custom_call_target="tpu_custom_call" | custom-call | tf_op jit(solution)/shard_map/pallas_call | solution.py:35
  192.2 12.4 %all_to_all.34.parts = f32[32,16,128]{2,1,0:T(8,128)S(1)} all-to-all(f32[32,16,128]{2,1,0:T(8,128)S(1)} %shard_map.124), channel_id=1, replica_groups=mesh['gx'=4,'gy_0'=4,'gy_1'=2,'gz'=8] {'gx','gy_0','gy_1'}, dimensions={0} | all-to-all | bytes 524288 | tf_op jit(solution)/shard_map/all_to_all | solution.py:709
  204.7 11.6 %all_to_all.35.parts = f32[8,16,128]{2,1,0:T(8,128)S(1)} all-to-all(f32[8,16,128]{2,1,0:T(8,128)S(1)} %shard_map.125), channel_id=1, replica_groups=mesh['gx'=4,'gy_0'=4,'gy_1'=2,'gz'=8] {'gz'}, dimensions={0} | all-to-all | bytes 131072 | tf_op jit(solution)/shard_map/all_to_all | solution.py:709
  216.3 0.7 shard_map.126
  (53 shorter events, 0.6 us)
Async XLA Ops:
  1.4 1.0 copy-start
  2.3 0.9 copy-start.2
  3.2 0.9 copy-start.4
  4.1 0.8 copy-start.5
  4.9 0.7 copy-start.6
  5.6 0.7 copy-start.7
  6.2 0.7 copy-start.9
  11.7 7.9 %collective-permute-start.1 = (f32[19,8,128]{2,1,0:T(8,128)S(1)}, f32[19,8,128]{2,1,0:T(8,128)S(1)}, u32[]{:S(2)}, u32[]{:S(2)}) collective-permute-start(f32[19,8,128]{2,1,0:T(8,128)S(1)} %get-tuple-element.46.own), channel_id=1, source_target_pairs={{1,0},{2,1},{3,2},{4,3},{5,4},{6,5},{7,6},{0,7},{9,8},{10,9},{11,1... | collective-permute-start | bytes 233480 | tf_op jit(solution)/shard_map/ppermute | solution.py:686
  18.2 4.5 %collective-permute-start = (f32[19,8,128]{2,1,0:T(8,128)S(1)}, f32[19,8,128]{2,1,0:T(8,128)S(1)}, u32[]{:S(2)}, u32[]{:S(2)}) collective-permute-start(f32[19,8,128]{2,1,0:T(8,128)S(1)} %get-tuple-element.46.own), channel_id=1, source_target_pairs={{0,1},{1,2},{2,3},{3,4},{4,5},{5,6},{6,7},{7,0},{8,9},{9,10},{10,1... | collective-permute-start | bytes 233480 | tf_op jit(solution)/shard_map/ppermute | solution.py:686
  23.3 5.3 %collective-permute-start.2 = (f32[17,8,256]{2,1,0:T(8,128)S(1)}, f32[17,8,256]{2,1,0:T(8,128)S(1)}, u32[]{:S(2)}, u32[]{:S(2)}) collective-permute-start(f32[17,8,256]{2,1,0:T(8,128)S(1)} %get-tuple-element.49), channel_id=1, source_target_pairs={{0,64},{64,128},{128,192},{192,0},{1,65},{65,129},{129,193},{193,1... | collective-permute-start | bytes 417800 | tf_op jit(solution)/shard_map/ppermute | solution.py:686
  24.7 3.7 %collective-permute-start.3 = (f32[15,8,256]{2,1,0:T(8,128)S(1)}, f32[15,8,256]{2,1,0:T(8,128)S(1)}, u32[]{:S(2)}, u32[]{:S(2)}) collective-permute-start(f32[15,8,256]{2,1,0:T(8,128)S(1)} %get-tuple-element.50), channel_id=1, source_target_pairs={{64,0},{128,64},{192,128},{0,192},{65,1},{129,65},{193,129},{1,193... | collective-permute-start | bytes 368648 | tf_op jit(solution)/shard_map/ppermute | solution.py:686
  29.1 10.3 %collective-permute-start.5 = (f32[48,8,256]{2,1,0:T(8,128)S(1)}, f32[48,8,256]{2,1,0:T(8,128)S(1)}, u32[]{:S(2)}, u32[]{:S(2)}) collective-permute-start(f32[48,8,256]{2,1,0:T(8,128)S(1)} %shard_map.113.own), channel_id=1, source_target_pairs={{8,0},{16,8},{24,16},{32,24},{40,32},{48,40},{56,48},{0,56},{9,1},... | collective-permute-start | bytes 1179656 | tf_op jit(solution)/shard_map/ppermute | solution.py:686
  32.5 6.9 %collective-permute-start.4 = (f32[48,8,256]{2,1,0:T(8,128)S(1)}, f32[48,8,256]{2,1,0:T(8,128)S(1)}, u32[]{:S(2)}, u32[]{:S(2)}) collective-permute-start(f32[48,8,256]{2,1,0:T(8,128)S(1)} %shard_map.113.own), channel_id=1, source_target_pairs={{0,8},{8,16},{16,24},{24,32},{32,40},{40,48},{48,56},{56,0},{1,9},... | collective-permute-start | bytes 1179656 | tf_op jit(solution)/shard_map/ppermute | solution.py:686
  70.6 4.1 %collective-permute-start.7 = (f32[8,8,128]{2,1,0:T(8,128)S(1)}, f32[8,8,128]{2,1,0:T(8,128)S(1)}, u32[]{:S(2)}, u32[]{:S(2)}) collective-permute-start(f32[8,8,128]{2,1,0:T(8,128)S(1)} %shard_map.116), channel_id=1, source_target_pairs={{0,1},{1,2},{2,3},{3,4},{4,5},{5,6},{6,7},{7,0},{8,9},{9,10},{10,1... | collective-permute-start | bytes 98312 | tf_op jit(solution)/shard_map/ppermute | solution.py:686
  70.7 4.0 %collective-permute-start.6 = (f32[8,8,128]{2,1,0:T(8,128)S(1)}, f32[8,8,128]{2,1,0:T(8,128)S(1)}, u32[]{:S(2)}, u32[]{:S(2)}) collective-permute-start(f32[8,8,128]{2,1,0:T(8,128)S(1)} %shard_map.116), channel_id=1, source_target_pairs={{1,0},{2,1},{3,2},{4,3},{5,4},{6,5},{7,6},{0,7},{9,8},{10,9},{11,1... | collective-permute-start | bytes 98312 | tf_op jit(solution)/shard_map/ppermute | solution.py:686
  74.7 4.3 %collective-permute-start.8 = (f32[7,8,256]{2,1,0:T(8,128)S(1)}, f32[7,8,256]{2,1,0:T(8,128)S(1)}, u32[]{:S(2)}, u32[]{:S(2)}) collective-permute-start(f32[7,8,256]{2,1,0:T(8,128)S(1)} %get-tuple-element.92), channel_id=1, source_target_pairs={{0,64},{64,128},{128,192},{192,0},{1,65},{65,129},{129,193},{193,1... | collective-permute-start | bytes 172040 | tf_op jit(solution)/shard_map/ppermute | solution.py:686
  75.7 3.4 %collective-permute-start.9 = (f32[7,8,256]{2,1,0:T(8,128)S(1)}, f32[7,8,256]{2,1,0:T(8,128)S(1)}, u32[]{:S(2)}, u32[]{:S(2)}) collective-permute-start(f32[7,8,256]{2,1,0:T(8,128)S(1)} %get-tuple-element.93), channel_id=1, source_target_pairs={{64,0},{128,64},{192,128},{0,192},{65,1},{129,65},{193,129},{1,193... | collective-permute-start | bytes 172040 | tf_op jit(solution)/shard_map/ppermute | solution.py:686
  79.1 6.1 %collective-permute-start.11 = (f32[22,8,256]{2,1,0:T(8,128)S(1)}, f32[22,8,256]{2,1,0:T(8,128)S(1)}, u32[]{:S(2)}, u32[]{:S(2)}) collective-permute-start(f32[22,8,256]{2,1,0:T(8,128)S(1)} %pad_maximum_fusion.3), channel_id=1, source_target_pairs={{8,0},{16,8},{24,16},{32,24},{40,32},{48,40},{56,48},{0,56},{9,1},... | collective-permute-start | bytes 540680 | tf_op jit(solution)/shard_map/ppermute | solution.py:686
  81.8 3.4 %collective-permute-start.10 = (f32[22,8,256]{2,1,0:T(8,128)S(1)}, f32[22,8,256]{2,1,0:T(8,128)S(1)}, u32[]{:S(2)}, u32[]{:S(2)}) collective-permute-start(f32[22,8,256]{2,1,0:T(8,128)S(1)} %pad_maximum_fusion.3), channel_id=1, source_target_pairs={{0,8},{8,16},{16,24},{24,32},{32,40},{40,48},{48,56},{56,0},{1,9},... | collective-permute-start | bytes 540680 | tf_op jit(solution)/shard_map/ppermute | solution.py:686
  104.4 5.2 %copy-start.3 = (f32[3,8,8,128]{3,2,1,0:T(8,128)S(1)}, f32[3,8,8,128]{3,2,1,0:T(8,128)}, u32[]{:S(2)}) copy-start(f32[3,8,8,128]{3,2,1,0:T(8,128)} %target.1) | copy-start | bytes 294916
  110.9 4.6 %collective-permute-start.13 = (f32[8,8,128]{2,1,0:T(8,128)S(1)}, f32[8,8,128]{2,1,0:T(8,128)S(1)}, u32[]{:S(2)}, u32[]{:S(2)}) collective-permute-start(f32[8,8,128]{2,1,0:T(8,128)S(1)} %get-tuple-element.76), channel_id=1, source_target_pairs={{0,1},{1,2},{2,3},{3,4},{4,5},{5,6},{6,7},{7,0},{8,9},{9,10},{10,1... | collective-permute-start | bytes 98312 | tf_op jit(solution)/shard_map/ppermute | solution.py:686
  110.9 4.6 %collective-permute-start.12 = (f32[8,8,128]{2,1,0:T(8,128)S(1)}, f32[8,8,128]{2,1,0:T(8,128)S(1)}, u32[]{:S(2)}, u32[]{:S(2)}) collective-permute-start(f32[8,8,128]{2,1,0:T(8,128)S(1)} %get-tuple-element.76), channel_id=1, source_target_pairs={{1,0},{2,1},{3,2},{4,3},{5,4},{6,5},{7,6},{0,7},{9,8},{10,9},{11,1... | collective-permute-start | bytes 98312 | tf_op jit(solution)/shard_map/ppermute | solution.py:686
  115.4 4.3 %collective-permute-start.14 = (f32[7,8,256]{2,1,0:T(8,128)S(1)}, f32[7,8,256]{2,1,0:T(8,128)S(1)}, u32[]{:S(2)}, u32[]{:S(2)}) collective-permute-start(f32[7,8,256]{2,1,0:T(8,128)S(1)} %get-tuple-element.90), channel_id=1, source_target_pairs={{0,64},{64,128},{128,192},{192,0},{1,65},{65,129},{129,193},{193,1... | collective-permute-start | bytes 172040 | tf_op jit(solution)/shard_map/ppermute | solution.py:686
  116.0 3.7 %collective-permute-start.15 = (f32[7,8,256]{2,1,0:T(8,128)S(1)}, f32[7,8,256]{2,1,0:T(8,128)S(1)}, u32[]{:S(2)}, u32[]{:S(2)}) collective-permute-start(f32[7,8,256]{2,1,0:T(8,128)S(1)} %get-tuple-element.91), channel_id=1, source_target_pairs={{64,0},{128,64},{192,128},{0,192},{65,1},{129,65},{193,129},{1,193... | collective-permute-start | bytes 172040 | tf_op jit(solution)/shard_map/ppermute | solution.py:686
  119.8 5.7 %collective-permute-start.17 = (f32[22,8,256]{2,1,0:T(8,128)S(1)}, f32[22,8,256]{2,1,0:T(8,128)S(1)}, u32[]{:S(2)}, u32[]{:S(2)}) collective-permute-start(f32[22,8,256]{2,1,0:T(8,128)S(1)} %pad_maximum_fusion.4), channel_id=1, source_target_pairs={{8,0},{16,8},{24,16},{32,24},{40,32},{48,40},{56,48},{0,56},{9,1},... | collective-permute-start | bytes 540680 | tf_op jit(solution)/shard_map/ppermute | solution.py:686
  121.7 3.9 %collective-permute-start.16 = (f32[22,8,256]{2,1,0:T(8,128)S(1)}, f32[22,8,256]{2,1,0:T(8,128)S(1)}, u32[]{:S(2)}, u32[]{:S(2)}) collective-permute-start(f32[22,8,256]{2,1,0:T(8,128)S(1)} %pad_maximum_fusion.4), channel_id=1, source_target_pairs={{0,8},{8,16},{16,24},{24,32},{32,40},{40,48},{48,56},{56,0},{1,9},... | collective-permute-start | bytes 540680 | tf_op jit(solution)/shard_map/ppermute | solution.py:686
  148.3 4.3 %collective-permute-start.19 = (f32[8,8,128]{2,1,0:T(8,128)S(1)}, f32[8,8,128]{2,1,0:T(8,128)S(1)}, u32[]{:S(2)}, u32[]{:S(2)}) collective-permute-start(f32[8,8,128]{2,1,0:T(8,128)S(1)} %shard_map.121), channel_id=1, source_target_pairs={{0,1},{1,2},{2,3},{3,4},{4,5},{5,6},{6,7},{7,0},{8,9},{9,10},{10,1... | collective-permute-start | bytes 98312 | tf_op jit(solution)/shard_map/ppermute | solution.py:686
  148.4 4.2 %collective-permute-start.18 = (f32[8,8,128]{2,1,0:T(8,128)S(1)}, f32[8,8,128]{2,1,0:T(8,128)S(1)}, u32[]{:S(2)}, u32[]{:S(2)}) collective-permute-start(f32[8,8,128]{2,1,0:T(8,128)S(1)} %shard_map.121), channel_id=1, source_target_pairs={{1,0},{2,1},{3,2},{4,3},{5,4},{6,5},{7,6},{0,7},{9,8},{10,9},{11,1... | collective-permute-start | bytes 98312 | tf_op jit(solution)/shard_map/ppermute | solution.py:686
  152.6 4.3 %collective-permute-start.20 = (f32[7,8,256]{2,1,0:T(8,128)S(1)}, f32[7,8,256]{2,1,0:T(8,128)S(1)}, u32[]{:S(2)}, u32[]{:S(2)}) collective-permute-start(f32[7,8,256]{2,1,0:T(8,128)S(1)} %get-tuple-element.88), channel_id=1, source_target_pairs={{0,64},{64,128},{128,192},{192,0},{1,65},{65,129},{129,193},{193,1... | collective-permute-start | bytes 172040 | tf_op jit(solution)/shard_map/ppermute | solution.py:686
  153.5 3.5 %collective-permute-start.21 = (f32[7,8,256]{2,1,0:T(8,128)S(1)}, f32[7,8,256]{2,1,0:T(8,128)S(1)}, u32[]{:S(2)}, u32[]{:S(2)}) collective-permute-start(f32[7,8,256]{2,1,0:T(8,128)S(1)} %get-tuple-element.89), channel_id=1, source_target_pairs={{64,0},{128,64},{192,128},{0,192},{65,1},{129,65},{193,129},{1,193... | collective-permute-start | bytes 172040 | tf_op jit(solution)/shard_map/ppermute | solution.py:686
  157.0 5.7 %collective-permute-start.23 = (f32[22,8,256]{2,1,0:T(8,128)S(1)}, f32[22,8,256]{2,1,0:T(8,128)S(1)}, u32[]{:S(2)}, u32[]{:S(2)}) collective-permute-start(f32[22,8,256]{2,1,0:T(8,128)S(1)} %pad_maximum_fusion.5), channel_id=1, source_target_pairs={{8,0},{16,8},{24,16},{32,24},{40,32},{48,40},{56,48},{0,56},{9,1},... | collective-permute-start | bytes 540680 | tf_op jit(solution)/shard_map/ppermute | solution.py:686
  159.2 3.6 %collective-permute-start.22 = (f32[22,8,256]{2,1,0:T(8,128)S(1)}, f32[22,8,256]{2,1,0:T(8,128)S(1)}, u32[]{:S(2)}, u32[]{:S(2)}) collective-permute-start(f32[22,8,256]{2,1,0:T(8,128)S(1)} %pad_maximum_fusion.5), channel_id=1, source_target_pairs={{0,8},{8,16},{16,24},{24,32},{32,40},{40,48},{48,56},{56,0},{1,9},... | collective-permute-start | bytes 540680 | tf_op jit(solution)/shard_map/ppermute | solution.py:686
  181.8 5.2 %copy-start.1 = (bf16[16,8,8,128]{3,2,1,0:T(8,128)(2,1)S(1)}, bf16[16,8,8,128]{3,2,1,0:T(8,128)(2,1)}, u32[]{:S(2)}) copy-start(bf16[16,8,8,128]{3,2,1,0:T(8,128)(2,1)} %features.1) | copy-start | bytes 786436
  181.8 5.2 %copy-start.8 = (bf16[64,3]{0,1:T(4,128)(2,1)S(1)}, bf16[64,3]{0,1:T(4,128)(2,1)}, u32[]{:S(2)}) copy-start(bf16[64,3]{0,1:T(4,128)(2,1)} %param.14) | copy-start | bytes 1156

commit v3 on v2

--- a/solution.py
+++ b/solution.py
@@ -7,7 +7,7 @@
 from jax.sharding import PartitionSpec as P
 
 GY = ("gy_0", "gy_1")
-GRANT = 12
+CLOSURE = 4
 XY = ("gx", "gy_0", "gy_1")
 ALL = ("gx", "gy_0", "gy_1", "gz")
 F32 = jnp.float32
@@ -20,16 +20,16 @@
 REGION = (NXP, NYP, NZP)
 L1 = (20, 32, 128)
 L2 = (10, 16, 128)
-UNROLL = {24: 2, 32: 8, 16: 8}
+MOST = {24: 7, 32: 8, 16: 8}
 
 
 def shaped(shape, dtype=F32):
     return jax.ShapeDtypeStruct(shape, dtype)
 
 
-def call(body, outs, args, scratch=(), smem=(), left=(), grant=12):
+def call(body, outs, args, scratch=(), smem=()):
     spaces = [
-        pltpu.SMEM if i in smem else pltpu.HBM if i in left else pltpu.VMEM for i in range(len(args))
+        pltpu.SMEM if i in smem else pltpu.VMEM for i in range(len(args))
     ]
     specs = [pl.BlockSpec(memory_space=space) for space in spaces]
     return pl.pallas_call(
@@ -38,7 +38,7 @@
         in_specs=specs,
         out_specs=[pl.BlockSpec(memory_space=pltpu.VMEM)] * len(outs),
         scratch_shapes=list(scratch),
-        compiler_params=pltpu.CompilerParams(vmem_limit_bytes=grant << 20),
+        compiler_params=pltpu.CompilerParams(vmem_limit_bytes=12 << 20),
     )(*args)
 
 
@@ -66,6 +66,10 @@
     return (parts[2 * count :] + parts[count : 2 * count]) + parts[:count]
 
 
+def steps(count, rows):
+    return max(k for k in range(1, MOST[rows] + 1) if count % k == 0)
+
+
 def planes(lo, hi, body, unroll=2):
     def step(i, carry):
         body(i)
@@ -87,14 +91,14 @@
         v, total = around(src, ax, ay, az, i)
         dst[i] = 0.2 * v + w[i] * (s[i] + total)
 
-    planes(lo, hi, one, UNROLL[src.shape[1]])
+    planes(lo, hi, one, steps(hi - lo, src.shape[1]))
 
 
 def first_sweep(dst, s, w, lo, hi):
     def one(i):
         dst[i] = w[i] * s[i]
 
-    planes(lo, hi, one, UNROLL[s.shape[1]])
+    planes(lo, hi, one, steps(hi - lo, s.shape[1]))
 
 
 def face(here, there, weight, low, high):
@@ -204,7 +208,7 @@
         centre, total = around(p, ax, ay, az, i)
         s[i] = b[i] + total - d[i] * centre
 
-    planes(1, 21, one)
+    planes(1, 21, one, 5)
     presmooth(s, v, va, (ax, ay, az, w, d), rows, out)
 
 
@@ -376,47 +380,30 @@
 
 def closure_body(
     sc,
-    features_far,
-    velocity_far,
-    target_far,
-    density_far,
-    weight_in,
-    bias_in,
-    weight_out,
+    features,
+    fields,
+    weights,
     flux,
     slope,
     hidden,
     message,
     target_faces,
     marks,
-    features,
-    velocity,
-    target,
     kin,
     bias,
     kout,
-    sems,
 ):
-    copies = [
-        pltpu.make_async_copy(source, place, sems.at[k])
-        for k, (source, place) in enumerate(
-            (
-                (features_far, features),
-                (velocity_far, velocity),
-                (target_far, target),
-                (density_far, message.at[8:16]),
-            )
-        )
-    ]
-    for copy in copies:
-        copy.start()
+    velocity, target = fields.at[0:3], fields.at[3:6]
+    message[8:16] = fields[6]
+    weight_in = weights[0:16, :].astype(BF16)
+    weight_out = weights[24:27, :].astype(BF16)
     units = members(512, 64)
-    narrow = dot_across(units, weight_in[...]).astype(BF16)
+    narrow = dot_across(units, weight_in).astype(BF16)
     kin[...] = same_row(dot_across(narrow, members(128, 16)))
-    narrow = jnp.dot(members(24, 3), weight_out[...], preferred_element_type=F32).astype(BF16)
+    narrow = jnp.dot(members(24, 3), weight_out, preferred_element_type=F32).astype(BF16)
     kout[...] = same_row(dot_across(narrow, units))
     bias[...] = dot_across(
-        units.astype(F32), jnp.broadcast_to(bias_in[...], (128, 64)), HIGHEST
+        units.astype(F32), jnp.broadcast_to(weights[16:17, :], (128, 64)), HIGHEST
     )
     _, high = opens_of(sc)
     high_x = jnp.where(sc[0] == 3, high[0], F32(1.0))
@@ -426,9 +413,6 @@
     col = lax.broadcasted_iota(jnp.int32, (8, 128), 1)
     factor_y = jnp.where(row == 7, high_y, F32(1.0))
     factor_z = jnp.where(col == 127, high_z, F32(1.0))
-    for copy in copies:
-        copy.wait()
-
     def one(x):
         columns = features[:, x, :, :].astype(F32).reshape(128, 128).astype(BF16)
         before = jnp.dot(kin[...], columns, preferred_element_type=F32) + bias[...]
@@ -442,7 +426,7 @@
         flux[1, x] = (velocity[1, x] + shift[8:16]) * factor_y
         flux[2, x] = (velocity[2, x] + shift[16:24]) * factor_z
 
-    planes(0, 8, one, 1)
+    planes(0, 8, one, CLOSURE)
     zero = jnp.zeros((8, 128), F32)
     ends = zero
     for x in range(8):
@@ -552,8 +536,9 @@
     low_faces[1] = low[47, :, 0:128]
 
 
-def middle_body(sc, near, flux, target, from_x, low_y, from_z, ax, ay, az, new, misfit, out):
+def middle_body(sc, near, flux, fields, from_x, low_y, from_z, ax, ay, az, new, misfit, out):
     scale = F32(1.0 / CELLS)
+    target = fields.at[3:6]
     inner = [jnp.where(sc[d] > 0, F32(1.0), F32(0.0)) for d in range(3)]
 
     def rises(i):
@@ -601,9 +586,9 @@
 
 
 def gradient_body(
-    sc, near, misfit, features, slope, hidden, weight_out, out, acc_in, acc_bias, acc_out, kback
+    sc, near, misfit, features, slope, hidden, weights, out, acc_in, acc_bias, acc_out, kback
 ):
-    narrow = dot_across(members(512, 64), weight_out[...]).astype(BF16)
+    narrow = dot_across(members(512, 64), weights[24:27, :].astype(BF16)).astype(BF16)
     kback[...] = same_row(dot_across(narrow, members(24, 3)))
     _, high = opens_of(sc)
     high_x = jnp.where(sc[0] == 3, high[0], F32(1.0))
@@ -640,7 +625,7 @@
         )
         acc_out[...] += lax.dot_general(grads, hidden[x], across, preferred_element_type=F32)
 
-    planes(0, 8, one, 1)
+    planes(0, 8, one, CLOSURE)
 
     def same(count):
         r = lax.broadcasted_iota(jnp.int32, (count, 512), 0)
@@ -713,7 +698,15 @@
     place = jnp.stack([lax.axis_index("gx"), lax.axis_index(GY), lax.axis_index("gz")])
     sc = jnp.concatenate([place.astype(jnp.int32), open_faces])
     block = (8, 8, 128)
-    narrow_out = weight_out.T
+    weights = jnp.concatenate(
+        [
+            weight_in.astype(F32),
+            jnp.broadcast_to(bias_in[None], (8, 64)),
+            jnp.pad(weight_out.T.astype(F32), ((0, 5), (0, 0))),
+        ],
+        axis=0,
+    )
+    fields = jnp.concatenate([velocity, target, density[None]], axis=0)
     flux, slope, hidden, message, target_faces, marks = call(
         closure_body,
         [
@@ -724,19 +717,13 @@
             shaped((2, 8, 128)),
             shaped((8, 256)),
         ],
-        (sc, features, velocity, target, density, weight_in, bias_in[None], narrow_out),
+        (sc, features, fields, weights),
         [
-            pltpu.VMEM((16, *block), BF16),
-            pltpu.VMEM((3, *block), F32),
-            pltpu.VMEM((3, *block), F32),
             pltpu.VMEM((512, 128), BF16),
             pltpu.VMEM((512, 128), F32),
             pltpu.VMEM((24, 512), BF16),
-            pltpu.SemaphoreType.DMA((4,)),
         ],
         smem=(0,),
-        left=(1, 2, 3, 4),
-        grant=GRANT,
     )
     from_z, after = ring(message, message, "gz")
     wide, up, down = call(
@@ -794,7 +781,7 @@
     new_velocity, misfit, grad_pressure = call(
         middle_body,
         [shaped((3, *block)), shaped((3, *block)), shaped(block)],
-        (sc, near, flux, target, from_x, low_y, from_z, ax, ay, az),
+        (sc, near, flux, fields, from_x, low_y, from_z, ax, ay, az),
         smem=(0,),
     )
     b = exchanged(grad_pressure, marks)
@@ -803,7 +790,7 @@
     (packed,) = call(
         gradient_body,
         [to_plane],
-        (sc, near, misfit, features, slope, hidden, narrow_out),
+        (sc, near, misfit, features, slope, hidden, weights),
         [
             pltpu.VMEM((128, 512), F32),
             pltpu.VMEM((512, 128), F32),

time: 218 us -> 208 us (0.954)
  Pallas kernels: 49.5 us -> 41.3 us
  local copies, waits for them, and re-layouts: 5.53 us -> 1.62 us
  other arithmetic: 1.1 us -> 3.46 us
    pallas_call x16, Pallas kernels: 49.5 us -> 41.3 us  [call(): pl.pallas_call(body, out_shape=outs, in_specs=specs, out_specs=[pl.BlockS...]
    unnamed x20 -> x4, local copies, waits for them, and re-layouts: 5.52 us -> 0.95 us
where the time goes in v3:
time: 208 us; the launch traced here: 207 us
  blocking collectives  90 us (43%)
  Pallas kernels  41.3 us (20%)
  starting transfers between devices  38.7 us (19%)
  waiting for transfers between devices  31.1 us (15%)
  other arithmetic  3.46 us (2%)
    all_to_all x6, blocking collectives, sent_to_all(): return lax.all_to_all(copies, axis, split_axis=0, concat_axis=0, tiled=True)  90 us
    pallas_call x16, Pallas kernels, call(): pl.pallas_call(body, out_shape=outs, in_specs=specs, out_specs=[pl.BlockS...  41.3 us
    ppermute x12, starting transfers between devices, ring(): lax.ppermute(down, axis, [(b, a) for a, b in ups])  32.6 us
    ppermute x12, waiting for transfers between devices, ring(): lax.ppermute(down, axis, [(b, a) for a, b in ups])  19.2 us
    ppermute x12, waiting for transfers between devices, ring(): lax.ppermute(up, axis, ups)  12 us
    ppermute x12, starting transfers between devices, ring(): lax.ppermute(up, axis, ups)  6.05 us
  transfers between devices with their start and end apart: 24, of which 14 were waited for; matrix products, arithmetic and copies ran while one was open for 0% of the time, Pallas kernels for 0%

profile of v3, /device:TPU:1, one launch (start us, length us, event | category | flops | bytes accessed | tf_op | source)
XLA Modules:
  0.0 207.1 jit_solution(14655632079309301066)
XLA Ops:
  0.6 0.7 pad_convert_fusion
  1.3 0.7 convert_element_type.9
  2.0 0.7 broadcast_in_dim.10
  2.7 1.0 pad_maximum_fusion.3.fields
  3.7 0.7 pad_add_fusion.sc
  4.4 0.9 copy-done
  5.3 3.6 %shard_map.111 = (f32[3,8,8,128]{3,2,1,0:T(8,128)S(1)}, f32[8,512,128]{2,1,0:T(8,128)S(1)}, bf16[8,512,128]{2,1,0:T(8,128)(2,1)S(1)}, f32[19,8,128]{2,1,0:T(8,12...) custom-call(s32[9]{0:T(128)S(1)} %pad_add_fusion.sc, bf16[16,8,8,128]{3,2,1,0:T(8,128)(2,1)S(1)} %copy-done, ...), custom_call_target="tpu_custom_call" | custom-call | tf_op jit(solution)/shard_map/pallas_call | solution.py:35
  9.0 6.5 %collective-permute-start.1 = (f32[19,8,128]{2,1,0:T(8,128)S(1)}, f32[19,8,128]{2,1,0:T(8,128)S(1)}, u32[]{:S(2)}, u32[]{:S(2)}) collective-permute-start(f32[19,8,128]{2,1,0:T(8,128)S(1)} %get-tuple-element.46.own), channel_id=1, source_target_pairs={{1,0},{2,1},{3,2},{4,3},{5,4},{6,5},{7,6},{0,7},{9,8},{10,9},{11,1... | collective-permute-start | bytes 233480 | tf_op jit(solution)/shard_map/ppermute | solution.py:671
  15.4 1.4 collective-permute-done.1.after
  16.9 3.0 %collective-permute-done.before.from_z = f32[19,8,128]{2,1,0:T(8,128)S(1)} collective-permute-done((f32[19,8,128]{2,1,0:T(8,128)S(1)}, f32[19,8,128]{2,1,0:T(8,128)S(1)}, u32[]{:S(2)}, u32[]{:S(2)}) %collective-permute-start) | collective-permute-done | bytes 77856 | tf_op jit(solution)/shard_map/ppermute | solution.py:671
  19.9 0.6 shard_map.112
  20.5 1.4 collective-permute-start.2
  21.9 1.5 collective-permute-start.3
  23.4 2.2 %collective-permute-done.3.high = f32[15,8,256]{2,1,0:T(8,128)S(1)} collective-permute-done((f32[15,8,256]{2,1,0:T(8,128)S(1)}, f32[15,8,256]{2,1,0:T(8,128)S(1)}, u32[]{:S(2)}, u32[]{:S(2)}) %collective-permute-start.3) | collective-permute-done | bytes 122912 | tf_op jit(solution)/shard_map/ppermute | solution.py:671
  25.6 0.2 collective-permute-done.2.low.from_x
  25.8 0.6 shard_map.113.own
  26.4 3.4 %collective-permute-start.5 = (f32[48,8,256]{2,1,0:T(8,128)S(1)}, f32[48,8,256]{2,1,0:T(8,128)S(1)}, u32[]{:S(2)}, u32[]{:S(2)}) collective-permute-start(f32[48,8,256]{2,1,0:T(8,128)S(1)} %shard_map.113.own), channel_id=1, source_target_pairs={{8,0},{16,8},{24,16},{32,24},{40,32},{48,40},{56,48},{0,56},{9,1},... | collective-permute-start | bytes 1179656 | tf_op jit(solution)/shard_map/ppermute | solution.py:671
  29.7 1.1 collective-permute-start.4
  30.9 5.7 %collective-permute-done.5.high = f32[48,8,256]{2,1,0:T(8,128)S(1)} collective-permute-done((f32[48,8,256]{2,1,0:T(8,128)S(1)}, f32[48,8,256]{2,1,0:T(8,128)S(1)}, u32[]{:S(2)}, u32[]{:S(2)}) %collective-permute-start.5) | collective-permute-done | bytes 393248 | tf_op jit(solution)/shard_map/ppermute | solution.py:671
  36.6 4.1 %shard_map.114 = (f32[22,24,256]{2,1,0:T(8,128)S(1)}, f32[22,24,256]{2,1,0:T(8,128)S(1)}, f32[22,24,256]{2,1,0:T(8,128)S(1)}, f32[22,24,256]{2,1,0:T(8,128)S(1)}...) custom-call(s32[9]{0:T(128)S(1)} %pad_add_fusion.sc, ...), custom_call_target="tpu_custom_call" | custom-call | tf_op jit(solution)/shard_map/pallas_call | solution.py:35
  40.7 18.4 %all_to_all.30.parts = f32[32,32,128]{2,1,0:T(8,128)S(1)} all-to-all(f32[32,32,128]{2,1,0:T(8,128)S(1)} %get-tuple-element.52), channel_id=1, replica_groups=mesh['gx'=4,'gy_0'=4,'gy_1'=2,'gz'=8] {'gx','gy_0','gy_1'}, dimensions={0} | all-to-all | bytes 1048576 | tf_op jit(solution)/shard_map/all_to_all | solution.py:694
  59.1 3.1 %shard_map.115 = (f32[20,32,128]{2,1,0:T(8,128)S(1)}, f32[20,32,128]{2,1,0:T(8,128)S(1)}, f32[20,32,128]{2,1,0:T(8,128)S(1)}, f32[20,32,128]{2,1,0:T(8,128)S(1)}...) custom-call(s32[9]{0:T(128)S(1)} %pad_add_fusion.sc, ...), custom_call_target="tpu_custom_call" | custom-call | tf_op jit(solution)/shard_map/pallas_call | solution.py:35
  62.2 4.5 %shard_map.116 = f32[8,8,128]{2,1,0:T(8,128)S(1)} custom-call(s32[9]{0:T(128)S(1)} %pad_add_fusion.sc, f32[32,32,128]{2,1,0:T(8,128)S(1)} %all_to_all.30.parts, f32[20,32,128]{2,1,0:T(8,128)S(1)} %get-tuple-element.53.ax1, f32[20,32,128]{2,1,0:T(8,128)S(1)} %get-tuple-element.54.ay1, f32[20,32,128]{2,1,0:T(8,128)S(1)} %get-tuple-element.55.az1, ...), custom_call_target="tpu_custom_call" | custom-call | tf_op jit(solution)/shard_map/pallas_call | solution.py:35
  66.6 0.1 collective-permute-start.7
  66.7 2.7 %collective-permute-start.6 = (f32[8,8,128]{2,1,0:T(8,128)S(1)}, f32[8,8,128]{2,1,0:T(8,128)S(1)}, u32[]{:S(2)}, u32[]{:S(2)}) collective-permute-start(f32[8,8,128]{2,1,0:T(8,128)S(1)} %shard_map.116), channel_id=1, source_target_pairs={{1,0},{2,1},{3,2},{4,3},{5,4},{6,5},{7,6},{0,7},{9,8},{10,9},{11,1... | collective-permute-start | bytes 98312 | tf_op jit(solution)/shard_map/ppermute | solution.py:671
  69.4 1.3 collective-permute-done.7
  70.7 0.0 collective-permute-done.6
  70.7 1.0 collective-permute-start.8
  71.7 1.8 collective-permute-start.9
  73.5 1.6 collective-permute-done.8
  75.1 2.7 %collective-permute-start.11 = (f32[22,8,256]{2,1,0:T(8,128)S(1)}, f32[22,8,256]{2,1,0:T(8,128)S(1)}, u32[]{:S(2)}, u32[]{:S(2)}) collective-permute-start(f32[22,8,256]{2,1,0:T(8,128)S(1)} %pad_maximum_fusion.4), channel_id=1, source_target_pairs={{8,0},{16,8},{24,16},{32,24},{40,32},{48,40},{56,48},{0,56},{9,1},... | collective-permute-start | bytes 540680 | tf_op jit(solution)/shard_map/ppermute | solution.py:671
  77.8 0.2 collective-permute-start.10
  78.0 3.2 %collective-permute-done.11 = f32[22,8,256]{2,1,0:T(8,128)S(1)} collective-permute-done((f32[22,8,256]{2,1,0:T(8,128)S(1)}, f32[22,8,256]{2,1,0:T(8,128)S(1)}, u32[]{:S(2)}, u32[]{:S(2)}) %collective-permute-start.11) | collective-permute-done | bytes 180256 | tf_op jit(solution)/shard_map/ppermute | solution.py:671
  81.3 2.1 %shard_map.117 = (f32[22,24,256]{2,1,0:T(8,128)S(1)}, f32[22,24,256]{2,1,0:T(8,128)S(1)}, f32[32,16,128]{2,1,0:T(8,128)S(1)}) custom-call(f32[22,24,256]{2,1,0:T(8,128)S(1)} %get-tuple-element.51.s.b, f32[22,24,256]{2,1,0:T(8,128)S(1)} %pad_maximum_fusion.p, f32[22,24,256]{2,1,0:T(8,128)S(1)} %get-tuple-element.64.ax, ...), custom_call_target="tpu_custom_call" | custom-call | tf_op jit(solution)/shard_map/pallas_call | solution.py:35
  83.4 16.1 %all_to_all.31.parts = f32[32,16,128]{2,1,0:T(8,128)S(1)} all-to-all(f32[32,16,128]{2,1,0:T(8,128)S(1)} %get-tuple-element.70), channel_id=1, replica_groups=mesh['gx'=4,'gy_0'=4,'gy_1'=2,'gz'=8] {'gx','gy_0','gy_1'}, dimensions={0} | all-to-all | bytes 524288 | tf_op jit(solution)/shard_map/all_to_all | solution.py:694
  99.4 4.6 %shard_map.118.near = f32[10,24,256]{2,1,0:T(8,128)S(1)} custom-call(s32[9]{0:T(128)S(1)} %pad_add_fusion.sc, f32[32,16,128]{2,1,0:T(8,128)S(1)} %all_to_all.31.parts, f32[20,32,128]{2,1,0:T(8,128)S(1)} %get-tuple-element.53.ax1, f32[20,32,128]{2,1,0:T(8,128)S(1)} %get-tuple-element.54.ay1, f32[20,32,128]{2,1,0:T(8,128)S(1)} %get-tuple-element.55.az1, ...), custom_call_target="tpu_custom_call" | custom-call | tf_op jit(solution)/shard_map/pallas_call | solution.py:35
  104.1 1.3 shard_map.119
  105.4 2.9 %collective-permute-start.12 = (f32[8,8,128]{2,1,0:T(8,128)S(1)}, f32[8,8,128]{2,1,0:T(8,128)S(1)}, u32[]{:S(2)}, u32[]{:S(2)}) collective-permute-start(f32[8,8,128]{2,1,0:T(8,128)S(1)} %get-tuple-element.76), channel_id=1, source_target_pairs={{1,0},{2,1},{3,2},{4,3},{5,4},{6,5},{7,6},{0,7},{9,8},{10,9},{11,1... | collective-permute-start | bytes 98312 | tf_op jit(solution)/shard_map/ppermute | solution.py:671
  108.3 1.6 collective-permute-done.13
  110.0 0.6 collective-permute-start.14
  110.6 2.2 %collective-permute-start.15 = (f32[7,8,256]{2,1,0:T(8,128)S(1)}, f32[7,8,256]{2,1,0:T(8,128)S(1)}, u32[]{:S(2)}, u32[]{:S(2)}) collective-permute-start(f32[7,8,256]{2,1,0:T(8,128)S(1)} %get-tuple-element.91), channel_id=1, source_target_pairs={{64,0},{128,64},{192,128},{0,192},{65,1},{129,65},{193,129},{1,193... | collective-permute-start | bytes 172040 | tf_op jit(solution)/shard_map/ppermute | solution.py:671
  112.7 1.6 collective-permute-done.14
  114.3 1.9 collective-permute-start.17
  116.2 0.4 collective-permute-start.16
  116.6 3.5 %collective-permute-done.17 = f32[22,8,256]{2,1,0:T(8,128)S(1)} collective-permute-done((f32[22,8,256]{2,1,0:T(8,128)S(1)}, f32[22,8,256]{2,1,0:T(8,128)S(1)}, u32[]{:S(2)}, u32[]{:S(2)}) %collective-permute-start.17) | collective-permute-done | bytes 180256 | tf_op jit(solution)/shard_map/ppermute | solution.py:671
  120.2 1.4 shard_map.120
  121.6 15.6 %all_to_all.32.parts = f32[32,16,128]{2,1,0:T(8,128)S(1)} all-to-all(f32[32,16,128]{2,1,0:T(8,128)S(1)} %get-tuple-element.77), channel_id=1, replica_groups=mesh['gx'=4,'gy_0'=4,'gy_1'=2,'gz'=8] {'gx','gy_0','gy_1'}, dimensions={0} | all-to-all | bytes 524288 | tf_op jit(solution)/shard_map/all_to_all | solution.py:694
  137.2 4.5 %shard_map.121 = f32[8,8,128]{2,1,0:T(8,128)S(1)} custom-call(s32[9]{0:T(128)S(1)} %pad_add_fusion.sc, f32[32,16,128]{2,1,0:T(8,128)S(1)} %all_to_all.32.parts, f32[20,32,128]{2,1,0:T(8,128)S(1)} %get-tuple-element.53.ax1, f32[20,32,128]{2,1,0:T(8,128)S(1)} %get-tuple-element.54.ay1, f32[20,32,128]{2,1,0:T(8,128)S(1)} %get-tuple-element.55.az1, ...), custom_call_target="tpu_custom_call" | custom-call | tf_op jit(solution)/shard_map/pallas_call | solution.py:35
  141.7 0.1 collective-permute-start.19
  141.8 3.0 %collective-permute-start.18 = (f32[8,8,128]{2,1,0:T(8,128)S(1)}, f32[8,8,128]{2,1,0:T(8,128)S(1)}, u32[]{:S(2)}, u32[]{:S(2)}) collective-permute-start(f32[8,8,128]{2,1,0:T(8,128)S(1)} %shard_map.121), channel_id=1, source_target_pairs={{1,0},{2,1},{3,2},{4,3},{5,4},{6,5},{7,6},{0,7},{9,8},{10,9},{11,1... | collective-permute-start | bytes 98312 | tf_op jit(solution)/shard_map/ppermute | solution.py:671
  144.8 1.2 collective-permute-done.19
  146.0 0.9 collective-permute-start.20
  146.9 1.9 collective-permute-start.21
  148.8 1.6 collective-permute-done.20
  150.4 2.2 %collective-permute-start.23 = (f32[22,8,256]{2,1,0:T(8,128)S(1)}, f32[22,8,256]{2,1,0:T(8,128)S(1)}, u32[]{:S(2)}, u32[]{:S(2)}) collective-permute-start(f32[22,8,256]{2,1,0:T(8,128)S(1)} %pad_maximum_fusion.6), channel_id=1, source_target_pairs={{8,0},{16,8},{24,16},{32,24},{40,32},{48,40},{56,48},{0,56},{9,1},... | collective-permute-start | bytes 540680 | tf_op jit(solution)/shard_map/ppermute | solution.py:671
  152.6 0.4 collective-permute-start.22
  153.0 3.2 %collective-permute-done.23 = f32[22,8,256]{2,1,0:T(8,128)S(1)} collective-permute-done((f32[22,8,256]{2,1,0:T(8,128)S(1)}, f32[22,8,256]{2,1,0:T(8,128)S(1)}, u32[]{:S(2)}, u32[]{:S(2)}) %collective-permute-start.23) | collective-permute-done | bytes 180256 | tf_op jit(solution)/shard_map/ppermute | solution.py:671
  156.2 2.1 %shard_map.122 = (f32[22,24,256]{2,1,0:T(8,128)S(1)}, f32[22,24,256]{2,1,0:T(8,128)S(1)}, f32[32,16,128]{2,1,0:T(8,128)S(1)}) custom-call(f32[22,24,256]{2,1,0:T(8,128)S(1)} %pad_maximum_fusion.1.b.s, f32[22,24,256]{2,1,0:T(8,128)S(1)} %pad_maximum_fusion.2.p, f32[22,24,256]{2,1,0:T(8,128)S(1)} %get-tuple-element.64.ax, ...), custom_call_target="tpu_custom_call" | custom-call | tf_op jit(solution)/shard_map/pallas_call | solution.py:35
  158.3 15.9 %all_to_all.33.parts = f32[32,16,128]{2,1,0:T(8,128)S(1)} all-to-all(f32[32,16,128]{2,1,0:T(8,128)S(1)} %get-tuple-element.79), channel_id=1, replica_groups=mesh['gx'=4,'gy_0'=4,'gy_1'=2,'gz'=8] {'gx','gy_0','gy_1'}, dimensions={0} | all-to-all | bytes 524288 | tf_op jit(solution)/shard_map/all_to_all | solution.py:694
  174.2 4.6 %shard_map.123.near = f32[10,24,256]{2,1,0:T(8,128)S(1)} custom-call(s32[9]{0:T(128)S(1)} %pad_add_fusion.sc, f32[32,16,128]{2,1,0:T(8,128)S(1)} %all_to_all.33.parts, f32[20,32,128]{2,1,0:T(8,128)S(1)} %get-tuple-element.53.ax1, f32[20,32,128]{2,1,0:T(8,128)S(1)} %get-tuple-element.54.ay1, f32[20,32,128]{2,1,0:T(8,128)S(1)} %get-tuple-element.55.az1, ...), custom_call_target="tpu_custom_call" | custom-call | tf_op jit(solution)/shard_map/pallas_call | solution.py:35
  178.9 3.5 %shard_map.124 = f32[32,16,128]{2,1,0:T(8,128)S(1)} custom-call(s32[9]{0:T(128)S(1)} %pad_add_fusion.sc, f32[10,24,256]{2,1,0:T(8,128)S(1)} %shard_map.123.near, f32[3,8,8,128]{3,2,1,0:T(8,128)S(1)} %get-tuple-element.82.misfit, bf16[16,8,8,128]{3,2,1,0:T(8,128)(2,1)S(1)} %copy-done.1, f32[8,512,128]{2,1,0:T(8,128)S(1)} %get-tuple-element.83.slope, ...), custom_call_target="tpu_custom_call" | custom-call | tf_op jit(solution)/shard_map/pallas_call | solution.py:35
  182.4 12.4 %all_to_all.34.parts = f32[32,16,128]{2,1,0:T(8,128)S(1)} all-to-all(f32[32,16,128]{2,1,0:T(8,128)S(1)} %shard_map.124), channel_id=1, replica_groups=mesh['gx'=4,'gy_0'=4,'gy_1'=2,'gz'=8] {'gx','gy_0','gy_1'}, dimensions={0} | all-to-all | bytes 524288 | tf_op jit(solution)/shard_map/all_to_all | solution.py:694
  194.8 11.6 %all_to_all.35.parts = f32[8,16,128]{2,1,0:T(8,128)S(1)} all-to-all(f32[8,16,128]{2,1,0:T(8,128)S(1)} %shard_map.125), channel_id=1, replica_groups=mesh['gx'=4,'gy_0'=4,'gy_1'=2,'gz'=8] {'gz'}, dimensions={0} | all-to-all | bytes 131072 | tf_op jit(solution)/shard_map/all_to_all | solution.py:694
  206.5 0.7 shard_map.126
  (42 shorter events, 0.5 us)
Async XLA Ops:
  4.4 1.0 copy-start
  9.0 7.9 %collective-permute-start.1 = (f32[19,8,128]{2,1,0:T(8,128)S(1)}, f32[19,8,128]{2,1,0:T(8,128)S(1)}, u32[]{:S(2)}, u32[]{:S(2)}) collective-permute-start(f32[19,8,128]{2,1,0:T(8,128)S(1)} %get-tuple-element.46.own), channel_id=1, source_target_pairs={{1,0},{2,1},{3,2},{4,3},{5,4},{6,5},{7,6},{0,7},{9,8},{10,9},{11,1... | collective-permute-start | bytes 233480 | tf_op jit(solution)/shard_map/ppermute | solution.py:671
  15.4 4.5 %collective-permute-start = (f32[19,8,128]{2,1,0:T(8,128)S(1)}, f32[19,8,128]{2,1,0:T(8,128)S(1)}, u32[]{:S(2)}, u32[]{:S(2)}) collective-permute-start(f32[19,8,128]{2,1,0:T(8,128)S(1)} %get-tuple-element.46.own), channel_id=1, source_target_pairs={{0,1},{1,2},{2,3},{3,4},{4,5},{5,6},{6,7},{7,0},{8,9},{9,10},{10,1... | collective-permute-start | bytes 233480 | tf_op jit(solution)/shard_map/ppermute | solution.py:671
  20.5 5.3 %collective-permute-start.2 = (f32[17,8,256]{2,1,0:T(8,128)S(1)}, f32[17,8,256]{2,1,0:T(8,128)S(1)}, u32[]{:S(2)}, u32[]{:S(2)}) collective-permute-start(f32[17,8,256]{2,1,0:T(8,128)S(1)} %get-tuple-element.49), channel_id=1, source_target_pairs={{0,64},{64,128},{128,192},{192,0},{1,65},{65,129},{129,193},{193,1... | collective-permute-start | bytes 417800 | tf_op jit(solution)/shard_map/ppermute | solution.py:671
  21.9 3.7 %collective-permute-start.3 = (f32[15,8,256]{2,1,0:T(8,128)S(1)}, f32[15,8,256]{2,1,0:T(8,128)S(1)}, u32[]{:S(2)}, u32[]{:S(2)}) collective-permute-start(f32[15,8,256]{2,1,0:T(8,128)S(1)} %get-tuple-element.50), channel_id=1, source_target_pairs={{64,0},{128,64},{192,128},{0,192},{65,1},{129,65},{193,129},{1,193... | collective-permute-start | bytes 368648 | tf_op jit(solution)/shard_map/ppermute | solution.py:671
  26.4 10.2 %collective-permute-start.5 = (f32[48,8,256]{2,1,0:T(8,128)S(1)}, f32[48,8,256]{2,1,0:T(8,128)S(1)}, u32[]{:S(2)}, u32[]{:S(2)}) collective-permute-start(f32[48,8,256]{2,1,0:T(8,128)S(1)} %shard_map.113.own), channel_id=1, source_target_pairs={{8,0},{16,8},{24,16},{32,24},{40,32},{48,40},{56,48},{0,56},{9,1},... | collective-permute-start | bytes 1179656 | tf_op jit(solution)/shard_map/ppermute | solution.py:671
  29.7 6.9 %collective-permute-start.4 = (f32[48,8,256]{2,1,0:T(8,128)S(1)}, f32[48,8,256]{2,1,0:T(8,128)S(1)}, u32[]{:S(2)}, u32[]{:S(2)}) collective-permute-start(f32[48,8,256]{2,1,0:T(8,128)S(1)} %shard_map.113.own), channel_id=1, source_target_pairs={{0,8},{8,16},{16,24},{24,32},{32,40},{40,48},{48,56},{56,0},{1,9},... | collective-permute-start | bytes 1179656 | tf_op jit(solution)/shard_map/ppermute | solution.py:671
  66.6 4.1 %collective-permute-start.7 = (f32[8,8,128]{2,1,0:T(8,128)S(1)}, f32[8,8,128]{2,1,0:T(8,128)S(1)}, u32[]{:S(2)}, u32[]{:S(2)}) collective-permute-start(f32[8,8,128]{2,1,0:T(8,128)S(1)} %shard_map.116), channel_id=1, source_target_pairs={{0,1},{1,2},{2,3},{3,4},{4,5},{5,6},{6,7},{7,0},{8,9},{9,10},{10,1... | collective-permute-start | bytes 98312 | tf_op jit(solution)/shard_map/ppermute | solution.py:671
  66.7 4.0 %collective-permute-start.6 = (f32[8,8,128]{2,1,0:T(8,128)S(1)}, f32[8,8,128]{2,1,0:T(8,128)S(1)}, u32[]{:S(2)}, u32[]{:S(2)}) collective-permute-start(f32[8,8,128]{2,1,0:T(8,128)S(1)} %shard_map.116), channel_id=1, source_target_pairs={{1,0},{2,1},{3,2},{4,3},{5,4},{6,5},{7,6},{0,7},{9,8},{10,9},{11,1... | collective-permute-start | bytes 98312 | tf_op jit(solution)/shard_map/ppermute | solution.py:671
  70.7 4.3 %collective-permute-start.8 = (f32[7,8,256]{2,1,0:T(8,128)S(1)}, f32[7,8,256]{2,1,0:T(8,128)S(1)}, u32[]{:S(2)}, u32[]{:S(2)}) collective-permute-start(f32[7,8,256]{2,1,0:T(8,128)S(1)} %get-tuple-element.92), channel_id=1, source_target_pairs={{0,64},{64,128},{128,192},{192,0},{1,65},{65,129},{129,193},{193,1... | collective-permute-start | bytes 172040 | tf_op jit(solution)/shard_map/ppermute | solution.py:671
  71.7 3.4 %collective-permute-start.9 = (f32[7,8,256]{2,1,0:T(8,128)S(1)}, f32[7,8,256]{2,1,0:T(8,128)S(1)}, u32[]{:S(2)}, u32[]{:S(2)}) collective-permute-start(f32[7,8,256]{2,1,0:T(8,128)S(1)} %get-tuple-element.93), channel_id=1, source_target_pairs={{64,0},{128,64},{192,128},{0,192},{65,1},{129,65},{193,129},{1,193... | collective-permute-start | bytes 172040 | tf_op jit(solution)/shard_map/ppermute | solution.py:671
  75.1 6.1 %collective-permute-start.11 = (f32[22,8,256]{2,1,0:T(8,128)S(1)}, f32[22,8,256]{2,1,0:T(8,128)S(1)}, u32[]{:S(2)}, u32[]{:S(2)}) collective-permute-start(f32[22,8,256]{2,1,0:T(8,128)S(1)} %pad_maximum_fusion.4), channel_id=1, source_target_pairs={{8,0},{16,8},{24,16},{32,24},{40,32},{48,40},{56,48},{0,56},{9,1},... | collective-permute-start | bytes 540680 | tf_op jit(solution)/shard_map/ppermute | solution.py:671
  77.8 3.4 %collective-permute-start.10 = (f32[22,8,256]{2,1,0:T(8,128)S(1)}, f32[22,8,256]{2,1,0:T(8,128)S(1)}, u32[]{:S(2)}, u32[]{:S(2)}) collective-permute-start(f32[22,8,256]{2,1,0:T(8,128)S(1)} %pad_maximum_fusion.4), channel_id=1, source_target_pairs={{0,8},{8,16},{16,24},{24,32},{32,40},{40,48},{48,56},{56,0},{1,9},... | collective-permute-start | bytes 540680 | tf_op jit(solution)/shard_map/ppermute | solution.py:671
  105.4 4.6 %collective-permute-start.13 = (f32[8,8,128]{2,1,0:T(8,128)S(1)}, f32[8,8,128]{2,1,0:T(8,128)S(1)}, u32[]{:S(2)}, u32[]{:S(2)}) collective-permute-start(f32[8,8,128]{2,1,0:T(8,128)S(1)} %get-tuple-element.76), channel_id=1, source_target_pairs={{0,1},{1,2},{2,3},{3,4},{4,5},{5,6},{6,7},{7,0},{8,9},{9,10},{10,1... | collective-permute-start | bytes 98312 | tf_op jit(solution)/shard_map/ppermute | solution.py:671
  105.4 4.6 %collective-permute-start.12 = (f32[8,8,128]{2,1,0:T(8,128)S(1)}, f32[8,8,128]{2,1,0:T(8,128)S(1)}, u32[]{:S(2)}, u32[]{:S(2)}) collective-permute-start(f32[8,8,128]{2,1,0:T(8,128)S(1)} %get-tuple-element.76), channel_id=1, source_target_pairs={{1,0},{2,1},{3,2},{4,3},{5,4},{6,5},{7,6},{0,7},{9,8},{10,9},{11,1... | collective-permute-start | bytes 98312 | tf_op jit(solution)/shard_map/ppermute | solution.py:671
  110.0 4.3 %collective-permute-start.14 = (f32[7,8,256]{2,1,0:T(8,128)S(1)}, f32[7,8,256]{2,1,0:T(8,128)S(1)}, u32[]{:S(2)}, u32[]{:S(2)}) collective-permute-start(f32[7,8,256]{2,1,0:T(8,128)S(1)} %get-tuple-element.90), channel_id=1, source_target_pairs={{0,64},{64,128},{128,192},{192,0},{1,65},{65,129},{129,193},{193,1... | collective-permute-start | bytes 172040 | tf_op jit(solution)/shard_map/ppermute | solution.py:671
  110.6 3.7 %collective-permute-start.15 = (f32[7,8,256]{2,1,0:T(8,128)S(1)}, f32[7,8,256]{2,1,0:T(8,128)S(1)}, u32[]{:S(2)}, u32[]{:S(2)}) collective-permute-start(f32[7,8,256]{2,1,0:T(8,128)S(1)} %get-tuple-element.91), channel_id=1, source_target_pairs={{64,0},{128,64},{192,128},{0,192},{65,1},{129,65},{193,129},{1,193... | collective-permute-start | bytes 172040 | tf_op jit(solution)/shard_map/ppermute | solution.py:671
  114.3 5.7 %collective-permute-start.17 = (f32[22,8,256]{2,1,0:T(8,128)S(1)}, f32[22,8,256]{2,1,0:T(8,128)S(1)}, u32[]{:S(2)}, u32[]{:S(2)}) collective-permute-start(f32[22,8,256]{2,1,0:T(8,128)S(1)} %pad_maximum_fusion.5), channel_id=1, source_target_pairs={{8,0},{16,8},{24,16},{32,24},{40,32},{48,40},{56,48},{0,56},{9,1},... | collective-permute-start | bytes 540680 | tf_op jit(solution)/shard_map/ppermute | solution.py:671
  116.2 3.9 %collective-permute-start.16 = (f32[22,8,256]{2,1,0:T(8,128)S(1)}, f32[22,8,256]{2,1,0:T(8,128)S(1)}, u32[]{:S(2)}, u32[]{:S(2)}) collective-permute-start(f32[22,8,256]{2,1,0:T(8,128)S(1)} %pad_maximum_fusion.5), channel_id=1, source_target_pairs={{0,8},{8,16},{16,24},{24,32},{32,40},{40,48},{48,56},{56,0},{1,9},... | collective-permute-start | bytes 540680 | tf_op jit(solution)/shard_map/ppermute | solution.py:671
  141.7 4.3 %collective-permute-start.19 = (f32[8,8,128]{2,1,0:T(8,128)S(1)}, f32[8,8,128]{2,1,0:T(8,128)S(1)}, u32[]{:S(2)}, u32[]{:S(2)}) collective-permute-start(f32[8,8,128]{2,1,0:T(8,128)S(1)} %shard_map.121), channel_id=1, source_target_pairs={{0,1},{1,2},{2,3},{3,4},{4,5},{5,6},{6,7},{7,0},{8,9},{9,10},{10,1... | collective-permute-start | bytes 98312 | tf_op jit(solution)/shard_map/ppermute | solution.py:671
  141.8 4.2 %collective-permute-start.18 = (f32[8,8,128]{2,1,0:T(8,128)S(1)}, f32[8,8,128]{2,1,0:T(8,128)S(1)}, u32[]{:S(2)}, u32[]{:S(2)}) collective-permute-start(f32[8,8,128]{2,1,0:T(8,128)S(1)} %shard_map.121), channel_id=1, source_target_pairs={{1,0},{2,1},{3,2},{4,3},{5,4},{6,5},{7,6},{0,7},{9,8},{10,9},{11,1... | collective-permute-start | bytes 98312 | tf_op jit(solution)/shard_map/ppermute | solution.py:671
  146.0 4.3 %collective-permute-start.20 = (f32[7,8,256]{2,1,0:T(8,128)S(1)}, f32[7,8,256]{2,1,0:T(8,128)S(1)}, u32[]{:S(2)}, u32[]{:S(2)}) collective-permute-start(f32[7,8,256]{2,1,0:T(8,128)S(1)} %get-tuple-element.88), channel_id=1, source_target_pairs={{0,64},{64,128},{128,192},{192,0},{1,65},{65,129},{129,193},{193,1... | collective-permute-start | bytes 172040 | tf_op jit(solution)/shard_map/ppermute | solution.py:671
  146.9 3.5 %collective-permute-start.21 = (f32[7,8,256]{2,1,0:T(8,128)S(1)}, f32[7,8,256]{2,1,0:T(8,128)S(1)}, u32[]{:S(2)}, u32[]{:S(2)}) collective-permute-start(f32[7,8,256]{2,1,0:T(8,128)S(1)} %get-tuple-element.89), channel_id=1, source_target_pairs={{64,0},{128,64},{192,128},{0,192},{65,1},{129,65},{193,129},{1,193... | collective-permute-start | bytes 172040 | tf_op jit(solution)/shard_map/ppermute | solution.py:671
  150.4 5.7 %collective-permute-start.23 = (f32[22,8,256]{2,1,0:T(8,128)S(1)}, f32[22,8,256]{2,1,0:T(8,128)S(1)}, u32[]{:S(2)}, u32[]{:S(2)}) collective-permute-start(f32[22,8,256]{2,1,0:T(8,128)S(1)} %pad_maximum_fusion.6), channel_id=1, source_target_pairs={{8,0},{16,8},{24,16},{32,24},{40,32},{48,40},{56,48},{0,56},{9,1},... | collective-permute-start | bytes 540680 | tf_op jit(solution)/shard_map/ppermute | solution.py:671
  152.6 3.6 %collective-permute-start.22 = (f32[22,8,256]{2,1,0:T(8,128)S(1)}, f32[22,8,256]{2,1,0:T(8,128)S(1)}, u32[]{:S(2)}, u32[]{:S(2)}) collective-permute-start(f32[22,8,256]{2,1,0:T(8,128)S(1)} %pad_maximum_fusion.6), channel_id=1, source_target_pairs={{0,8},{8,16},{16,24},{24,32},{32,40},{40,48},{48,56},{56,0},{1,9},... | collective-permute-start | bytes 540680 | tf_op jit(solution)/shard_map/ppermute | solution.py:671
  174.2 4.6 %copy-start.1 = (bf16[16,8,8,128]{3,2,1,0:T(8,128)(2,1)S(1)}, bf16[16,8,8,128]{3,2,1,0:T(8,128)(2,1)}, u32[]{:S(2)}) copy-start(bf16[16,8,8,128]{3,2,1,0:T(8,128)(2,1)} %features.3) | copy-start | bytes 786436

commit v4 on v3

--- a/solution.py
+++ b/solution.py
@@ -7,7 +7,7 @@
 from jax.sharding import PartitionSpec as P
 
 GY = ("gy_0", "gy_1")
-CLOSURE = 4
+CLOSURE = 8
 XY = ("gx", "gy_0", "gy_1")
 ALL = ("gx", "gy_0", "gy_1", "gz")
 F32 = jnp.float32
@@ -20,7 +20,7 @@
 REGION = (NXP, NYP, NZP)
 L1 = (20, 32, 128)
 L2 = (10, 16, 128)
-MOST = {24: 7, 32: 8, 16: 8}
+MOST = {24: 7, 32: 16, 16: 8}
 
 
 def shaped(shape, dtype=F32):
@@ -118,7 +118,7 @@
     def one_face(i):
         ax[i] = face(rho[i], rho[i + 1], weight, low[0], high[0])
 
-    planes(lo - 1, hi, one_face, 2)
+    planes(lo - 1, hi, one_face, 7 if count == 24 else 1)
 
     def one(i):
         r = rho[i]
@@ -139,7 +139,7 @@
         d[i] = diagonal
         w[i] = jnp.where(r > 0.0, 0.8 / diagonal, F32(0.0))
 
-    planes(lo, hi, one, 2)
+    planes(lo, hi, one, 4)
 
 
 def lane_pairs(cells, kept, repeat):
@@ -698,13 +698,10 @@
     place = jnp.stack([lax.axis_index("gx"), lax.axis_index(GY), lax.axis_index("gz")])
     sc = jnp.concatenate([place.astype(jnp.int32), open_faces])
     block = (8, 8, 128)
-    weights = jnp.concatenate(
-        [
-            weight_in.astype(F32),
-            jnp.broadcast_to(bias_in[None], (8, 64)),
-            jnp.pad(weight_out.T.astype(F32), ((0, 5), (0, 0))),
-        ],
-        axis=0,
+    weights = (
+        jnp.pad(weight_in.astype(F32), ((0, 16), (0, 0)))
+        + jnp.pad(bias_in[None], ((16, 15), (0, 0)))
+        + jnp.pad(weight_out.T.astype(F32), ((24, 5), (0, 0)))
     )
     fields = jnp.concatenate([velocity, target, density[None]], axis=0)
     flux, slope, hidden, message, target_faces, marks = call(

time: 208 us -> 202 us (0.971)
  Pallas kernels: 41.3 us -> 36.4 us
    pallas_call x16, Pallas kernels: 41.3 us -> 36.4 us  [call(): pl.pallas_call(body, out_shape=outs, in_specs=specs, out_specs=[pl.BlockS...]
where the time goes in v4:
time: 202 us; the launch traced here: 201 us
  blocking collectives  89.7 us (44%)
  starting transfers between devices  38.9 us (19%)
  Pallas kernels  36.4 us (18%)
  waiting for transfers between devices  31.4 us (16%)
  other arithmetic  2.8 us (1%)
    all_to_all x6, blocking collectives, sent_to_all(): return lax.all_to_all(copies, axis, split_axis=0, concat_axis=0, tiled=True)  89.7 us
    pallas_call x16, Pallas kernels, call(): pl.pallas_call(body, out_shape=outs, in_specs=specs, out_specs=[pl.BlockS...  36.4 us
    ppermute x12, starting transfers between devices, ring(): lax.ppermute(down, axis, [(b, a) for a, b in ups])  32.6 us
    ppermute x12, waiting for transfers between devices, ring(): lax.ppermute(down, axis, [(b, a) for a, b in ups])  19.4 us
    ppermute x12, waiting for transfers between devices, ring(): lax.ppermute(up, axis, ups)  12 us
    ppermute x12, starting transfers between devices, ring(): lax.ppermute(up, axis, ups)  6.26 us
  transfers between devices with their start and end apart: 24, of which 14 were waited for; matrix products, arithmetic and copies ran while one was open for 0% of the time, Pallas kernels for 0%

profile of v4, /device:TPU:1, one launch (start us, length us, event | category | flops | bytes accessed | tf_op | source)
XLA Modules:
  0.0 201.1 jit_solution(6707719200432495038)
XLA Ops:
  0.6 0.7 convert_add_fusion.weights
  1.4 1.0 pad_maximum_fusion.3.fields
  2.3 0.7 pad_add_fusion.sc
  3.1 0.9 copy-done
  4.0 3.3 %shard_map.111 = (f32[3,8,8,128]{3,2,1,0:T(8,128)S(1)}, f32[8,512,128]{2,1,0:T(8,128)S(1)}, bf16[8,512,128]{2,1,0:T(8,128)(2,1)S(1)}, f32[19,8,128]{2,1,0:T(8,12...) custom-call(s32[9]{0:T(128)S(1)} %pad_add_fusion.sc, bf16[16,8,8,128]{3,2,1,0:T(8,128)(2,1)S(1)} %copy-done, ...), custom_call_target="tpu_custom_call" | custom-call | tf_op jit(solution)/shard_map/pallas_call | solution.py:35
  7.4 6.4 %collective-permute-start.1 = (f32[19,8,128]{2,1,0:T(8,128)S(1)}, f32[19,8,128]{2,1,0:T(8,128)S(1)}, u32[]{:S(2)}, u32[]{:S(2)}) collective-permute-start(f32[19,8,128]{2,1,0:T(8,128)S(1)} %get-tuple-element.46.own), channel_id=1, source_target_pairs={{1,0},{2,1},{3,2},{4,3},{5,4},{6,5},{7,6},{0,7},{9,8},{10,9},{11,1... | collective-permute-start | bytes 233480 | tf_op jit(solution)/shard_map/ppermute | solution.py:671
  13.8 0.0 collective-permute-start
  13.8 1.4 collective-permute-done.1.after
  15.2 3.0 %collective-permute-done.before.from_z = f32[19,8,128]{2,1,0:T(8,128)S(1)} collective-permute-done((f32[19,8,128]{2,1,0:T(8,128)S(1)}, f32[19,8,128]{2,1,0:T(8,128)S(1)}, u32[]{:S(2)}, u32[]{:S(2)}) %collective-permute-start) | collective-permute-done | bytes 77856 | tf_op jit(solution)/shard_map/ppermute | solution.py:671
  18.3 0.6 shard_map.112
  18.9 1.4 collective-permute-start.2
  20.3 1.5 collective-permute-start.3
  21.8 2.2 %collective-permute-done.3.high = f32[15,8,256]{2,1,0:T(8,128)S(1)} collective-permute-done((f32[15,8,256]{2,1,0:T(8,128)S(1)}, f32[15,8,256]{2,1,0:T(8,128)S(1)}, u32[]{:S(2)}, u32[]{:S(2)}) %collective-permute-start.3) | collective-permute-done | bytes 122912 | tf_op jit(solution)/shard_map/ppermute | solution.py:671
  24.0 0.2 collective-permute-done.2.low.from_x
  24.1 0.6 shard_map.113.own
  24.7 3.4 %collective-permute-start.5 = (f32[48,8,256]{2,1,0:T(8,128)S(1)}, f32[48,8,256]{2,1,0:T(8,128)S(1)}, u32[]{:S(2)}, u32[]{:S(2)}) collective-permute-start(f32[48,8,256]{2,1,0:T(8,128)S(1)} %shard_map.113.own), channel_id=1, source_target_pairs={{8,0},{16,8},{24,16},{32,24},{40,32},{48,40},{56,48},{0,56},{9,1},... | collective-permute-start | bytes 1179656 | tf_op jit(solution)/shard_map/ppermute | solution.py:671
  28.1 1.1 collective-permute-start.4
  29.2 5.7 %collective-permute-done.5.high = f32[48,8,256]{2,1,0:T(8,128)S(1)} collective-permute-done((f32[48,8,256]{2,1,0:T(8,128)S(1)}, f32[48,8,256]{2,1,0:T(8,128)S(1)}, u32[]{:S(2)}, u32[]{:S(2)}) %collective-permute-start.5) | collective-permute-done | bytes 393248 | tf_op jit(solution)/shard_map/ppermute | solution.py:671
  35.0 3.2 %shard_map.114 = (f32[22,24,256]{2,1,0:T(8,128)S(1)}, f32[22,24,256]{2,1,0:T(8,128)S(1)}, f32[22,24,256]{2,1,0:T(8,128)S(1)}, f32[22,24,256]{2,1,0:T(8,128)S(1)}...) custom-call(s32[9]{0:T(128)S(1)} %pad_add_fusion.sc, ...), custom_call_target="tpu_custom_call" | custom-call | tf_op jit(solution)/shard_map/pallas_call | solution.py:35
  38.2 18.4 %all_to_all.30.parts = f32[32,32,128]{2,1,0:T(8,128)S(1)} all-to-all(f32[32,32,128]{2,1,0:T(8,128)S(1)} %get-tuple-element.52), channel_id=1, replica_groups=mesh['gx'=4,'gy_0'=4,'gy_1'=2,'gz'=8] {'gx','gy_0','gy_1'}, dimensions={0} | all-to-all | bytes 1048576 | tf_op jit(solution)/shard_map/all_to_all | solution.py:694
  56.6 2.3 %shard_map.115 = (f32[20,32,128]{2,1,0:T(8,128)S(1)}, f32[20,32,128]{2,1,0:T(8,128)S(1)}, f32[20,32,128]{2,1,0:T(8,128)S(1)}, f32[20,32,128]{2,1,0:T(8,128)S(1)}...) custom-call(s32[9]{0:T(128)S(1)} %pad_add_fusion.sc, ...), custom_call_target="tpu_custom_call" | custom-call | tf_op jit(solution)/shard_map/pallas_call | solution.py:35
  58.9 3.9 %shard_map.116 = f32[8,8,128]{2,1,0:T(8,128)S(1)} custom-call(s32[9]{0:T(128)S(1)} %pad_add_fusion.sc, f32[32,32,128]{2,1,0:T(8,128)S(1)} %all_to_all.30.parts, f32[20,32,128]{2,1,0:T(8,128)S(1)} %get-tuple-element.53.ax1, f32[20,32,128]{2,1,0:T(8,128)S(1)} %get-tuple-element.54.ay1, f32[20,32,128]{2,1,0:T(8,128)S(1)} %get-tuple-element.55.az1, ...), custom_call_target="tpu_custom_call" | custom-call | tf_op jit(solution)/shard_map/pallas_call | solution.py:35
  62.8 0.1 collective-permute-start.7
  62.9 2.7 %collective-permute-start.6 = (f32[8,8,128]{2,1,0:T(8,128)S(1)}, f32[8,8,128]{2,1,0:T(8,128)S(1)}, u32[]{:S(2)}, u32[]{:S(2)}) collective-permute-start(f32[8,8,128]{2,1,0:T(8,128)S(1)} %shard_map.116), channel_id=1, source_target_pairs={{1,0},{2,1},{3,2},{4,3},{5,4},{6,5},{7,6},{0,7},{9,8},{10,9},{11,1... | collective-permute-start | bytes 98312 | tf_op jit(solution)/shard_map/ppermute | solution.py:671
  65.6 1.3 collective-permute-done.7
  66.9 0.0 collective-permute-done.6
  66.9 1.0 collective-permute-start.8
  67.9 1.8 collective-permute-start.9
  69.7 1.6 collective-permute-done.8
  71.3 2.7 %collective-permute-start.11 = (f32[22,8,256]{2,1,0:T(8,128)S(1)}, f32[22,8,256]{2,1,0:T(8,128)S(1)}, u32[]{:S(2)}, u32[]{:S(2)}) collective-permute-start(f32[22,8,256]{2,1,0:T(8,128)S(1)} %pad_maximum_fusion.4), channel_id=1, source_target_pairs={{8,0},{16,8},{24,16},{32,24},{40,32},{48,40},{56,48},{0,56},{9,1},... | collective-permute-start | bytes 540680 | tf_op jit(solution)/shard_map/ppermute | solution.py:671
  74.0 0.2 collective-permute-start.10
  74.2 3.2 %collective-permute-done.11 = f32[22,8,256]{2,1,0:T(8,128)S(1)} collective-permute-done((f32[22,8,256]{2,1,0:T(8,128)S(1)}, f32[22,8,256]{2,1,0:T(8,128)S(1)}, u32[]{:S(2)}, u32[]{:S(2)}) %collective-permute-start.11) | collective-permute-done | bytes 180256 | tf_op jit(solution)/shard_map/ppermute | solution.py:671
  77.4 0.0 collective-permute-done.10
  77.4 2.1 %shard_map.117 = (f32[22,24,256]{2,1,0:T(8,128)S(1)}, f32[22,24,256]{2,1,0:T(8,128)S(1)}, f32[32,16,128]{2,1,0:T(8,128)S(1)}) custom-call(f32[22,24,256]{2,1,0:T(8,128)S(1)} %get-tuple-element.51.s.b, f32[22,24,256]{2,1,0:T(8,128)S(1)} %pad_maximum_fusion.p, f32[22,24,256]{2,1,0:T(8,128)S(1)} %get-tuple-element.64.ax, ...), custom_call_target="tpu_custom_call" | custom-call | tf_op jit(solution)/shard_map/pallas_call | solution.py:35
  79.6 16.1 %all_to_all.31.parts = f32[32,16,128]{2,1,0:T(8,128)S(1)} all-to-all(f32[32,16,128]{2,1,0:T(8,128)S(1)} %get-tuple-element.70), channel_id=1, replica_groups=mesh['gx'=4,'gy_0'=4,'gy_1'=2,'gz'=8] {'gx','gy_0','gy_1'}, dimensions={0} | all-to-all | bytes 524288 | tf_op jit(solution)/shard_map/all_to_all | solution.py:694
  95.6 4.1 %shard_map.118.near = f32[10,24,256]{2,1,0:T(8,128)S(1)} custom-call(s32[9]{0:T(128)S(1)} %pad_add_fusion.sc, f32[32,16,128]{2,1,0:T(8,128)S(1)} %all_to_all.31.parts, f32[20,32,128]{2,1,0:T(8,128)S(1)} %get-tuple-element.53.ax1, f32[20,32,128]{2,1,0:T(8,128)S(1)} %get-tuple-element.54.ay1, f32[20,32,128]{2,1,0:T(8,128)S(1)} %get-tuple-element.55.az1, ...), custom_call_target="tpu_custom_call" | custom-call | tf_op jit(solution)/shard_map/pallas_call | solution.py:35
  99.7 1.3 shard_map.119
  101.0 2.9 %collective-permute-start.12 = (f32[8,8,128]{2,1,0:T(8,128)S(1)}, f32[8,8,128]{2,1,0:T(8,128)S(1)}, u32[]{:S(2)}, u32[]{:S(2)}) collective-permute-start(f32[8,8,128]{2,1,0:T(8,128)S(1)} %get-tuple-element.76), channel_id=1, source_target_pairs={{1,0},{2,1},{3,2},{4,3},{5,4},{6,5},{7,6},{0,7},{9,8},{10,9},{11,1... | collective-permute-start | bytes 98312 | tf_op jit(solution)/shard_map/ppermute | solution.py:671
  104.0 1.6 collective-permute-done.13
  105.6 0.6 collective-permute-start.14
  106.2 2.2 %collective-permute-start.15 = (f32[7,8,256]{2,1,0:T(8,128)S(1)}, f32[7,8,256]{2,1,0:T(8,128)S(1)}, u32[]{:S(2)}, u32[]{:S(2)}) collective-permute-start(f32[7,8,256]{2,1,0:T(8,128)S(1)} %get-tuple-element.91), channel_id=1, source_target_pairs={{64,0},{128,64},{192,128},{0,192},{65,1},{129,65},{193,129},{1,193... | collective-permute-start | bytes 172040 | tf_op jit(solution)/shard_map/ppermute | solution.py:671
  108.4 1.6 collective-permute-done.14
  110.0 1.9 collective-permute-start.17
  111.9 0.4 collective-permute-start.16
  112.2 3.5 %collective-permute-done.17 = f32[22,8,256]{2,1,0:T(8,128)S(1)} collective-permute-done((f32[22,8,256]{2,1,0:T(8,128)S(1)}, f32[22,8,256]{2,1,0:T(8,128)S(1)}, u32[]{:S(2)}, u32[]{:S(2)}) %collective-permute-start.17) | collective-permute-done | bytes 180256 | tf_op jit(solution)/shard_map/ppermute | solution.py:671
  115.8 1.4 shard_map.120
  117.2 15.6 %all_to_all.32.parts = f32[32,16,128]{2,1,0:T(8,128)S(1)} all-to-all(f32[32,16,128]{2,1,0:T(8,128)S(1)} %get-tuple-element.77), channel_id=1, replica_groups=mesh['gx'=4,'gy_0'=4,'gy_1'=2,'gz'=8] {'gx','gy_0','gy_1'}, dimensions={0} | all-to-all | bytes 524288 | tf_op jit(solution)/shard_map/all_to_all | solution.py:694
  132.8 3.9 %shard_map.121 = f32[8,8,128]{2,1,0:T(8,128)S(1)} custom-call(s32[9]{0:T(128)S(1)} %pad_add_fusion.sc, f32[32,16,128]{2,1,0:T(8,128)S(1)} %all_to_all.32.parts, f32[20,32,128]{2,1,0:T(8,128)S(1)} %get-tuple-element.53.ax1, f32[20,32,128]{2,1,0:T(8,128)S(1)} %get-tuple-element.54.ay1, f32[20,32,128]{2,1,0:T(8,128)S(1)} %get-tuple-element.55.az1, ...), custom_call_target="tpu_custom_call" | custom-call | tf_op jit(solution)/shard_map/pallas_call | solution.py:35
  136.7 0.1 collective-permute-start.19
  136.8 3.0 %collective-permute-start.18 = (f32[8,8,128]{2,1,0:T(8,128)S(1)}, f32[8,8,128]{2,1,0:T(8,128)S(1)}, u32[]{:S(2)}, u32[]{:S(2)}) collective-permute-start(f32[8,8,128]{2,1,0:T(8,128)S(1)} %shard_map.121), channel_id=1, source_target_pairs={{1,0},{2,1},{3,2},{4,3},{5,4},{6,5},{7,6},{0,7},{9,8},{10,9},{11,1... | collective-permute-start | bytes 98312 | tf_op jit(solution)/shard_map/ppermute | solution.py:671
  139.8 1.2 collective-permute-done.19
  141.1 1.1 collective-permute-start.20
  142.2 1.9 collective-permute-start.21
  144.1 1.6 collective-permute-done.20
  145.7 2.2 %collective-permute-start.23 = (f32[22,8,256]{2,1,0:T(8,128)S(1)}, f32[22,8,256]{2,1,0:T(8,128)S(1)}, u32[]{:S(2)}, u32[]{:S(2)}) collective-permute-start(f32[22,8,256]{2,1,0:T(8,128)S(1)} %pad_maximum_fusion.6), channel_id=1, source_target_pairs={{8,0},{16,8},{24,16},{32,24},{40,32},{48,40},{56,48},{0,56},{9,1},... | collective-permute-start | bytes 540680 | tf_op jit(solution)/shard_map/ppermute | solution.py:671
  147.9 0.4 collective-permute-start.22
  148.3 3.5 %collective-permute-done.23 = f32[22,8,256]{2,1,0:T(8,128)S(1)} collective-permute-done((f32[22,8,256]{2,1,0:T(8,128)S(1)}, f32[22,8,256]{2,1,0:T(8,128)S(1)}, u32[]{:S(2)}, u32[]{:S(2)}) %collective-permute-start.23) | collective-permute-done | bytes 180256 | tf_op jit(solution)/shard_map/ppermute | solution.py:671
  151.8 2.1 %shard_map.122 = (f32[22,24,256]{2,1,0:T(8,128)S(1)}, f32[22,24,256]{2,1,0:T(8,128)S(1)}, f32[32,16,128]{2,1,0:T(8,128)S(1)}) custom-call(f32[22,24,256]{2,1,0:T(8,128)S(1)} %pad_maximum_fusion.1.b.s, f32[22,24,256]{2,1,0:T(8,128)S(1)} %pad_maximum_fusion.2.p, f32[22,24,256]{2,1,0:T(8,128)S(1)} %get-tuple-element.64.ax, ...), custom_call_target="tpu_custom_call" | custom-call | tf_op jit(solution)/shard_map/pallas_call | solution.py:35
  153.9 15.6 %all_to_all.33.parts = f32[32,16,128]{2,1,0:T(8,128)S(1)} all-to-all(f32[32,16,128]{2,1,0:T(8,128)S(1)} %get-tuple-element.79), channel_id=1, replica_groups=mesh['gx'=4,'gy_0'=4,'gy_1'=2,'gz'=8] {'gx','gy_0','gy_1'}, dimensions={0} | all-to-all | bytes 524288 | tf_op jit(solution)/shard_map/all_to_all | solution.py:694
  169.5 4.1 %shard_map.123.near = f32[10,24,256]{2,1,0:T(8,128)S(1)} custom-call(s32[9]{0:T(128)S(1)} %pad_add_fusion.sc, f32[32,16,128]{2,1,0:T(8,128)S(1)} %all_to_all.33.parts, f32[20,32,128]{2,1,0:T(8,128)S(1)} %get-tuple-element.53.ax1, f32[20,32,128]{2,1,0:T(8,128)S(1)} %get-tuple-element.54.ay1, f32[20,32,128]{2,1,0:T(8,128)S(1)} %get-tuple-element.55.az1, ...), custom_call_target="tpu_custom_call" | custom-call | tf_op jit(solution)/shard_map/pallas_call | solution.py:35
  173.6 2.7 %shard_map.124 = f32[32,16,128]{2,1,0:T(8,128)S(1)} custom-call(s32[9]{0:T(128)S(1)} %pad_add_fusion.sc, f32[10,24,256]{2,1,0:T(8,128)S(1)} %shard_map.123.near, f32[3,8,8,128]{3,2,1,0:T(8,128)S(1)} %get-tuple-element.82.misfit, bf16[16,8,8,128]{3,2,1,0:T(8,128)(2,1)S(1)} %copy-done.1, f32[8,512,128]{2,1,0:T(8,128)S(1)} %get-tuple-element.83.slope, ...), custom_call_target="tpu_custom_call" | custom-call | tf_op jit(solution)/shard_map/pallas_call | solution.py:35
  176.3 12.4 %all_to_all.34.parts = f32[32,16,128]{2,1,0:T(8,128)S(1)} all-to-all(f32[32,16,128]{2,1,0:T(8,128)S(1)} %shard_map.124), channel_id=1, replica_groups=mesh['gx'=4,'gy_0'=4,'gy_1'=2,'gz'=8] {'gx','gy_0','gy_1'}, dimensions={0} | all-to-all | bytes 524288 | tf_op jit(solution)/shard_map/all_to_all | solution.py:694
  188.8 11.6 %all_to_all.35.parts = f32[8,16,128]{2,1,0:T(8,128)S(1)} all-to-all(f32[8,16,128]{2,1,0:T(8,128)S(1)} %shard_map.125), channel_id=1, replica_groups=mesh['gx'=4,'gy_0'=4,'gy_1'=2,'gz'=8] {'gz'}, dimensions={0} | all-to-all | bytes 131072 | tf_op jit(solution)/shard_map/all_to_all | solution.py:694
  200.4 0.7 shard_map.126
  (39 shorter events, 0.4 us)
Async XLA Ops:
  3.1 1.0 copy-start
  7.4 7.9 %collective-permute-start.1 = (f32[19,8,128]{2,1,0:T(8,128)S(1)}, f32[19,8,128]{2,1,0:T(8,128)S(1)}, u32[]{:S(2)}, u32[]{:S(2)}) collective-permute-start(f32[19,8,128]{2,1,0:T(8,128)S(1)} %get-tuple-element.46.own), channel_id=1, source_target_pairs={{1,0},{2,1},{3,2},{4,3},{5,4},{6,5},{7,6},{0,7},{9,8},{10,9},{11,1... | collective-permute-start | bytes 233480 | tf_op jit(solution)/shard_map/ppermute | solution.py:671
  13.8 4.5 %collective-permute-start = (f32[19,8,128]{2,1,0:T(8,128)S(1)}, f32[19,8,128]{2,1,0:T(8,128)S(1)}, u32[]{:S(2)}, u32[]{:S(2)}) collective-permute-start(f32[19,8,128]{2,1,0:T(8,128)S(1)} %get-tuple-element.46.own), channel_id=1, source_target_pairs={{0,1},{1,2},{2,3},{3,4},{4,5},{5,6},{6,7},{7,0},{8,9},{9,10},{10,1... | collective-permute-start | bytes 233480 | tf_op jit(solution)/shard_map/ppermute | solution.py:671
  18.9 5.3 %collective-permute-start.2 = (f32[17,8,256]{2,1,0:T(8,128)S(1)}, f32[17,8,256]{2,1,0:T(8,128)S(1)}, u32[]{:S(2)}, u32[]{:S(2)}) collective-permute-start(f32[17,8,256]{2,1,0:T(8,128)S(1)} %get-tuple-element.49), channel_id=1, source_target_pairs={{0,64},{64,128},{128,192},{192,0},{1,65},{65,129},{129,193},{193,1... | collective-permute-start | bytes 417800 | tf_op jit(solution)/shard_map/ppermute | solution.py:671
  20.3 3.7 %collective-permute-start.3 = (f32[15,8,256]{2,1,0:T(8,128)S(1)}, f32[15,8,256]{2,1,0:T(8,128)S(1)}, u32[]{:S(2)}, u32[]{:S(2)}) collective-permute-start(f32[15,8,256]{2,1,0:T(8,128)S(1)} %get-tuple-element.50), channel_id=1, source_target_pairs={{64,0},{128,64},{192,128},{0,192},{65,1},{129,65},{193,129},{1,193... | collective-permute-start | bytes 368648 | tf_op jit(solution)/shard_map/ppermute | solution.py:671
  24.7 10.2 %collective-permute-start.5 = (f32[48,8,256]{2,1,0:T(8,128)S(1)}, f32[48,8,256]{2,1,0:T(8,128)S(1)}, u32[]{:S(2)}, u32[]{:S(2)}) collective-permute-start(f32[48,8,256]{2,1,0:T(8,128)S(1)} %shard_map.113.own), channel_id=1, source_target_pairs={{8,0},{16,8},{24,16},{32,24},{40,32},{48,40},{56,48},{0,56},{9,1},... | collective-permute-start | bytes 1179656 | tf_op jit(solution)/shard_map/ppermute | solution.py:671
  28.1 6.9 %collective-permute-start.4 = (f32[48,8,256]{2,1,0:T(8,128)S(1)}, f32[48,8,256]{2,1,0:T(8,128)S(1)}, u32[]{:S(2)}, u32[]{:S(2)}) collective-permute-start(f32[48,8,256]{2,1,0:T(8,128)S(1)} %shard_map.113.own), channel_id=1, source_target_pairs={{0,8},{8,16},{16,24},{24,32},{32,40},{40,48},{48,56},{56,0},{1,9},... | collective-permute-start | bytes 1179656 | tf_op jit(solution)/shard_map/ppermute | solution.py:671
  62.8 4.1 %collective-permute-start.7 = (f32[8,8,128]{2,1,0:T(8,128)S(1)}, f32[8,8,128]{2,1,0:T(8,128)S(1)}, u32[]{:S(2)}, u32[]{:S(2)}) collective-permute-start(f32[8,8,128]{2,1,0:T(8,128)S(1)} %shard_map.116), channel_id=1, source_target_pairs={{0,1},{1,2},{2,3},{3,4},{4,5},{5,6},{6,7},{7,0},{8,9},{9,10},{10,1... | collective-permute-start | bytes 98312 | tf_op jit(solution)/shard_map/ppermute | solution.py:671
  62.9 4.0 %collective-permute-start.6 = (f32[8,8,128]{2,1,0:T(8,128)S(1)}, f32[8,8,128]{2,1,0:T(8,128)S(1)}, u32[]{:S(2)}, u32[]{:S(2)}) collective-permute-start(f32[8,8,128]{2,1,0:T(8,128)S(1)} %shard_map.116), channel_id=1, source_target_pairs={{1,0},{2,1},{3,2},{4,3},{5,4},{6,5},{7,6},{0,7},{9,8},{10,9},{11,1... | collective-permute-start | bytes 98312 | tf_op jit(solution)/shard_map/ppermute | solution.py:671
  66.9 4.3 %collective-permute-start.8 = (f32[7,8,256]{2,1,0:T(8,128)S(1)}, f32[7,8,256]{2,1,0:T(8,128)S(1)}, u32[]{:S(2)}, u32[]{:S(2)}) collective-permute-start(f32[7,8,256]{2,1,0:T(8,128)S(1)} %get-tuple-element.92), channel_id=1, source_target_pairs={{0,64},{64,128},{128,192},{192,0},{1,65},{65,129},{129,193},{193,1... | collective-permute-start | bytes 172040 | tf_op jit(solution)/shard_map/ppermute | solution.py:671
  67.9 3.4 %collective-permute-start.9 = (f32[7,8,256]{2,1,0:T(8,128)S(1)}, f32[7,8,256]{2,1,0:T(8,128)S(1)}, u32[]{:S(2)}, u32[]{:S(2)}) collective-permute-start(f32[7,8,256]{2,1,0:T(8,128)S(1)} %get-tuple-element.93), channel_id=1, source_target_pairs={{64,0},{128,64},{192,128},{0,192},{65,1},{129,65},{193,129},{1,193... | collective-permute-start | bytes 172040 | tf_op jit(solution)/shard_map/ppermute | solution.py:671
  71.3 6.1 %collective-permute-start.11 = (f32[22,8,256]{2,1,0:T(8,128)S(1)}, f32[22,8,256]{2,1,0:T(8,128)S(1)}, u32[]{:S(2)}, u32[]{:S(2)}) collective-permute-start(f32[22,8,256]{2,1,0:T(8,128)S(1)} %pad_maximum_fusion.4), channel_id=1, source_target_pairs={{8,0},{16,8},{24,16},{32,24},{40,32},{48,40},{56,48},{0,56},{9,1},... | collective-permute-start | bytes 540680 | tf_op jit(solution)/shard_map/ppermute | solution.py:671
  74.0 3.4 %collective-permute-start.10 = (f32[22,8,256]{2,1,0:T(8,128)S(1)}, f32[22,8,256]{2,1,0:T(8,128)S(1)}, u32[]{:S(2)}, u32[]{:S(2)}) collective-permute-start(f32[22,8,256]{2,1,0:T(8,128)S(1)} %pad_maximum_fusion.4), channel_id=1, source_target_pairs={{0,8},{8,16},{16,24},{24,32},{32,40},{40,48},{48,56},{56,0},{1,9},... | collective-permute-start | bytes 540680 | tf_op jit(solution)/shard_map/ppermute | solution.py:671
  101.0 4.6 %collective-permute-start.13 = (f32[8,8,128]{2,1,0:T(8,128)S(1)}, f32[8,8,128]{2,1,0:T(8,128)S(1)}, u32[]{:S(2)}, u32[]{:S(2)}) collective-permute-start(f32[8,8,128]{2,1,0:T(8,128)S(1)} %get-tuple-element.76), channel_id=1, source_target_pairs={{0,1},{1,2},{2,3},{3,4},{4,5},{5,6},{6,7},{7,0},{8,9},{9,10},{10,1... | collective-permute-start | bytes 98312 | tf_op jit(solution)/shard_map/ppermute | solution.py:671
  101.0 4.6 %collective-permute-start.12 = (f32[8,8,128]{2,1,0:T(8,128)S(1)}, f32[8,8,128]{2,1,0:T(8,128)S(1)}, u32[]{:S(2)}, u32[]{:S(2)}) collective-permute-start(f32[8,8,128]{2,1,0:T(8,128)S(1)} %get-tuple-element.76), channel_id=1, source_target_pairs={{1,0},{2,1},{3,2},{4,3},{5,4},{6,5},{7,6},{0,7},{9,8},{10,9},{11,1... | collective-permute-start | bytes 98312 | tf_op jit(solution)/shard_map/ppermute | solution.py:671
  105.6 4.3 %collective-permute-start.14 = (f32[7,8,256]{2,1,0:T(8,128)S(1)}, f32[7,8,256]{2,1,0:T(8,128)S(1)}, u32[]{:S(2)}, u32[]{:S(2)}) collective-permute-start(f32[7,8,256]{2,1,0:T(8,128)S(1)} %get-tuple-element.90), channel_id=1, source_target_pairs={{0,64},{64,128},{128,192},{192,0},{1,65},{65,129},{129,193},{193,1... | collective-permute-start | bytes 172040 | tf_op jit(solution)/shard_map/ppermute | solution.py:671
  106.2 3.7 %collective-permute-start.15 = (f32[7,8,256]{2,1,0:T(8,128)S(1)}, f32[7,8,256]{2,1,0:T(8,128)S(1)}, u32[]{:S(2)}, u32[]{:S(2)}) collective-permute-start(f32[7,8,256]{2,1,0:T(8,128)S(1)} %get-tuple-element.91), channel_id=1, source_target_pairs={{64,0},{128,64},{192,128},{0,192},{65,1},{129,65},{193,129},{1,193... | collective-permute-start | bytes 172040 | tf_op jit(solution)/shard_map/ppermute | solution.py:671
  110.0 5.7 %collective-permute-start.17 = (f32[22,8,256]{2,1,0:T(8,128)S(1)}, f32[22,8,256]{2,1,0:T(8,128)S(1)}, u32[]{:S(2)}, u32[]{:S(2)}) collective-permute-start(f32[22,8,256]{2,1,0:T(8,128)S(1)} %pad_maximum_fusion.5), channel_id=1, source_target_pairs={{8,0},{16,8},{24,16},{32,24},{40,32},{48,40},{56,48},{0,56},{9,1},... | collective-permute-start | bytes 540680 | tf_op jit(solution)/shard_map/ppermute | solution.py:671
  111.9 3.9 %collective-permute-start.16 = (f32[22,8,256]{2,1,0:T(8,128)S(1)}, f32[22,8,256]{2,1,0:T(8,128)S(1)}, u32[]{:S(2)}, u32[]{:S(2)}) collective-permute-start(f32[22,8,256]{2,1,0:T(8,128)S(1)} %pad_maximum_fusion.5), channel_id=1, source_target_pairs={{0,8},{8,16},{16,24},{24,32},{32,40},{40,48},{48,56},{56,0},{1,9},... | collective-permute-start | bytes 540680 | tf_op jit(solution)/shard_map/ppermute | solution.py:671
  136.7 4.3 %collective-permute-start.19 = (f32[8,8,128]{2,1,0:T(8,128)S(1)}, f32[8,8,128]{2,1,0:T(8,128)S(1)}, u32[]{:S(2)}, u32[]{:S(2)}) collective-permute-start(f32[8,8,128]{2,1,0:T(8,128)S(1)} %shard_map.121), channel_id=1, source_target_pairs={{0,1},{1,2},{2,3},{3,4},{4,5},{5,6},{6,7},{7,0},{8,9},{9,10},{10,1... | collective-permute-start | bytes 98312 | tf_op jit(solution)/shard_map/ppermute | solution.py:671
  136.8 4.2 %collective-permute-start.18 = (f32[8,8,128]{2,1,0:T(8,128)S(1)}, f32[8,8,128]{2,1,0:T(8,128)S(1)}, u32[]{:S(2)}, u32[]{:S(2)}) collective-permute-start(f32[8,8,128]{2,1,0:T(8,128)S(1)} %shard_map.121), channel_id=1, source_target_pairs={{1,0},{2,1},{3,2},{4,3},{5,4},{6,5},{7,6},{0,7},{9,8},{10,9},{11,1... | collective-permute-start | bytes 98312 | tf_op jit(solution)/shard_map/ppermute | solution.py:671
  141.1 4.5 %collective-permute-start.20 = (f32[7,8,256]{2,1,0:T(8,128)S(1)}, f32[7,8,256]{2,1,0:T(8,128)S(1)}, u32[]{:S(2)}, u32[]{:S(2)}) collective-permute-start(f32[7,8,256]{2,1,0:T(8,128)S(1)} %get-tuple-element.88), channel_id=1, source_target_pairs={{0,64},{64,128},{128,192},{192,0},{1,65},{65,129},{129,193},{193,1... | collective-permute-start | bytes 172040 | tf_op jit(solution)/shard_map/ppermute | solution.py:671
  142.2 3.5 %collective-permute-start.21 = (f32[7,8,256]{2,1,0:T(8,128)S(1)}, f32[7,8,256]{2,1,0:T(8,128)S(1)}, u32[]{:S(2)}, u32[]{:S(2)}) collective-permute-start(f32[7,8,256]{2,1,0:T(8,128)S(1)} %get-tuple-element.89), channel_id=1, source_target_pairs={{64,0},{128,64},{192,128},{0,192},{65,1},{129,65},{193,129},{1,193... | collective-permute-start | bytes 172040 | tf_op jit(solution)/shard_map/ppermute | solution.py:671
  145.7 6.0 %collective-permute-start.23 = (f32[22,8,256]{2,1,0:T(8,128)S(1)}, f32[22,8,256]{2,1,0:T(8,128)S(1)}, u32[]{:S(2)}, u32[]{:S(2)}) collective-permute-start(f32[22,8,256]{2,1,0:T(8,128)S(1)} %pad_maximum_fusion.6), channel_id=1, source_target_pairs={{8,0},{16,8},{24,16},{32,24},{40,32},{48,40},{56,48},{0,56},{9,1},... | collective-permute-start | bytes 540680 | tf_op jit(solution)/shard_map/ppermute | solution.py:671
  147.9 3.9 %collective-permute-start.22 = (f32[22,8,256]{2,1,0:T(8,128)S(1)}, f32[22,8,256]{2,1,0:T(8,128)S(1)}, u32[]{:S(2)}, u32[]{:S(2)}) collective-permute-start(f32[22,8,256]{2,1,0:T(8,128)S(1)} %pad_maximum_fusion.6), channel_id=1, source_target_pairs={{0,8},{8,16},{16,24},{24,32},{32,40},{40,48},{48,56},{56,0},{1,9},... | collective-permute-start | bytes 540680 | tf_op jit(solution)/shard_map/ppermute | solution.py:671
  169.5 4.1 %copy-start.1 = (bf16[16,8,8,128]{3,2,1,0:T(8,128)(2,1)S(1)}, bf16[16,8,8,128]{3,2,1,0:T(8,128)(2,1)}, u32[]{:S(2)}) copy-start(bf16[16,8,8,128]{3,2,1,0:T(8,128)(2,1)} %features.3) | copy-start | bytes 786436

commit v5 on v4

--- a/solution.py
+++ b/solution.py
@@ -20,7 +20,7 @@
 REGION = (NXP, NYP, NZP)
 L1 = (20, 32, 128)
 L2 = (10, 16, 128)
-MOST = {24: 7, 32: 16, 16: 8}
+MOST = {24: 10, 32: 16, 16: 8}
 
 
 def shaped(shape, dtype=F32):
@@ -118,7 +118,7 @@
     def one_face(i):
         ax[i] = face(rho[i], rho[i + 1], weight, low[0], high[0])
 
-    planes(lo - 1, hi, one_face, 7 if count == 24 else 1)
+    planes(lo - 1, hi, one_face, 7 if count == 24 else (hi - lo + 1))
 
     def one(i):
         r = rho[i]
@@ -139,7 +139,7 @@
         d[i] = diagonal
         w[i] = jnp.where(r > 0.0, 0.8 / diagonal, F32(0.0))
 
-    planes(lo, hi, one, 4)
+    planes(lo, hi, one, 5 if count == 24 else 8)
 
 
 def lane_pairs(cells, kept, repeat):
@@ -208,7 +208,7 @@
         centre, total = around(p, ax, ay, az, i)
         s[i] = b[i] + total - d[i] * centre
 
-    planes(1, 21, one, 5)
+    planes(1, 21, one, 10)
     presmooth(s, v, va, (ax, ay, az, w, d), rows, out)
 
 

time: 202 us -> 200 us (0.990)
  no operation moved by 1% of the time
where the time goes in v5:
time: 200 us; the launch traced here: 199 us
  blocking collectives  89.7 us (45%)
  starting transfers between devices  38.9 us (19%)
  Pallas kernels  34.8 us (17%)
  waiting for transfers between devices  31.2 us (16%)
  other arithmetic  2.8 us (1%)
    all_to_all x6, blocking collectives, sent_to_all(): return lax.all_to_all(copies, axis, split_axis=0, concat_axis=0, tiled=True)  89.7 us
    pallas_call x16, Pallas kernels, call(): pl.pallas_call(body, out_shape=outs, in_specs=specs, out_specs=[pl.BlockS...  34.8 us
    ppermute x12, starting transfers between devices, ring(): lax.ppermute(down, axis, [(b, a) for a, b in ups])  32.8 us
    ppermute x12, waiting for transfers between devices, ring(): lax.ppermute(down, axis, [(b, a) for a, b in ups])  19.5 us
    ppermute x12, waiting for transfers between devices, ring(): lax.ppermute(up, axis, ups)  11.8 us
    ppermute x12, starting transfers between devices, ring(): lax.ppermute(up, axis, ups)  6.03 us
  transfers between devices with their start and end apart: 24, of which 14 were waited for; matrix products, arithmetic and copies ran while one was open for 0% of the time, Pallas kernels for 0%

profile of v5, /device:TPU:1, one launch (start us, length us, event | category | flops | bytes accessed | tf_op | source)
XLA Modules:
  0.0 199.3 jit_solution(517792163528976202)
XLA Ops:
  0.6 0.7 convert_add_fusion.weights
  1.4 1.0 pad_maximum_fusion.3.fields
  2.3 0.7 pad_add_fusion.sc
  3.1 0.9 copy-done
  4.0 3.3 %shard_map.111 = (f32[3,8,8,128]{3,2,1,0:T(8,128)S(1)}, f32[8,512,128]{2,1,0:T(8,128)S(1)}, bf16[8,512,128]{2,1,0:T(8,128)(2,1)S(1)}, f32[19,8,128]{2,1,0:T(8,12...) custom-call(s32[9]{0:T(128)S(1)} %pad_add_fusion.sc, bf16[16,8,8,128]{3,2,1,0:T(8,128)(2,1)S(1)} %copy-done, ...), custom_call_target="tpu_custom_call" | custom-call | tf_op jit(solution)/shard_map/pallas_call | solution.py:35
  7.4 6.4 %collective-permute-start.1 = (f32[19,8,128]{2,1,0:T(8,128)S(1)}, f32[19,8,128]{2,1,0:T(8,128)S(1)}, u32[]{:S(2)}, u32[]{:S(2)}) collective-permute-start(f32[19,8,128]{2,1,0:T(8,128)S(1)} %get-tuple-element.46.own), channel_id=1, source_target_pairs={{1,0},{2,1},{3,2},{4,3},{5,4},{6,5},{7,6},{0,7},{9,8},{10,9},{11,1... | collective-permute-start | bytes 233480 | tf_op jit(solution)/shard_map/ppermute | solution.py:671
  13.8 0.0 collective-permute-start
  13.8 1.4 collective-permute-done.1.after
  15.2 3.0 %collective-permute-done.before.from_z = f32[19,8,128]{2,1,0:T(8,128)S(1)} collective-permute-done((f32[19,8,128]{2,1,0:T(8,128)S(1)}, f32[19,8,128]{2,1,0:T(8,128)S(1)}, u32[]{:S(2)}, u32[]{:S(2)}) %collective-permute-start) | collective-permute-done | bytes 77856 | tf_op jit(solution)/shard_map/ppermute | solution.py:671
  18.3 0.6 shard_map.112
  18.9 1.4 collective-permute-start.2
  20.3 1.5 collective-permute-start.3
  21.8 2.2 %collective-permute-done.3.high = f32[15,8,256]{2,1,0:T(8,128)S(1)} collective-permute-done((f32[15,8,256]{2,1,0:T(8,128)S(1)}, f32[15,8,256]{2,1,0:T(8,128)S(1)}, u32[]{:S(2)}, u32[]{:S(2)}) %collective-permute-start.3) | collective-permute-done | bytes 122912 | tf_op jit(solution)/shard_map/ppermute | solution.py:671
  24.0 0.2 collective-permute-done.2.low.from_x
  24.1 0.6 shard_map.113.own
  24.7 3.4 %collective-permute-start.5 = (f32[48,8,256]{2,1,0:T(8,128)S(1)}, f32[48,8,256]{2,1,0:T(8,128)S(1)}, u32[]{:S(2)}, u32[]{:S(2)}) collective-permute-start(f32[48,8,256]{2,1,0:T(8,128)S(1)} %shard_map.113.own), channel_id=1, source_target_pairs={{8,0},{16,8},{24,16},{32,24},{40,32},{48,40},{56,48},{0,56},{9,1},... | collective-permute-start | bytes 1179656 | tf_op jit(solution)/shard_map/ppermute | solution.py:671
  28.1 1.1 collective-permute-start.4
  29.2 5.7 %collective-permute-done.5.high = f32[48,8,256]{2,1,0:T(8,128)S(1)} collective-permute-done((f32[48,8,256]{2,1,0:T(8,128)S(1)}, f32[48,8,256]{2,1,0:T(8,128)S(1)}, u32[]{:S(2)}, u32[]{:S(2)}) %collective-permute-start.5) | collective-permute-done | bytes 393248 | tf_op jit(solution)/shard_map/ppermute | solution.py:671
  35.0 3.0 %shard_map.114 = (f32[22,24,256]{2,1,0:T(8,128)S(1)}, f32[22,24,256]{2,1,0:T(8,128)S(1)}, f32[22,24,256]{2,1,0:T(8,128)S(1)}, f32[22,24,256]{2,1,0:T(8,128)S(1)}...) custom-call(s32[9]{0:T(128)S(1)} %pad_add_fusion.sc, ...), custom_call_target="tpu_custom_call" | custom-call | tf_op jit(solution)/shard_map/pallas_call | solution.py:35
  38.0 18.4 %all_to_all.30.parts = f32[32,32,128]{2,1,0:T(8,128)S(1)} all-to-all(f32[32,32,128]{2,1,0:T(8,128)S(1)} %get-tuple-element.52), channel_id=1, replica_groups=mesh['gx'=4,'gy_0'=4,'gy_1'=2,'gz'=8] {'gx','gy_0','gy_1'}, dimensions={0} | all-to-all | bytes 1048576 | tf_op jit(solution)/shard_map/all_to_all | solution.py:694
  56.4 1.6 shard_map.115
  57.9 3.9 %shard_map.116 = f32[8,8,128]{2,1,0:T(8,128)S(1)} custom-call(s32[9]{0:T(128)S(1)} %pad_add_fusion.sc, f32[32,32,128]{2,1,0:T(8,128)S(1)} %all_to_all.30.parts, f32[20,32,128]{2,1,0:T(8,128)S(1)} %get-tuple-element.53.ax1, f32[20,32,128]{2,1,0:T(8,128)S(1)} %get-tuple-element.54.ay1, f32[20,32,128]{2,1,0:T(8,128)S(1)} %get-tuple-element.55.az1, ...), custom_call_target="tpu_custom_call" | custom-call | tf_op jit(solution)/shard_map/pallas_call | solution.py:35
  61.8 0.1 collective-permute-start.7
  61.9 2.7 %collective-permute-start.6 = (f32[8,8,128]{2,1,0:T(8,128)S(1)}, f32[8,8,128]{2,1,0:T(8,128)S(1)}, u32[]{:S(2)}, u32[]{:S(2)}) collective-permute-start(f32[8,8,128]{2,1,0:T(8,128)S(1)} %shard_map.116), channel_id=1, source_target_pairs={{1,0},{2,1},{3,2},{4,3},{5,4},{6,5},{7,6},{0,7},{9,8},{10,9},{11,1... | collective-permute-start | bytes 98312 | tf_op jit(solution)/shard_map/ppermute | solution.py:671
  64.6 1.3 collective-permute-done.7
  65.9 0.0 collective-permute-done.6
  65.9 1.0 collective-permute-start.8
  66.9 1.8 collective-permute-start.9
  68.7 1.6 collective-permute-done.8
  70.3 2.7 %collective-permute-start.11 = (f32[22,8,256]{2,1,0:T(8,128)S(1)}, f32[22,8,256]{2,1,0:T(8,128)S(1)}, u32[]{:S(2)}, u32[]{:S(2)}) collective-permute-start(f32[22,8,256]{2,1,0:T(8,128)S(1)} %pad_maximum_fusion.4), channel_id=1, source_target_pairs={{8,0},{16,8},{24,16},{32,24},{40,32},{48,40},{56,48},{0,56},{9,1},... | collective-permute-start | bytes 540680 | tf_op jit(solution)/shard_map/ppermute | solution.py:671
  73.0 0.2 collective-permute-start.10
  73.2 3.2 %collective-permute-done.11 = f32[22,8,256]{2,1,0:T(8,128)S(1)} collective-permute-done((f32[22,8,256]{2,1,0:T(8,128)S(1)}, f32[22,8,256]{2,1,0:T(8,128)S(1)}, u32[]{:S(2)}, u32[]{:S(2)}) %collective-permute-start.11) | collective-permute-done | bytes 180256 | tf_op jit(solution)/shard_map/ppermute | solution.py:671
  76.5 1.9 shard_map.117
  78.4 16.1 %all_to_all.31.parts = f32[32,16,128]{2,1,0:T(8,128)S(1)} all-to-all(f32[32,16,128]{2,1,0:T(8,128)S(1)} %get-tuple-element.70), channel_id=1, replica_groups=mesh['gx'=4,'gy_0'=4,'gy_1'=2,'gz'=8] {'gx','gy_0','gy_1'}, dimensions={0} | all-to-all | bytes 524288 | tf_op jit(solution)/shard_map/all_to_all | solution.py:694
  94.4 4.1 %shard_map.118.near = f32[10,24,256]{2,1,0:T(8,128)S(1)} custom-call(s32[9]{0:T(128)S(1)} %pad_add_fusion.sc, f32[32,16,128]{2,1,0:T(8,128)S(1)} %all_to_all.31.parts, f32[20,32,128]{2,1,0:T(8,128)S(1)} %get-tuple-element.53.ax1, f32[20,32,128]{2,1,0:T(8,128)S(1)} %get-tuple-element.54.ay1, f32[20,32,128]{2,1,0:T(8,128)S(1)} %get-tuple-element.55.az1, ...), custom_call_target="tpu_custom_call" | custom-call | tf_op jit(solution)/shard_map/pallas_call | solution.py:35
  98.5 1.3 shard_map.119
  99.8 2.9 %collective-permute-start.12 = (f32[8,8,128]{2,1,0:T(8,128)S(1)}, f32[8,8,128]{2,1,0:T(8,128)S(1)}, u32[]{:S(2)}, u32[]{:S(2)}) collective-permute-start(f32[8,8,128]{2,1,0:T(8,128)S(1)} %get-tuple-element.76), channel_id=1, source_target_pairs={{1,0},{2,1},{3,2},{4,3},{5,4},{6,5},{7,6},{0,7},{9,8},{10,9},{11,1... | collective-permute-start | bytes 98312 | tf_op jit(solution)/shard_map/ppermute | solution.py:671
  102.8 1.6 collective-permute-done.13
  104.4 0.6 collective-permute-start.14
  105.0 2.2 %collective-permute-start.15 = (f32[7,8,256]{2,1,0:T(8,128)S(1)}, f32[7,8,256]{2,1,0:T(8,128)S(1)}, u32[]{:S(2)}, u32[]{:S(2)}) collective-permute-start(f32[7,8,256]{2,1,0:T(8,128)S(1)} %get-tuple-element.91), channel_id=1, source_target_pairs={{64,0},{128,64},{192,128},{0,192},{65,1},{129,65},{193,129},{1,193... | collective-permute-start | bytes 172040 | tf_op jit(solution)/shard_map/ppermute | solution.py:671
  107.2 1.6 collective-permute-done.14
  108.8 1.9 collective-permute-start.17
  110.7 0.4 collective-permute-start.16
  111.0 3.5 %collective-permute-done.17 = f32[22,8,256]{2,1,0:T(8,128)S(1)} collective-permute-done((f32[22,8,256]{2,1,0:T(8,128)S(1)}, f32[22,8,256]{2,1,0:T(8,128)S(1)}, u32[]{:S(2)}, u32[]{:S(2)}) %collective-permute-start.17) | collective-permute-done | bytes 180256 | tf_op jit(solution)/shard_map/ppermute | solution.py:671
  114.6 1.3 shard_map.120
  115.9 15.6 %all_to_all.32.parts = f32[32,16,128]{2,1,0:T(8,128)S(1)} all-to-all(f32[32,16,128]{2,1,0:T(8,128)S(1)} %get-tuple-element.77), channel_id=1, replica_groups=mesh['gx'=4,'gy_0'=4,'gy_1'=2,'gz'=8] {'gx','gy_0','gy_1'}, dimensions={0} | all-to-all | bytes 524288 | tf_op jit(solution)/shard_map/all_to_all | solution.py:694
  131.5 3.9 %shard_map.121 = f32[8,8,128]{2,1,0:T(8,128)S(1)} custom-call(s32[9]{0:T(128)S(1)} %pad_add_fusion.sc, f32[32,16,128]{2,1,0:T(8,128)S(1)} %all_to_all.32.parts, f32[20,32,128]{2,1,0:T(8,128)S(1)} %get-tuple-element.53.ax1, f32[20,32,128]{2,1,0:T(8,128)S(1)} %get-tuple-element.54.ay1, f32[20,32,128]{2,1,0:T(8,128)S(1)} %get-tuple-element.55.az1, ...), custom_call_target="tpu_custom_call" | custom-call | tf_op jit(solution)/shard_map/pallas_call | solution.py:35
  135.4 0.1 collective-permute-start.19
  135.5 3.2 %collective-permute-start.18 = (f32[8,8,128]{2,1,0:T(8,128)S(1)}, f32[8,8,128]{2,1,0:T(8,128)S(1)}, u32[]{:S(2)}, u32[]{:S(2)}) collective-permute-start(f32[8,8,128]{2,1,0:T(8,128)S(1)} %shard_map.121), channel_id=1, source_target_pairs={{1,0},{2,1},{3,2},{4,3},{5,4},{6,5},{7,6},{0,7},{9,8},{10,9},{11,1... | collective-permute-start | bytes 98312 | tf_op jit(solution)/shard_map/ppermute | solution.py:671
  138.7 1.0 collective-permute-done.19
  139.7 0.0 collective-permute-done.18
  139.7 0.9 collective-permute-start.20
  140.6 1.9 collective-permute-start.21
  142.5 1.6 collective-permute-done.20
  144.1 2.2 %collective-permute-start.23 = (f32[22,8,256]{2,1,0:T(8,128)S(1)}, f32[22,8,256]{2,1,0:T(8,128)S(1)}, u32[]{:S(2)}, u32[]{:S(2)}) collective-permute-start(f32[22,8,256]{2,1,0:T(8,128)S(1)} %pad_maximum_fusion.6), channel_id=1, source_target_pairs={{8,0},{16,8},{24,16},{32,24},{40,32},{48,40},{56,48},{0,56},{9,1},... | collective-permute-start | bytes 540680 | tf_op jit(solution)/shard_map/ppermute | solution.py:671
  146.3 0.4 collective-permute-start.22
  146.7 3.5 %collective-permute-done.23 = f32[22,8,256]{2,1,0:T(8,128)S(1)} collective-permute-done((f32[22,8,256]{2,1,0:T(8,128)S(1)}, f32[22,8,256]{2,1,0:T(8,128)S(1)}, u32[]{:S(2)}, u32[]{:S(2)}) %collective-permute-start.23) | collective-permute-done | bytes 180256 | tf_op jit(solution)/shard_map/ppermute | solution.py:671
  150.2 1.9 shard_map.122
  152.1 15.6 %all_to_all.33.parts = f32[32,16,128]{2,1,0:T(8,128)S(1)} all-to-all(f32[32,16,128]{2,1,0:T(8,128)S(1)} %get-tuple-element.79), channel_id=1, replica_groups=mesh['gx'=4,'gy_0'=4,'gy_1'=2,'gz'=8] {'gx','gy_0','gy_1'}, dimensions={0} | all-to-all | bytes 524288 | tf_op jit(solution)/shard_map/all_to_all | solution.py:694
  167.7 4.1 %shard_map.123.near = f32[10,24,256]{2,1,0:T(8,128)S(1)} custom-call(s32[9]{0:T(128)S(1)} %pad_add_fusion.sc, f32[32,16,128]{2,1,0:T(8,128)S(1)} %all_to_all.33.parts, f32[20,32,128]{2,1,0:T(8,128)S(1)} %get-tuple-element.53.ax1, f32[20,32,128]{2,1,0:T(8,128)S(1)} %get-tuple-element.54.ay1, f32[20,32,128]{2,1,0:T(8,128)S(1)} %get-tuple-element.55.az1, ...), custom_call_target="tpu_custom_call" | custom-call | tf_op jit(solution)/shard_map/pallas_call | solution.py:35
  171.8 2.7 %shard_map.124 = f32[32,16,128]{2,1,0:T(8,128)S(1)} custom-call(s32[9]{0:T(128)S(1)} %pad_add_fusion.sc, f32[10,24,256]{2,1,0:T(8,128)S(1)} %shard_map.123.near, f32[3,8,8,128]{3,2,1,0:T(8,128)S(1)} %get-tuple-element.82.misfit, bf16[16,8,8,128]{3,2,1,0:T(8,128)(2,1)S(1)} %copy-done.1, f32[8,512,128]{2,1,0:T(8,128)S(1)} %get-tuple-element.83.slope, ...), custom_call_target="tpu_custom_call" | custom-call | tf_op jit(solution)/shard_map/pallas_call | solution.py:35
  174.5 12.4 %all_to_all.34.parts = f32[32,16,128]{2,1,0:T(8,128)S(1)} all-to-all(f32[32,16,128]{2,1,0:T(8,128)S(1)} %shard_map.124), channel_id=1, replica_groups=mesh['gx'=4,'gy_0'=4,'gy_1'=2,'gz'=8] {'gx','gy_0','gy_1'}, dimensions={0} | all-to-all | bytes 524288 | tf_op jit(solution)/shard_map/all_to_all | solution.py:694
  186.9 11.6 %all_to_all.35.parts = f32[8,16,128]{2,1,0:T(8,128)S(1)} all-to-all(f32[8,16,128]{2,1,0:T(8,128)S(1)} %shard_map.125), channel_id=1, replica_groups=mesh['gx'=4,'gy_0'=4,'gy_1'=2,'gz'=8] {'gz'}, dimensions={0} | all-to-all | bytes 131072 | tf_op jit(solution)/shard_map/all_to_all | solution.py:694
  198.6 0.7 shard_map.126
  (39 shorter events, 0.4 us)
Async XLA Ops:
  3.1 1.0 copy-start
  7.4 7.9 %collective-permute-start.1 = (f32[19,8,128]{2,1,0:T(8,128)S(1)}, f32[19,8,128]{2,1,0:T(8,128)S(1)}, u32[]{:S(2)}, u32[]{:S(2)}) collective-permute-start(f32[19,8,128]{2,1,0:T(8,128)S(1)} %get-tuple-element.46.own), channel_id=1, source_target_pairs={{1,0},{2,1},{3,2},{4,3},{5,4},{6,5},{7,6},{0,7},{9,8},{10,9},{11,1... | collective-permute-start | bytes 233480 | tf_op jit(solution)/shard_map/ppermute | solution.py:671
  13.8 4.5 %collective-permute-start = (f32[19,8,128]{2,1,0:T(8,128)S(1)}, f32[19,8,128]{2,1,0:T(8,128)S(1)}, u32[]{:S(2)}, u32[]{:S(2)}) collective-permute-start(f32[19,8,128]{2,1,0:T(8,128)S(1)} %get-tuple-element.46.own), channel_id=1, source_target_pairs={{0,1},{1,2},{2,3},{3,4},{4,5},{5,6},{6,7},{7,0},{8,9},{9,10},{10,1... | collective-permute-start | bytes 233480 | tf_op jit(solution)/shard_map/ppermute | solution.py:671
  18.9 5.3 %collective-permute-start.2 = (f32[17,8,256]{2,1,0:T(8,128)S(1)}, f32[17,8,256]{2,1,0:T(8,128)S(1)}, u32[]{:S(2)}, u32[]{:S(2)}) collective-permute-start(f32[17,8,256]{2,1,0:T(8,128)S(1)} %get-tuple-element.49), channel_id=1, source_target_pairs={{0,64},{64,128},{128,192},{192,0},{1,65},{65,129},{129,193},{193,1... | collective-permute-start | bytes 417800 | tf_op jit(solution)/shard_map/ppermute | solution.py:671
  20.3 3.7 %collective-permute-start.3 = (f32[15,8,256]{2,1,0:T(8,128)S(1)}, f32[15,8,256]{2,1,0:T(8,128)S(1)}, u32[]{:S(2)}, u32[]{:S(2)}) collective-permute-start(f32[15,8,256]{2,1,0:T(8,128)S(1)} %get-tuple-element.50), channel_id=1, source_target_pairs={{64,0},{128,64},{192,128},{0,192},{65,1},{129,65},{193,129},{1,193... | collective-permute-start | bytes 368648 | tf_op jit(solution)/shard_map/ppermute | solution.py:671
  24.7 10.2 %collective-permute-start.5 = (f32[48,8,256]{2,1,0:T(8,128)S(1)}, f32[48,8,256]{2,1,0:T(8,128)S(1)}, u32[]{:S(2)}, u32[]{:S(2)}) collective-permute-start(f32[48,8,256]{2,1,0:T(8,128)S(1)} %shard_map.113.own), channel_id=1, source_target_pairs={{8,0},{16,8},{24,16},{32,24},{40,32},{48,40},{56,48},{0,56},{9,1},... | collective-permute-start | bytes 1179656 | tf_op jit(solution)/shard_map/ppermute | solution.py:671
  28.1 6.9 %collective-permute-start.4 = (f32[48,8,256]{2,1,0:T(8,128)S(1)}, f32[48,8,256]{2,1,0:T(8,128)S(1)}, u32[]{:S(2)}, u32[]{:S(2)}) collective-permute-start(f32[48,8,256]{2,1,0:T(8,128)S(1)} %shard_map.113.own), channel_id=1, source_target_pairs={{0,8},{8,16},{16,24},{24,32},{32,40},{40,48},{48,56},{56,0},{1,9},... | collective-permute-start | bytes 1179656 | tf_op jit(solution)/shard_map/ppermute | solution.py:671
  61.8 4.1 %collective-permute-start.7 = (f32[8,8,128]{2,1,0:T(8,128)S(1)}, f32[8,8,128]{2,1,0:T(8,128)S(1)}, u32[]{:S(2)}, u32[]{:S(2)}) collective-permute-start(f32[8,8,128]{2,1,0:T(8,128)S(1)} %shard_map.116), channel_id=1, source_target_pairs={{0,1},{1,2},{2,3},{3,4},{4,5},{5,6},{6,7},{7,0},{8,9},{9,10},{10,1... | collective-permute-start | bytes 98312 | tf_op jit(solution)/shard_map/ppermute | solution.py:671
  61.9 4.0 %collective-permute-start.6 = (f32[8,8,128]{2,1,0:T(8,128)S(1)}, f32[8,8,128]{2,1,0:T(8,128)S(1)}, u32[]{:S(2)}, u32[]{:S(2)}) collective-permute-start(f32[8,8,128]{2,1,0:T(8,128)S(1)} %shard_map.116), channel_id=1, source_target_pairs={{1,0},{2,1},{3,2},{4,3},{5,4},{6,5},{7,6},{0,7},{9,8},{10,9},{11,1... | collective-permute-start | bytes 98312 | tf_op jit(solution)/shard_map/ppermute | solution.py:671
  65.9 4.3 %collective-permute-start.8 = (f32[7,8,256]{2,1,0:T(8,128)S(1)}, f32[7,8,256]{2,1,0:T(8,128)S(1)}, u32[]{:S(2)}, u32[]{:S(2)}) collective-permute-start(f32[7,8,256]{2,1,0:T(8,128)S(1)} %get-tuple-element.92), channel_id=1, source_target_pairs={{0,64},{64,128},{128,192},{192,0},{1,65},{65,129},{129,193},{193,1... | collective-permute-start | bytes 172040 | tf_op jit(solution)/shard_map/ppermute | solution.py:671
  66.9 3.4 %collective-permute-start.9 = (f32[7,8,256]{2,1,0:T(8,128)S(1)}, f32[7,8,256]{2,1,0:T(8,128)S(1)}, u32[]{:S(2)}, u32[]{:S(2)}) collective-permute-start(f32[7,8,256]{2,1,0:T(8,128)S(1)} %get-tuple-element.93), channel_id=1, source_target_pairs={{64,0},{128,64},{192,128},{0,192},{65,1},{129,65},{193,129},{1,193... | collective-permute-start | bytes 172040 | tf_op jit(solution)/shard_map/ppermute | solution.py:671
  70.3 6.1 %collective-permute-start.11 = (f32[22,8,256]{2,1,0:T(8,128)S(1)}, f32[22,8,256]{2,1,0:T(8,128)S(1)}, u32[]{:S(2)}, u32[]{:S(2)}) collective-permute-start(f32[22,8,256]{2,1,0:T(8,128)S(1)} %pad_maximum_fusion.4), channel_id=1, source_target_pairs={{8,0},{16,8},{24,16},{32,24},{40,32},{48,40},{56,48},{0,56},{9,1},... | collective-permute-start | bytes 540680 | tf_op jit(solution)/shard_map/ppermute | solution.py:671
  73.0 3.4 %collective-permute-start.10 = (f32[22,8,256]{2,1,0:T(8,128)S(1)}, f32[22,8,256]{2,1,0:T(8,128)S(1)}, u32[]{:S(2)}, u32[]{:S(2)}) collective-permute-start(f32[22,8,256]{2,1,0:T(8,128)S(1)} %pad_maximum_fusion.4), channel_id=1, source_target_pairs={{0,8},{8,16},{16,24},{24,32},{32,40},{40,48},{48,56},{56,0},{1,9},... | collective-permute-start | bytes 540680 | tf_op jit(solution)/shard_map/ppermute | solution.py:671
  99.8 4.6 %collective-permute-start.13 = (f32[8,8,128]{2,1,0:T(8,128)S(1)}, f32[8,8,128]{2,1,0:T(8,128)S(1)}, u32[]{:S(2)}, u32[]{:S(2)}) collective-permute-start(f32[8,8,128]{2,1,0:T(8,128)S(1)} %get-tuple-element.76), channel_id=1, source_target_pairs={{0,1},{1,2},{2,3},{3,4},{4,5},{5,6},{6,7},{7,0},{8,9},{9,10},{10,1... | collective-permute-start | bytes 98312 | tf_op jit(solution)/shard_map/ppermute | solution.py:671
  99.8 4.6 %collective-permute-start.12 = (f32[8,8,128]{2,1,0:T(8,128)S(1)}, f32[8,8,128]{2,1,0:T(8,128)S(1)}, u32[]{:S(2)}, u32[]{:S(2)}) collective-permute-start(f32[8,8,128]{2,1,0:T(8,128)S(1)} %get-tuple-element.76), channel_id=1, source_target_pairs={{1,0},{2,1},{3,2},{4,3},{5,4},{6,5},{7,6},{0,7},{9,8},{10,9},{11,1... | collective-permute-start | bytes 98312 | tf_op jit(solution)/shard_map/ppermute | solution.py:671
  104.4 4.3 %collective-permute-start.14 = (f32[7,8,256]{2,1,0:T(8,128)S(1)}, f32[7,8,256]{2,1,0:T(8,128)S(1)}, u32[]{:S(2)}, u32[]{:S(2)}) collective-permute-start(f32[7,8,256]{2,1,0:T(8,128)S(1)} %get-tuple-element.90), channel_id=1, source_target_pairs={{0,64},{64,128},{128,192},{192,0},{1,65},{65,129},{129,193},{193,1... | collective-permute-start | bytes 172040 | tf_op jit(solution)/shard_map/ppermute | solution.py:671
  105.0 3.7 %collective-permute-start.15 = (f32[7,8,256]{2,1,0:T(8,128)S(1)}, f32[7,8,256]{2,1,0:T(8,128)S(1)}, u32[]{:S(2)}, u32[]{:S(2)}) collective-permute-start(f32[7,8,256]{2,1,0:T(8,128)S(1)} %get-tuple-element.91), channel_id=1, source_target_pairs={{64,0},{128,64},{192,128},{0,192},{65,1},{129,65},{193,129},{1,193... | collective-permute-start | bytes 172040 | tf_op jit(solution)/shard_map/ppermute | solution.py:671
  108.8 5.7 %collective-permute-start.17 = (f32[22,8,256]{2,1,0:T(8,128)S(1)}, f32[22,8,256]{2,1,0:T(8,128)S(1)}, u32[]{:S(2)}, u32[]{:S(2)}) collective-permute-start(f32[22,8,256]{2,1,0:T(8,128)S(1)} %pad_maximum_fusion.5), channel_id=1, source_target_pairs={{8,0},{16,8},{24,16},{32,24},{40,32},{48,40},{56,48},{0,56},{9,1},... | collective-permute-start | bytes 540680 | tf_op jit(solution)/shard_map/ppermute | solution.py:671
  110.7 3.9 %collective-permute-start.16 = (f32[22,8,256]{2,1,0:T(8,128)S(1)}, f32[22,8,256]{2,1,0:T(8,128)S(1)}, u32[]{:S(2)}, u32[]{:S(2)}) collective-permute-start(f32[22,8,256]{2,1,0:T(8,128)S(1)} %pad_maximum_fusion.5), channel_id=1, source_target_pairs={{0,8},{8,16},{16,24},{24,32},{32,40},{40,48},{48,56},{56,0},{1,9},... | collective-permute-start | bytes 540680 | tf_op jit(solution)/shard_map/ppermute | solution.py:671
  135.4 4.3 %collective-permute-start.19 = (f32[8,8,128]{2,1,0:T(8,128)S(1)}, f32[8,8,128]{2,1,0:T(8,128)S(1)}, u32[]{:S(2)}, u32[]{:S(2)}) collective-permute-start(f32[8,8,128]{2,1,0:T(8,128)S(1)} %shard_map.121), channel_id=1, source_target_pairs={{0,1},{1,2},{2,3},{3,4},{4,5},{5,6},{6,7},{7,0},{8,9},{9,10},{10,1... | collective-permute-start | bytes 98312 | tf_op jit(solution)/shard_map/ppermute | solution.py:671
  135.5 4.2 %collective-permute-start.18 = (f32[8,8,128]{2,1,0:T(8,128)S(1)}, f32[8,8,128]{2,1,0:T(8,128)S(1)}, u32[]{:S(2)}, u32[]{:S(2)}) collective-permute-start(f32[8,8,128]{2,1,0:T(8,128)S(1)} %shard_map.121), channel_id=1, source_target_pairs={{1,0},{2,1},{3,2},{4,3},{5,4},{6,5},{7,6},{0,7},{9,8},{10,9},{11,1... | collective-permute-start | bytes 98312 | tf_op jit(solution)/shard_map/ppermute | solution.py:671
  139.7 4.3 %collective-permute-start.20 = (f32[7,8,256]{2,1,0:T(8,128)S(1)}, f32[7,8,256]{2,1,0:T(8,128)S(1)}, u32[]{:S(2)}, u32[]{:S(2)}) collective-permute-start(f32[7,8,256]{2,1,0:T(8,128)S(1)} %get-tuple-element.88), channel_id=1, source_target_pairs={{0,64},{64,128},{128,192},{192,0},{1,65},{65,129},{129,193},{193,1... | collective-permute-start | bytes 172040 | tf_op jit(solution)/shard_map/ppermute | solution.py:671
  140.6 3.5 %collective-permute-start.21 = (f32[7,8,256]{2,1,0:T(8,128)S(1)}, f32[7,8,256]{2,1,0:T(8,128)S(1)}, u32[]{:S(2)}, u32[]{:S(2)}) collective-permute-start(f32[7,8,256]{2,1,0:T(8,128)S(1)} %get-tuple-element.89), channel_id=1, source_target_pairs={{64,0},{128,64},{192,128},{0,192},{65,1},{129,65},{193,129},{1,193... | collective-permute-start | bytes 172040 | tf_op jit(solution)/shard_map/ppermute | solution.py:671
  144.1 6.0 %collective-permute-start.23 = (f32[22,8,256]{2,1,0:T(8,128)S(1)}, f32[22,8,256]{2,1,0:T(8,128)S(1)}, u32[]{:S(2)}, u32[]{:S(2)}) collective-permute-start(f32[22,8,256]{2,1,0:T(8,128)S(1)} %pad_maximum_fusion.6), channel_id=1, source_target_pairs={{8,0},{16,8},{24,16},{32,24},{40,32},{48,40},{56,48},{0,56},{9,1},... | collective-permute-start | bytes 540680 | tf_op jit(solution)/shard_map/ppermute | solution.py:671
  146.3 3.9 %collective-permute-start.22 = (f32[22,8,256]{2,1,0:T(8,128)S(1)}, f32[22,8,256]{2,1,0:T(8,128)S(1)}, u32[]{:S(2)}, u32[]{:S(2)}) collective-permute-start(f32[22,8,256]{2,1,0:T(8,128)S(1)} %pad_maximum_fusion.6), channel_id=1, source_target_pairs={{0,8},{8,16},{16,24},{24,32},{32,40},{40,48},{48,56},{56,0},{1,9},... | collective-permute-start | bytes 540680 | tf_op jit(solution)/shard_map/ppermute | solution.py:671
  167.7 4.1 %copy-start.1 = (bf16[16,8,8,128]{3,2,1,0:T(8,128)(2,1)S(1)}, bf16[16,8,8,128]{3,2,1,0:T(8,128)(2,1)}, u32[]{:S(2)}) copy-start(bf16[16,8,8,128]{3,2,1,0:T(8,128)(2,1)} %features.3) | copy-start | bytes 786436

commit v6 on v5

--- a/solution.py
+++ b/solution.py
@@ -118,7 +118,7 @@
     def one_face(i):
         ax[i] = face(rho[i], rho[i + 1], weight, low[0], high[0])
 
-    planes(lo - 1, hi, one_face, 7 if count == 24 else (hi - lo + 1))
+    planes(lo - 1, hi, one_face, hi - lo + 1)
 
     def one(i):
         r = rho[i]
@@ -139,7 +139,7 @@
         d[i] = diagonal
         w[i] = jnp.where(r > 0.0, 0.8 / diagonal, F32(0.0))
 
-    planes(lo, hi, one, 5 if count == 24 else 8)
+    planes(lo, hi, one, 10 if count == 24 else hi - lo)
 
 
 def lane_pairs(cells, kept, repeat):

time: 200 us -> 199 us (level)
  no operation moved by 1% of the time
where the time goes in v6:
time: 199 us
  blocking collectives  90 us (45%)
  starting transfers between devices  38.9 us (20%)
  Pallas kernels  34.2 us (17%)
  waiting for transfers between devices  30.9 us (16%)
  other arithmetic  2.8 us (1%)
    all_to_all x6, blocking collectives, sent_to_all(): return lax.all_to_all(copies, axis, split_axis=0, concat_axis=0, tiled=True)  90 us
    pallas_call x16, Pallas kernels, call(): pl.pallas_call(body, out_shape=outs, in_specs=specs, out_specs=[pl.BlockS...  34.2 us
    ppermute x12, starting transfers between devices, ring(): lax.ppermute(down, axis, [(b, a) for a, b in ups])  32.8 us
    ppermute x12, waiting for transfers between devices, ring(): lax.ppermute(down, axis, [(b, a) for a, b in ups])  19.2 us
    ppermute x12, waiting for transfers between devices, ring(): lax.ppermute(up, axis, ups)  11.8 us
    ppermute x12, starting transfers between devices, ring(): lax.ppermute(up, axis, ups)  6.02 us
  transfers between devices with their start and end apart: 24, of which 14 were waited for; matrix products, arithmetic and copies ran while one was open for 0% of the time, Pallas kernels for 0%

profile of v6, /device:TPU:1, one launch (start us, length us, event | category | flops | bytes accessed | tf_op | source)
XLA Modules:
  0.0 198.7 jit_solution(12883052425095579174)
XLA Ops:
  0.6 0.7 convert_add_fusion.weights
  1.4 1.0 pad_maximum_fusion.3.fields
  2.3 0.7 pad_add_fusion.sc
  3.1 0.9 copy-done
  4.0 3.3 %shard_map.111 = (f32[3,8,8,128]{3,2,1,0:T(8,128)S(1)}, f32[8,512,128]{2,1,0:T(8,128)S(1)}, bf16[8,512,128]{2,1,0:T(8,128)(2,1)S(1)}, f32[19,8,128]{2,1,0:T(8,12...) custom-call(s32[9]{0:T(128)S(1)} %pad_add_fusion.sc, bf16[16,8,8,128]{3,2,1,0:T(8,128)(2,1)S(1)} %copy-done, ...), custom_call_target="tpu_custom_call" | custom-call | tf_op jit(solution)/shard_map/pallas_call | solution.py:35
  7.4 6.4 %collective-permute-start.1 = (f32[19,8,128]{2,1,0:T(8,128)S(1)}, f32[19,8,128]{2,1,0:T(8,128)S(1)}, u32[]{:S(2)}, u32[]{:S(2)}) collective-permute-start(f32[19,8,128]{2,1,0:T(8,128)S(1)} %get-tuple-element.46.own), channel_id=1, source_target_pairs={{1,0},{2,1},{3,2},{4,3},{5,4},{6,5},{7,6},{0,7},{9,8},{10,9},{11,1... | collective-permute-start | bytes 233480 | tf_op jit(solution)/shard_map/ppermute | solution.py:671
  13.8 0.0 collective-permute-start
  13.8 1.4 collective-permute-done.1.after
  15.2 3.0 %collective-permute-done.before.from_z = f32[19,8,128]{2,1,0:T(8,128)S(1)} collective-permute-done((f32[19,8,128]{2,1,0:T(8,128)S(1)}, f32[19,8,128]{2,1,0:T(8,128)S(1)}, u32[]{:S(2)}, u32[]{:S(2)}) %collective-permute-start) | collective-permute-done | bytes 77856 | tf_op jit(solution)/shard_map/ppermute | solution.py:671
  18.3 0.6 shard_map.112
  18.9 1.4 collective-permute-start.2
  20.3 1.5 collective-permute-start.3
  21.8 2.2 %collective-permute-done.3.high = f32[15,8,256]{2,1,0:T(8,128)S(1)} collective-permute-done((f32[15,8,256]{2,1,0:T(8,128)S(1)}, f32[15,8,256]{2,1,0:T(8,128)S(1)}, u32[]{:S(2)}, u32[]{:S(2)}) %collective-permute-start.3) | collective-permute-done | bytes 122912 | tf_op jit(solution)/shard_map/ppermute | solution.py:671
  24.0 0.2 collective-permute-done.2.low.from_x
  24.1 0.6 shard_map.113.own
  24.7 3.4 %collective-permute-start.5 = (f32[48,8,256]{2,1,0:T(8,128)S(1)}, f32[48,8,256]{2,1,0:T(8,128)S(1)}, u32[]{:S(2)}, u32[]{:S(2)}) collective-permute-start(f32[48,8,256]{2,1,0:T(8,128)S(1)} %shard_map.113.own), channel_id=1, source_target_pairs={{8,0},{16,8},{24,16},{32,24},{40,32},{48,40},{56,48},{0,56},{9,1},... | collective-permute-start | bytes 1179656 | tf_op jit(solution)/shard_map/ppermute | solution.py:671
  28.1 1.1 collective-permute-start.4
  29.2 5.7 %collective-permute-done.5.high = f32[48,8,256]{2,1,0:T(8,128)S(1)} collective-permute-done((f32[48,8,256]{2,1,0:T(8,128)S(1)}, f32[48,8,256]{2,1,0:T(8,128)S(1)}, u32[]{:S(2)}, u32[]{:S(2)}) %collective-permute-start.5) | collective-permute-done | bytes 393248 | tf_op jit(solution)/shard_map/ppermute | solution.py:671
  35.0 2.8 %shard_map.114 = (f32[22,24,256]{2,1,0:T(8,128)S(1)}, f32[22,24,256]{2,1,0:T(8,128)S(1)}, f32[22,24,256]{2,1,0:T(8,128)S(1)}, f32[22,24,256]{2,1,0:T(8,128)S(1)}...) custom-call(s32[9]{0:T(128)S(1)} %pad_add_fusion.sc, ...), custom_call_target="tpu_custom_call" | custom-call | tf_op jit(solution)/shard_map/pallas_call | solution.py:35
  37.8 18.4 %all_to_all.30.parts = f32[32,32,128]{2,1,0:T(8,128)S(1)} all-to-all(f32[32,32,128]{2,1,0:T(8,128)S(1)} %get-tuple-element.52), channel_id=1, replica_groups=mesh['gx'=4,'gy_0'=4,'gy_1'=2,'gz'=8] {'gx','gy_0','gy_1'}, dimensions={0} | all-to-all | bytes 1048576 | tf_op jit(solution)/shard_map/all_to_all | solution.py:694
  56.2 1.2 shard_map.115
  57.4 3.9 %shard_map.116 = f32[8,8,128]{2,1,0:T(8,128)S(1)} custom-call(s32[9]{0:T(128)S(1)} %pad_add_fusion.sc, f32[32,32,128]{2,1,0:T(8,128)S(1)} %all_to_all.30.parts, f32[20,32,128]{2,1,0:T(8,128)S(1)} %get-tuple-element.53.ax1, f32[20,32,128]{2,1,0:T(8,128)S(1)} %get-tuple-element.54.ay1, f32[20,32,128]{2,1,0:T(8,128)S(1)} %get-tuple-element.55.az1, ...), custom_call_target="tpu_custom_call" | custom-call | tf_op jit(solution)/shard_map/pallas_call | solution.py:35
  61.3 0.1 collective-permute-start.7
  61.4 2.7 %collective-permute-start.6 = (f32[8,8,128]{2,1,0:T(8,128)S(1)}, f32[8,8,128]{2,1,0:T(8,128)S(1)}, u32[]{:S(2)}, u32[]{:S(2)}) collective-permute-start(f32[8,8,128]{2,1,0:T(8,128)S(1)} %shard_map.116), channel_id=1, source_target_pairs={{1,0},{2,1},{3,2},{4,3},{5,4},{6,5},{7,6},{0,7},{9,8},{10,9},{11,1... | collective-permute-start | bytes 98312 | tf_op jit(solution)/shard_map/ppermute | solution.py:671
  64.1 1.3 collective-permute-done.7
  65.4 0.0 collective-permute-done.6
  65.4 1.0 collective-permute-start.8
  66.4 1.8 collective-permute-start.9
  68.1 1.6 collective-permute-done.8
  69.8 2.7 %collective-permute-start.11 = (f32[22,8,256]{2,1,0:T(8,128)S(1)}, f32[22,8,256]{2,1,0:T(8,128)S(1)}, u32[]{:S(2)}, u32[]{:S(2)}) collective-permute-start(f32[22,8,256]{2,1,0:T(8,128)S(1)} %pad_maximum_fusion.4), channel_id=1, source_target_pairs={{8,0},{16,8},{24,16},{32,24},{40,32},{48,40},{56,48},{0,56},{9,1},... | collective-permute-start | bytes 540680 | tf_op jit(solution)/shard_map/ppermute | solution.py:671
  72.5 0.2 collective-permute-start.10
  72.7 3.2 %collective-permute-done.11 = f32[22,8,256]{2,1,0:T(8,128)S(1)} collective-permute-done((f32[22,8,256]{2,1,0:T(8,128)S(1)}, f32[22,8,256]{2,1,0:T(8,128)S(1)}, u32[]{:S(2)}, u32[]{:S(2)}) %collective-permute-start.11) | collective-permute-done | bytes 180256 | tf_op jit(solution)/shard_map/ppermute | solution.py:671
  75.9 1.9 shard_map.117
  77.8 16.1 %all_to_all.31.parts = f32[32,16,128]{2,1,0:T(8,128)S(1)} all-to-all(f32[32,16,128]{2,1,0:T(8,128)S(1)} %get-tuple-element.70), channel_id=1, replica_groups=mesh['gx'=4,'gy_0'=4,'gy_1'=2,'gz'=8] {'gx','gy_0','gy_1'}, dimensions={0} | all-to-all | bytes 524288 | tf_op jit(solution)/shard_map/all_to_all | solution.py:694
  93.9 4.1 %shard_map.118.near = f32[10,24,256]{2,1,0:T(8,128)S(1)} custom-call(s32[9]{0:T(128)S(1)} %pad_add_fusion.sc, f32[32,16,128]{2,1,0:T(8,128)S(1)} %all_to_all.31.parts, f32[20,32,128]{2,1,0:T(8,128)S(1)} %get-tuple-element.53.ax1, f32[20,32,128]{2,1,0:T(8,128)S(1)} %get-tuple-element.54.ay1, f32[20,32,128]{2,1,0:T(8,128)S(1)} %get-tuple-element.55.az1, ...), custom_call_target="tpu_custom_call" | custom-call | tf_op jit(solution)/shard_map/pallas_call | solution.py:35
  98.0 1.3 shard_map.119
  99.3 2.9 %collective-permute-start.12 = (f32[8,8,128]{2,1,0:T(8,128)S(1)}, f32[8,8,128]{2,1,0:T(8,128)S(1)}, u32[]{:S(2)}, u32[]{:S(2)}) collective-permute-start(f32[8,8,128]{2,1,0:T(8,128)S(1)} %get-tuple-element.76), channel_id=1, source_target_pairs={{1,0},{2,1},{3,2},{4,3},{5,4},{6,5},{7,6},{0,7},{9,8},{10,9},{11,1... | collective-permute-start | bytes 98312 | tf_op jit(solution)/shard_map/ppermute | solution.py:671
  102.2 1.6 collective-permute-done.13
  103.9 0.6 collective-permute-start.14
  104.5 2.2 %collective-permute-start.15 = (f32[7,8,256]{2,1,0:T(8,128)S(1)}, f32[7,8,256]{2,1,0:T(8,128)S(1)}, u32[]{:S(2)}, u32[]{:S(2)}) collective-permute-start(f32[7,8,256]{2,1,0:T(8,128)S(1)} %get-tuple-element.91), channel_id=1, source_target_pairs={{64,0},{128,64},{192,128},{0,192},{65,1},{129,65},{193,129},{1,193... | collective-permute-start | bytes 172040 | tf_op jit(solution)/shard_map/ppermute | solution.py:671
  106.6 1.6 collective-permute-done.14
  108.2 1.9 collective-permute-start.17
  110.1 0.4 collective-permute-start.16
  110.5 3.5 %collective-permute-done.17 = f32[22,8,256]{2,1,0:T(8,128)S(1)} collective-permute-done((f32[22,8,256]{2,1,0:T(8,128)S(1)}, f32[22,8,256]{2,1,0:T(8,128)S(1)}, u32[]{:S(2)}, u32[]{:S(2)}) %collective-permute-start.17) | collective-permute-done | bytes 180256 | tf_op jit(solution)/shard_map/ppermute | solution.py:671
  114.1 1.3 shard_map.120
  115.3 15.6 %all_to_all.32.parts = f32[32,16,128]{2,1,0:T(8,128)S(1)} all-to-all(f32[32,16,128]{2,1,0:T(8,128)S(1)} %get-tuple-element.77), channel_id=1, replica_groups=mesh['gx'=4,'gy_0'=4,'gy_1'=2,'gz'=8] {'gx','gy_0','gy_1'}, dimensions={0} | all-to-all | bytes 524288 | tf_op jit(solution)/shard_map/all_to_all | solution.py:694
  130.9 3.9 %shard_map.121 = f32[8,8,128]{2,1,0:T(8,128)S(1)} custom-call(s32[9]{0:T(128)S(1)} %pad_add_fusion.sc, f32[32,16,128]{2,1,0:T(8,128)S(1)} %all_to_all.32.parts, f32[20,32,128]{2,1,0:T(8,128)S(1)} %get-tuple-element.53.ax1, f32[20,32,128]{2,1,0:T(8,128)S(1)} %get-tuple-element.54.ay1, f32[20,32,128]{2,1,0:T(8,128)S(1)} %get-tuple-element.55.az1, ...), custom_call_target="tpu_custom_call" | custom-call | tf_op jit(solution)/shard_map/pallas_call | solution.py:35
  134.8 0.1 collective-permute-start.19
  134.9 3.2 %collective-permute-start.18 = (f32[8,8,128]{2,1,0:T(8,128)S(1)}, f32[8,8,128]{2,1,0:T(8,128)S(1)}, u32[]{:S(2)}, u32[]{:S(2)}) collective-permute-start(f32[8,8,128]{2,1,0:T(8,128)S(1)} %shard_map.121), channel_id=1, source_target_pairs={{1,0},{2,1},{3,2},{4,3},{5,4},{6,5},{7,6},{0,7},{9,8},{10,9},{11,1... | collective-permute-start | bytes 98312 | tf_op jit(solution)/shard_map/ppermute | solution.py:671
  138.2 1.0 collective-permute-done.19
  139.1 0.0 collective-permute-done.18
  139.2 0.9 collective-permute-start.20
  140.0 1.9 collective-permute-start.21
  142.0 1.6 collective-permute-done.20
  143.6 2.2 %collective-permute-start.23 = (f32[22,8,256]{2,1,0:T(8,128)S(1)}, f32[22,8,256]{2,1,0:T(8,128)S(1)}, u32[]{:S(2)}, u32[]{:S(2)}) collective-permute-start(f32[22,8,256]{2,1,0:T(8,128)S(1)} %pad_maximum_fusion.6), channel_id=1, source_target_pairs={{8,0},{16,8},{24,16},{32,24},{40,32},{48,40},{56,48},{0,56},{9,1},... | collective-permute-start | bytes 540680 | tf_op jit(solution)/shard_map/ppermute | solution.py:671
  145.8 0.4 collective-permute-start.22
  146.1 3.2 %collective-permute-done.23 = f32[22,8,256]{2,1,0:T(8,128)S(1)} collective-permute-done((f32[22,8,256]{2,1,0:T(8,128)S(1)}, f32[22,8,256]{2,1,0:T(8,128)S(1)}, u32[]{:S(2)}, u32[]{:S(2)}) %collective-permute-start.23) | collective-permute-done | bytes 180256 | tf_op jit(solution)/shard_map/ppermute | solution.py:671
  149.4 1.9 shard_map.122
  151.3 15.9 %all_to_all.33.parts = f32[32,16,128]{2,1,0:T(8,128)S(1)} all-to-all(f32[32,16,128]{2,1,0:T(8,128)S(1)} %get-tuple-element.79), channel_id=1, replica_groups=mesh['gx'=4,'gy_0'=4,'gy_1'=2,'gz'=8] {'gx','gy_0','gy_1'}, dimensions={0} | all-to-all | bytes 524288 | tf_op jit(solution)/shard_map/all_to_all | solution.py:694
  167.2 4.1 %shard_map.123.near = f32[10,24,256]{2,1,0:T(8,128)S(1)} custom-call(s32[9]{0:T(128)S(1)} %pad_add_fusion.sc, f32[32,16,128]{2,1,0:T(8,128)S(1)} %all_to_all.33.parts, f32[20,32,128]{2,1,0:T(8,128)S(1)} %get-tuple-element.53.ax1, f32[20,32,128]{2,1,0:T(8,128)S(1)} %get-tuple-element.54.ay1, f32[20,32,128]{2,1,0:T(8,128)S(1)} %get-tuple-element.55.az1, ...), custom_call_target="tpu_custom_call" | custom-call | tf_op jit(solution)/shard_map/pallas_call | solution.py:35
  171.2 2.7 %shard_map.124 = f32[32,16,128]{2,1,0:T(8,128)S(1)} custom-call(s32[9]{0:T(128)S(1)} %pad_add_fusion.sc, f32[10,24,256]{2,1,0:T(8,128)S(1)} %shard_map.123.near, f32[3,8,8,128]{3,2,1,0:T(8,128)S(1)} %get-tuple-element.82.misfit, bf16[16,8,8,128]{3,2,1,0:T(8,128)(2,1)S(1)} %copy-done.1, f32[8,512,128]{2,1,0:T(8,128)S(1)} %get-tuple-element.83.slope, ...), custom_call_target="tpu_custom_call" | custom-call | tf_op jit(solution)/shard_map/pallas_call | solution.py:35
  173.9 12.4 %all_to_all.34.parts = f32[32,16,128]{2,1,0:T(8,128)S(1)} all-to-all(f32[32,16,128]{2,1,0:T(8,128)S(1)} %shard_map.124), channel_id=1, replica_groups=mesh['gx'=4,'gy_0'=4,'gy_1'=2,'gz'=8] {'gx','gy_0','gy_1'}, dimensions={0} | all-to-all | bytes 524288 | tf_op jit(solution)/shard_map/all_to_all | solution.py:694
  186.4 11.6 %all_to_all.35.parts = f32[8,16,128]{2,1,0:T(8,128)S(1)} all-to-all(f32[8,16,128]{2,1,0:T(8,128)S(1)} %shard_map.125), channel_id=1, replica_groups=mesh['gx'=4,'gy_0'=4,'gy_1'=2,'gz'=8] {'gz'}, dimensions={0} | all-to-all | bytes 131072 | tf_op jit(solution)/shard_map/all_to_all | solution.py:694
  198.0 0.7 shard_map.126
  (39 shorter events, 0.4 us)
Async XLA Ops:
  3.1 1.0 copy-start
  7.4 7.9 %collective-permute-start.1 = (f32[19,8,128]{2,1,0:T(8,128)S(1)}, f32[19,8,128]{2,1,0:T(8,128)S(1)}, u32[]{:S(2)}, u32[]{:S(2)}) collective-permute-start(f32[19,8,128]{2,1,0:T(8,128)S(1)} %get-tuple-element.46.own), channel_id=1, source_target_pairs={{1,0},{2,1},{3,2},{4,3},{5,4},{6,5},{7,6},{0,7},{9,8},{10,9},{11,1... | collective-permute-start | bytes 233480 | tf_op jit(solution)/shard_map/ppermute | solution.py:671
  13.8 4.5 %collective-permute-start = (f32[19,8,128]{2,1,0:T(8,128)S(1)}, f32[19,8,128]{2,1,0:T(8,128)S(1)}, u32[]{:S(2)}, u32[]{:S(2)}) collective-permute-start(f32[19,8,128]{2,1,0:T(8,128)S(1)} %get-tuple-element.46.own), channel_id=1, source_target_pairs={{0,1},{1,2},{2,3},{3,4},{4,5},{5,6},{6,7},{7,0},{8,9},{9,10},{10,1... | collective-permute-start | bytes 233480 | tf_op jit(solution)/shard_map/ppermute | solution.py:671
  18.9 5.3 %collective-permute-start.2 = (f32[17,8,256]{2,1,0:T(8,128)S(1)}, f32[17,8,256]{2,1,0:T(8,128)S(1)}, u32[]{:S(2)}, u32[]{:S(2)}) collective-permute-start(f32[17,8,256]{2,1,0:T(8,128)S(1)} %get-tuple-element.49), channel_id=1, source_target_pairs={{0,64},{64,128},{128,192},{192,0},{1,65},{65,129},{129,193},{193,1... | collective-permute-start | bytes 417800 | tf_op jit(solution)/shard_map/ppermute | solution.py:671
  20.3 3.7 %collective-permute-start.3 = (f32[15,8,256]{2,1,0:T(8,128)S(1)}, f32[15,8,256]{2,1,0:T(8,128)S(1)}, u32[]{:S(2)}, u32[]{:S(2)}) collective-permute-start(f32[15,8,256]{2,1,0:T(8,128)S(1)} %get-tuple-element.50), channel_id=1, source_target_pairs={{64,0},{128,64},{192,128},{0,192},{65,1},{129,65},{193,129},{1,193... | collective-permute-start | bytes 368648 | tf_op jit(solution)/shard_map/ppermute | solution.py:671
  24.7 10.2 %collective-permute-start.5 = (f32[48,8,256]{2,1,0:T(8,128)S(1)}, f32[48,8,256]{2,1,0:T(8,128)S(1)}, u32[]{:S(2)}, u32[]{:S(2)}) collective-permute-start(f32[48,8,256]{2,1,0:T(8,128)S(1)} %shard_map.113.own), channel_id=1, source_target_pairs={{8,0},{16,8},{24,16},{32,24},{40,32},{48,40},{56,48},{0,56},{9,1},... | collective-permute-start | bytes 1179656 | tf_op jit(solution)/shard_map/ppermute | solution.py:671
  28.1 6.9 %collective-permute-start.4 = (f32[48,8,256]{2,1,0:T(8,128)S(1)}, f32[48,8,256]{2,1,0:T(8,128)S(1)}, u32[]{:S(2)}, u32[]{:S(2)}) collective-permute-start(f32[48,8,256]{2,1,0:T(8,128)S(1)} %shard_map.113.own), channel_id=1, source_target_pairs={{0,8},{8,16},{16,24},{24,32},{32,40},{40,48},{48,56},{56,0},{1,9},... | collective-permute-start | bytes 1179656 | tf_op jit(solution)/shard_map/ppermute | solution.py:671
  61.3 4.1 %collective-permute-start.7 = (f32[8,8,128]{2,1,0:T(8,128)S(1)}, f32[8,8,128]{2,1,0:T(8,128)S(1)}, u32[]{:S(2)}, u32[]{:S(2)}) collective-permute-start(f32[8,8,128]{2,1,0:T(8,128)S(1)} %shard_map.116), channel_id=1, source_target_pairs={{0,1},{1,2},{2,3},{3,4},{4,5},{5,6},{6,7},{7,0},{8,9},{9,10},{10,1... | collective-permute-start | bytes 98312 | tf_op jit(solution)/shard_map/ppermute | solution.py:671
  61.4 4.0 %collective-permute-start.6 = (f32[8,8,128]{2,1,0:T(8,128)S(1)}, f32[8,8,128]{2,1,0:T(8,128)S(1)}, u32[]{:S(2)}, u32[]{:S(2)}) collective-permute-start(f32[8,8,128]{2,1,0:T(8,128)S(1)} %shard_map.116), channel_id=1, source_target_pairs={{1,0},{2,1},{3,2},{4,3},{5,4},{6,5},{7,6},{0,7},{9,8},{10,9},{11,1... | collective-permute-start | bytes 98312 | tf_op jit(solution)/shard_map/ppermute | solution.py:671
  65.4 4.3 %collective-permute-start.8 = (f32[7,8,256]{2,1,0:T(8,128)S(1)}, f32[7,8,256]{2,1,0:T(8,128)S(1)}, u32[]{:S(2)}, u32[]{:S(2)}) collective-permute-start(f32[7,8,256]{2,1,0:T(8,128)S(1)} %get-tuple-element.92), channel_id=1, source_target_pairs={{0,64},{64,128},{128,192},{192,0},{1,65},{65,129},{129,193},{193,1... | collective-permute-start | bytes 172040 | tf_op jit(solution)/shard_map/ppermute | solution.py:671
  66.4 3.4 %collective-permute-start.9 = (f32[7,8,256]{2,1,0:T(8,128)S(1)}, f32[7,8,256]{2,1,0:T(8,128)S(1)}, u32[]{:S(2)}, u32[]{:S(2)}) collective-permute-start(f32[7,8,256]{2,1,0:T(8,128)S(1)} %get-tuple-element.93), channel_id=1, source_target_pairs={{64,0},{128,64},{192,128},{0,192},{65,1},{129,65},{193,129},{1,193... | collective-permute-start | bytes 172040 | tf_op jit(solution)/shard_map/ppermute | solution.py:671
  69.8 6.1 %collective-permute-start.11 = (f32[22,8,256]{2,1,0:T(8,128)S(1)}, f32[22,8,256]{2,1,0:T(8,128)S(1)}, u32[]{:S(2)}, u32[]{:S(2)}) collective-permute-start(f32[22,8,256]{2,1,0:T(8,128)S(1)} %pad_maximum_fusion.4), channel_id=1, source_target_pairs={{8,0},{16,8},{24,16},{32,24},{40,32},{48,40},{56,48},{0,56},{9,1},... | collective-permute-start | bytes 540680 | tf_op jit(solution)/shard_map/ppermute | solution.py:671
  72.5 3.4 %collective-permute-start.10 = (f32[22,8,256]{2,1,0:T(8,128)S(1)}, f32[22,8,256]{2,1,0:T(8,128)S(1)}, u32[]{:S(2)}, u32[]{:S(2)}) collective-permute-start(f32[22,8,256]{2,1,0:T(8,128)S(1)} %pad_maximum_fusion.4), channel_id=1, source_target_pairs={{0,8},{8,16},{16,24},{24,32},{32,40},{40,48},{48,56},{56,0},{1,9},... | collective-permute-start | bytes 540680 | tf_op jit(solution)/shard_map/ppermute | solution.py:671
  99.3 4.6 %collective-permute-start.13 = (f32[8,8,128]{2,1,0:T(8,128)S(1)}, f32[8,8,128]{2,1,0:T(8,128)S(1)}, u32[]{:S(2)}, u32[]{:S(2)}) collective-permute-start(f32[8,8,128]{2,1,0:T(8,128)S(1)} %get-tuple-element.76), channel_id=1, source_target_pairs={{0,1},{1,2},{2,3},{3,4},{4,5},{5,6},{6,7},{7,0},{8,9},{9,10},{10,1... | collective-permute-start | bytes 98312 | tf_op jit(solution)/shard_map/ppermute | solution.py:671
  99.3 4.6 %collective-permute-start.12 = (f32[8,8,128]{2,1,0:T(8,128)S(1)}, f32[8,8,128]{2,1,0:T(8,128)S(1)}, u32[]{:S(2)}, u32[]{:S(2)}) collective-permute-start(f32[8,8,128]{2,1,0:T(8,128)S(1)} %get-tuple-element.76), channel_id=1, source_target_pairs={{1,0},{2,1},{3,2},{4,3},{5,4},{6,5},{7,6},{0,7},{9,8},{10,9},{11,1... | collective-permute-start | bytes 98312 | tf_op jit(solution)/shard_map/ppermute | solution.py:671
  103.9 4.3 %collective-permute-start.14 = (f32[7,8,256]{2,1,0:T(8,128)S(1)}, f32[7,8,256]{2,1,0:T(8,128)S(1)}, u32[]{:S(2)}, u32[]{:S(2)}) collective-permute-start(f32[7,8,256]{2,1,0:T(8,128)S(1)} %get-tuple-element.90), channel_id=1, source_target_pairs={{0,64},{64,128},{128,192},{192,0},{1,65},{65,129},{129,193},{193,1... | collective-permute-start | bytes 172040 | tf_op jit(solution)/shard_map/ppermute | solution.py:671
  104.5 3.7 %collective-permute-start.15 = (f32[7,8,256]{2,1,0:T(8,128)S(1)}, f32[7,8,256]{2,1,0:T(8,128)S(1)}, u32[]{:S(2)}, u32[]{:S(2)}) collective-permute-start(f32[7,8,256]{2,1,0:T(8,128)S(1)} %get-tuple-element.91), channel_id=1, source_target_pairs={{64,0},{128,64},{192,128},{0,192},{65,1},{129,65},{193,129},{1,193... | collective-permute-start | bytes 172040 | tf_op jit(solution)/shard_map/ppermute | solution.py:671
  108.2 5.7 %collective-permute-start.17 = (f32[22,8,256]{2,1,0:T(8,128)S(1)}, f32[22,8,256]{2,1,0:T(8,128)S(1)}, u32[]{:S(2)}, u32[]{:S(2)}) collective-permute-start(f32[22,8,256]{2,1,0:T(8,128)S(1)} %pad_maximum_fusion.5), channel_id=1, source_target_pairs={{8,0},{16,8},{24,16},{32,24},{40,32},{48,40},{56,48},{0,56},{9,1},... | collective-permute-start | bytes 540680 | tf_op jit(solution)/shard_map/ppermute | solution.py:671
  110.1 3.9 %collective-permute-start.16 = (f32[22,8,256]{2,1,0:T(8,128)S(1)}, f32[22,8,256]{2,1,0:T(8,128)S(1)}, u32[]{:S(2)}, u32[]{:S(2)}) collective-permute-start(f32[22,8,256]{2,1,0:T(8,128)S(1)} %pad_maximum_fusion.5), channel_id=1, source_target_pairs={{0,8},{8,16},{16,24},{24,32},{32,40},{40,48},{48,56},{56,0},{1,9},... | collective-permute-start | bytes 540680 | tf_op jit(solution)/shard_map/ppermute | solution.py:671
  134.8 4.3 %collective-permute-start.19 = (f32[8,8,128]{2,1,0:T(8,128)S(1)}, f32[8,8,128]{2,1,0:T(8,128)S(1)}, u32[]{:S(2)}, u32[]{:S(2)}) collective-permute-start(f32[8,8,128]{2,1,0:T(8,128)S(1)} %shard_map.121), channel_id=1, source_target_pairs={{0,1},{1,2},{2,3},{3,4},{4,5},{5,6},{6,7},{7,0},{8,9},{9,10},{10,1... | collective-permute-start | bytes 98312 | tf_op jit(solution)/shard_map/ppermute | solution.py:671
  134.9 4.2 %collective-permute-start.18 = (f32[8,8,128]{2,1,0:T(8,128)S(1)}, f32[8,8,128]{2,1,0:T(8,128)S(1)}, u32[]{:S(2)}, u32[]{:S(2)}) collective-permute-start(f32[8,8,128]{2,1,0:T(8,128)S(1)} %shard_map.121), channel_id=1, source_target_pairs={{1,0},{2,1},{3,2},{4,3},{5,4},{6,5},{7,6},{0,7},{9,8},{10,9},{11,1... | collective-permute-start | bytes 98312 | tf_op jit(solution)/shard_map/ppermute | solution.py:671
  139.2 4.3 %collective-permute-start.20 = (f32[7,8,256]{2,1,0:T(8,128)S(1)}, f32[7,8,256]{2,1,0:T(8,128)S(1)}, u32[]{:S(2)}, u32[]{:S(2)}) collective-permute-start(f32[7,8,256]{2,1,0:T(8,128)S(1)} %get-tuple-element.88), channel_id=1, source_target_pairs={{0,64},{64,128},{128,192},{192,0},{1,65},{65,129},{129,193},{193,1... | collective-permute-start | bytes 172040 | tf_op jit(solution)/shard_map/ppermute | solution.py:671
  140.0 3.5 %collective-permute-start.21 = (f32[7,8,256]{2,1,0:T(8,128)S(1)}, f32[7,8,256]{2,1,0:T(8,128)S(1)}, u32[]{:S(2)}, u32[]{:S(2)}) collective-permute-start(f32[7,8,256]{2,1,0:T(8,128)S(1)} %get-tuple-element.89), channel_id=1, source_target_pairs={{64,0},{128,64},{192,128},{0,192},{65,1},{129,65},{193,129},{1,193... | collective-permute-start | bytes 172040 | tf_op jit(solution)/shard_map/ppermute | solution.py:671
  143.6 5.7 %collective-permute-start.23 = (f32[22,8,256]{2,1,0:T(8,128)S(1)}, f32[22,8,256]{2,1,0:T(8,128)S(1)}, u32[]{:S(2)}, u32[]{:S(2)}) collective-permute-start(f32[22,8,256]{2,1,0:T(8,128)S(1)} %pad_maximum_fusion.6), channel_id=1, source_target_pairs={{8,0},{16,8},{24,16},{32,24},{40,32},{48,40},{56,48},{0,56},{9,1},... | collective-permute-start | bytes 540680 | tf_op jit(solution)/shard_map/ppermute | solution.py:671
  145.8 3.6 %collective-permute-start.22 = (f32[22,8,256]{2,1,0:T(8,128)S(1)}, f32[22,8,256]{2,1,0:T(8,128)S(1)}, u32[]{:S(2)}, u32[]{:S(2)}) collective-permute-start(f32[22,8,256]{2,1,0:T(8,128)S(1)} %pad_maximum_fusion.6), channel_id=1, source_target_pairs={{0,8},{8,16},{16,24},{24,32},{32,40},{40,48},{48,56},{56,0},{1,9},... | collective-permute-start | bytes 540680 | tf_op jit(solution)/shard_map/ppermute | solution.py:671
  167.2 4.1 %copy-start.1 = (bf16[16,8,8,128]{3,2,1,0:T(8,128)(2,1)S(1)}, bf16[16,8,8,128]{3,2,1,0:T(8,128)(2,1)}, u32[]{:S(2)}) copy-start(bf16[16,8,8,128]{3,2,1,0:T(8,128)(2,1)} %features.3) | copy-start | bytes 786436
